TPU v7x, 32 devices: a whole 2x2x4 slice. The times are simulated.
32 devices in a mesh: rows: 16 (over z, x, core), cols: 2 (over y).
Axes of the slice: x: 2, y: 2, z: 4, core: 2. Of those that a mesh axis runs over, the one named last changes fastest.
Arguments:
- states: float32 [32, 16384], P('cols', 'rows'), may hold values from -120 to 120, as said below
- adj_weight: bfloat16 [128, 3, 128, 128], P('rows'), may hold values from 0.099609375 to 2
- adj_index: int32 [128, 3], P('rows'), may hold values from 0 to 127, as said below
- partner: int32 [128], P('rows'), may hold values from 0 to 127, as said below
Outputs:
- correction: float32 [32, 16384], P('cols', 'rows')
Inputs may be any that keep to these rules, and one draw needn't show every extreme that they name: adj_index[b, 0] = b; every other entry lies within 4 blocks of b. partner[partner[b]] = b and partner[b] != b; the 8 blocks of one index of rows have their partners on 8 different other indices of rows, at most one block on each. `states`: finite values.
All inputs are finite; a program needn't handle non-finite values.
Results may differ from a plain program's by a relative error of at most 0.0003.
Values sent between devices are 32-bit elements; how exact they have to be, the bound alone decides.
No kernel may reach another device: no remote copies, remote signals or barrier semaphores. Data moves between devices by JAX's collectives and lax.ppermute only.
A program may use at most 64 MiB of HBM per device.

v0:
```python
import jax
import jax.numpy as jnp
from jax import lax
from jax.sharding import PartitionSpec as P

DAMPING = 2.0 / 3.0
EPSILON = 1e-06
EXACT = lax.Precision.HIGHEST


def extended(shard, sides, width):
    for axis, dim in sides:
        peers, length = (lax.axis_size(axis), shard.shape[dim])
        up = [(i, (i + 1) % peers) for i in range(peers - 1)]
        down = [(j, i) for i, j in up]
        last = lax.slice_in_dim(shard, length - width, length, axis=dim)
        initial = lax.slice_in_dim(shard, 0, width, axis=dim)
        before = lax.ppermute(last, axis, up)
        after = lax.ppermute(initial, axis, down)
        shard = jnp.concatenate([before, shard, after], axis=dim)
    return shard


def to_slots(values, owner_dev, row_devices):
    empty = jnp.zeros((values.shape[0], row_devices, values.shape[2]), values.dtype)
    return empty.at[:, owner_dev].set(values)


def from_slots(arrived, owner_dev):
    return arrived[:, owner_dev]


def solve_ritz(gram_matrix, rayleigh):
    factor = jnp.linalg.cholesky(gram_matrix)
    return jax.scipy.linalg.cho_solve((factor, True), rayleigh)


def local(states, adj_weight, adj_index, partner):
    local_cols, vertices = states.shape
    blocks_here = adj_weight.shape[0]
    block_len = adj_weight.shape[2]
    row_devices = lax.axis_size("rows")
    margin_blocks = blocks_here // 2
    local_ids = adj_index - (lax.axis_index("rows") * blocks_here - margin_blocks)
    owner_dev = partner // blocks_here
    degree = jnp.sum(adj_weight, axis=(1, 3), dtype=jnp.float32).reshape(vertices)
    degree_blocks = degree.reshape(1, blocks_here, block_len)

    def operate(vector_in):
        widened = extended(vector_in, (("rows", 1),), margin_blocks * block_len)
        grid_blocks = widened.reshape(local_cols, -1, block_len)
        picked = grid_blocks[:, local_ids]
        neighbour = jnp.einsum(
            "bkij,cbkj->cbi",
            adj_weight,
            picked,
            precision=EXACT,
            preferred_element_type=jnp.float32,
        )
        return degree * vector_in - neighbour.reshape(local_cols, vertices)

    applied = operate(states)
    all_states = lax.all_gather(states, "cols", axis=0, tiled=True)
    gram_part = jnp.einsum("cv,dv->cd", all_states * degree, all_states, precision=EXACT)
    rayleigh_part = jnp.einsum("cv,dv->cd", all_states, applied, precision=EXACT)
    gram_matrix, rayleigh = lax.psum((gram_part, rayleigh_part), "rows")
    ritz_matrix = solve_ritz(gram_matrix, rayleigh)
    residual = applied - degree * jnp.einsum("cd,cv->dv", ritz_matrix, all_states, precision=EXACT)
    presmooth = DAMPING * residual / degree
    remain = (residual - operate(presmooth)).reshape(local_cols, blocks_here, block_len)
    arrived, arrived_degree = (
        lax.all_to_all(
            to_slots(remain, owner_dev, row_devices),
            "rows",
            split_axis=1,
            concat_axis=1,
            tiled=True,
        ),
        lax.all_to_all(
            to_slots(degree_blocks, owner_dev, row_devices),
            "rows",
            split_axis=1,
            concat_axis=1,
            tiled=True,
        ),
    )
    coarse_degree = (degree_blocks + from_slots(arrived_degree, owner_dev)).reshape(vertices)
    coarse = (remain + from_slots(arrived, owner_dev)).reshape(local_cols, vertices)
    coarse_fix = DAMPING * coarse / coarse_degree
    product = operate(coarse_fix).reshape(local_cols, blocks_here, block_len)
    arrived_product = lax.all_to_all(
        to_slots(product, owner_dev, row_devices), "rows", split_axis=1, concat_axis=1, tiled=True
    )
    coarse_image = (product + from_slots(arrived_product, owner_dev)).reshape(local_cols, vertices)
    coarse_fix = coarse_fix + DAMPING * (coarse - coarse_image) / coarse_degree
    second = presmooth + coarse_fix
    smooth = second + DAMPING * (residual - operate(second)) / degree
    squares = lax.psum(jnp.sum(smooth * smooth, axis=1), "rows")
    return smooth / jnp.sqrt(squares / (vertices * row_devices) + EPSILON)[:, None]


def solution(mesh):
    return jax.shard_map(
        local,
        mesh=mesh,
        in_specs=(P("cols", "rows"), P("rows", None, None, None), P("rows", None), P("rows")),
        out_specs=P("cols", "rows"),
        check_vma=False,
    )
```

profile of v0, /device:TPU:0, one launch (start us, length us, event | category | flops | bytes accessed | tf_op | source)
XLA Modules:
  0.0 170.4 jit_solution(17137495620325622604)
XLA Ops:
  0.0 0.8 fusion.28
  0.8 2.4 %collective-permute-start = (f32[16,512]{1,0:T(8,128)S(1)}, f32[16,512]{1,0:T(8,128)S(1)}, u32[]{:S(2)}, u32[]{:S(2)}) collective-permute-start(f32[16,512]{1,0:T(8,128)S(1)} %get-tuple-element.15), channel_id=1, source_target_pairs={{0,2},{2,4},{4,6},{6,8},{8,10},{10,12},{12,14},{14,16},{16,18},{18... | collective-permute-start | bytes 98312 | tf_op jit(solution)/shard_map/ppermute | solution.py:18
  3.2 1.3 collective-permute-start.1
  4.5 5.5 %all_gather.3 = f32[32,1024]{1,0:T(8,128)S(1)} all-gather(f32[16,1024]{1,0:T(8,128)} %param.4), channel_id=1, replica_groups=mesh['rows'=16,'cols'=2] {'cols'}, dimensions={0}, use_global_device_ids=true | all-gather | bytes 196608 | tf_op jit(solution)/shard_map/all_gather | solution.py:63
  10.1 0.7 compare_select_fusion
  10.9 1.4 convert_reduce_fusion
  13.3 0.9 convolution_bitcast_fusion.3
  14.4 62.2 %all-reduce = (f32[32,16]{0,1:T(8,128)S(1)}, f32[32,32]{0,1:T(8,128)S(1)}) all-reduce(f32[32,16]{0,1:T(8,128)S(1)} %convolution_bitcast_fusion.4, f32[32,32]{0,1:T(8,128)S(1)} %fusion.1), channel_id=1, replica_groups=mesh['rows'=16,'cols'=2] {'rows'}, use_global_device_ids=true, to_apply=%region_4.5 | all-reduce | flops 1536 | bytes 12288 | tf_op jit(solution)/shard_map/psum | solution.py:66
  76.7 2.9 %cholesky.16 = f32[32,32]{1,0:T(8,128)S(1)} custom-call(f32[32,32]{1,0:T(8,128)S(1)} %fusion.20), custom_call_target="Cholesky" | custom-call | tf_op jit(solution)/shard_map/jit(cholesky)/cholesky | solution.py:34
  80.3 0.7 fusion.15
  81.0 2.4 %custom-call.10 = f32[1,32,32]{1,2,0:T(8,128)S(1)} custom-call(f32[1,32,32]{2,1,0:T(8,128)S(1)} %fusion.15), custom_call_target="InvertDiagBlocksLowerTriangular" | custom-call | tf_op jit(solution)/shard_map/jit(_cho_solve)/triangular_solve | solution.py:35
  83.9 1.3 collective-permute-start.2
  85.2 1.3 collective-permute-start.3
  86.6 1.2 scatter_custom_fusion.1
  87.7 3.5 %all-to-all-start.1 = ((f32[1,16,128]{2,0,1:T(1,128)}), f32[1,16,128]{2,0,1:T(1,128)S(1)}, u32[]{:S(2)}, u32[]{:S(2)}) async-start(f32[1,16,128]{2,0,1:T(1,128)} %bitcast.17), calls=%async_computation.1 | async-start | bytes 16384 | tf_op jit(solution)/shard_map/all_to_all | solution.py:79
  91.8 0.9 convolution_bitcast_fusion.2
  93.4 2.0 %scatter_fusion = f32[16,16,128]{2,0,1:T(8,128)} fusion(f32[16,16,128]{2,0,1:T(8,128)} %broadcast.109.clone, s32[8]{0:T(128)S(1)} %compare_select_fusion.1, f32[8,16,128]{2,1,0:T(8,128)S(1)} %bitcast_bitcast_fusion.1), kind=kCustom, calls=%fused_computation.7 | custom fusion | bytes 196640 | tf_op jit(solution)/shard_map/scatter | solution.py:26
  95.4 2.1 %all-to-all-done.1 = f32[1,16,128]{2,0,1:T(1,128)S(1)} async-done(((f32[1,16,128]{2,0,1:T(1,128)}), f32[1,16,128]{2,0,1:T(1,128)S(1)}, u32[]{:S(2)}, u32[]{:S(2)}) %all-to-all-start.1) | async-done | bytes 8224 | tf_op jit(solution)/shard_map/all_to_all | solution.py:79
  97.5 3.9 %all-to-all-start = ((f32[16,16,128]{2,0,1:T(8,128)}), f32[16,16,128]{2,0,1:T(8,128)S(1)}, u32[]{:S(2)}, u32[]{:S(2)}) async-start(f32[16,16,128]{2,0,1:T(8,128)} %scatter_fusion), calls=%async_computation | async-start | bytes 262144 | tf_op jit(solution)/shard_map/all_to_all | solution.py:72
  102.0 7.3 %all-to-all-done = f32[16,16,128]{2,0,1:T(8,128)S(1)} async-done(((f32[16,16,128]{2,0,1:T(8,128)}), f32[16,16,128]{2,0,1:T(8,128)S(1)}, u32[]{:S(2)}, u32[]{:S(2)}) %all-to-all-start) | async-done | bytes 131104 | tf_op jit(solution)/shard_map/all_to_all | solution.py:72
  109.9 1.3 collective-permute-start.4
  111.2 1.3 collective-permute-start.5
  112.5 1.8 %collective-permute-done.5 = f32[16,512]{1,0:T(8,128)S(1)} collective-permute-done((f32[16,512]{1,0:T(8,128)S(1)}, f32[16,512]{1,0:T(8,128)S(1)}, u32[]{:S(2)}, u32[]{:S(2)}) %collective-permute-start.5) | collective-permute-done | bytes 32800 | tf_op jit(solution)/shard_map/ppermute | solution.py:19
  114.9 0.9 convolution_bitcast_fusion.1
  115.9 0.7 scatter_fusion.1
  116.6 14.6 %all_to_all.15 = f32[16,16,128]{2,0,1:T(8,128)S(1)} all-to-all(f32[16,16,128]{2,0,1:T(8,128)S(1)} %scatter_fusion.1), channel_id=1, replica_groups=mesh['rows'=16,'cols'=2] {'rows'}, dimensions={1} | all-to-all | bytes 262144 | tf_op jit(solution)/shard_map/all_to_all | solution.py:91
  131.9 1.3 collective-permute-start.6
  133.2 1.3 collective-permute-start.7
  134.5 1.8 %collective-permute-done.7 = f32[16,512]{1,0:T(8,128)S(1)} collective-permute-done((f32[16,512]{1,0:T(8,128)S(1)}, f32[16,512]{1,0:T(8,128)S(1)}, u32[]{:S(2)}, u32[]{:S(2)}) %collective-permute-start.7) | collective-permute-done | bytes 32800 | tf_op jit(solution)/shard_map/ppermute | solution.py:19
  136.9 0.9 convolution_bitcast_fusion
  137.9 31.7 %psum.23 = f32[16]{0:T(128)S(1)} all-reduce(f32[16]{0:T(128)S(1)} %get-tuple-element.7), channel_id=1, replica_groups=mesh['rows'=16,'cols'=2] {'rows'}, use_global_device_ids=true, to_apply=%region_9.10 | all-reduce | flops 16 | bytes 128 | tf_op jit(solution)/shard_map/psum | solution.py:98
  169.7 0.7 broadcast_divide_fusion
  (49 shorter events, 6.9 us)
Async XLA Ops:
  0.0 12.6 %copy-start.1 = (f32[16,1024]{1,0:T(8,128)S(1)}, f32[16,1024]{1,0:T(8,128)}, u32[]{:S(2)}) copy-start(f32[16,1024]{1,0:T(8,128)} %param.4) | copy-start | bytes 196612
  0.8 11.8 %collective-permute-start = (f32[16,512]{1,0:T(8,128)S(1)}, f32[16,512]{1,0:T(8,128)S(1)}, u32[]{:S(2)}, u32[]{:S(2)}) collective-permute-start(f32[16,512]{1,0:T(8,128)S(1)} %get-tuple-element.15), channel_id=1, source_target_pairs={{0,2},{2,4},{4,6},{6,8},{8,10},{10,12},{12,14},{14,16},{16,18},{18... | collective-permute-start | bytes 98312 | tf_op jit(solution)/shard_map/ppermute | solution.py:18
  3.2 9.4 %collective-permute-start.1 = (f32[16,512]{1,0:T(8,128)S(1)}, f32[16,512]{1,0:T(8,128)S(1)}, u32[]{:S(2)}, u32[]{:S(2)}) collective-permute-start(f32[16,512]{1,0:T(8,128)S(1)} %get-tuple-element.16), channel_id=1, source_target_pairs={{2,0},{4,2},{6,4},{8,6},{10,8},{12,10},{14,12},{16,14},{18,16},{20... | collective-permute-start | bytes 98312 | tf_op jit(solution)/shard_map/ppermute | solution.py:19
  10.9 2.3 %copy-start = (bf16[8,3,128,128]{3,2,1,0:T(8,128)(2,1)S(1)}, bf16[8,3,128,128]{3,2,1,0:T(8,128)(2,1)}, u32[]{:S(2)}) copy-start(bf16[8,3,128,128]{3,2,1,0:T(8,128)(2,1)} %param.5) | copy-start | bytes 2359300
  14.2 72.4 %copy-start.2 = (s32[8]{0:T(128)S(1)}, s32[8]{0:T(128)}, u32[]{:S(2)}) copy-start(s32[8]{0:T(128)} %param.7) | copy-start | bytes 100
  83.9 7.3 %collective-permute-start.2 = (f32[16,512]{1,0:T(8,128)S(1)}, f32[16,512]{1,0:T(8,128)S(1)}, u32[]{:S(2)}, u32[]{:S(2)}) collective-permute-start(f32[16,512]{1,0:T(8,128)S(1)} %get-tuple-element.13), channel_id=1, source_target_pairs={{0,2},{2,4},{4,6},{6,8},{8,10},{10,12},{12,14},{14,16},{16,18},{18... | collective-permute-start | bytes 98312 | tf_op jit(solution)/shard_map/ppermute | solution.py:18
  85.2 6.0 %collective-permute-start.3 = (f32[16,512]{1,0:T(8,128)S(1)}, f32[16,512]{1,0:T(8,128)S(1)}, u32[]{:S(2)}, u32[]{:S(2)}) collective-permute-start(f32[16,512]{1,0:T(8,128)S(1)} %get-tuple-element.14), channel_id=1, source_target_pairs={{2,0},{4,2},{6,4},{8,6},{10,8},{12,10},{14,12},{16,14},{18,16},{20... | collective-permute-start | bytes 98312 | tf_op jit(solution)/shard_map/ppermute | solution.py:19
  87.7 9.8 %all-to-all-start.1 = ((f32[1,16,128]{2,0,1:T(1,128)}), f32[1,16,128]{2,0,1:T(1,128)S(1)}, u32[]{:S(2)}, u32[]{:S(2)}) async-start(f32[1,16,128]{2,0,1:T(1,128)} %bitcast.17), calls=%async_computation.1 | async-start | bytes 16384 | tf_op jit(solution)/shard_map/all_to_all | solution.py:79
  97.5 11.8 %all-to-all-start = ((f32[16,16,128]{2,0,1:T(8,128)}), f32[16,16,128]{2,0,1:T(8,128)S(1)}, u32[]{:S(2)}, u32[]{:S(2)}) async-start(f32[16,16,128]{2,0,1:T(8,128)} %scatter_fusion), calls=%async_computation | async-start | bytes 262144 | tf_op jit(solution)/shard_map/all_to_all | solution.py:72
  109.9 2.6 %collective-permute-start.4 = (f32[16,512]{1,0:T(8,128)S(1)}, f32[16,512]{1,0:T(8,128)S(1)}, u32[]{:S(2)}, u32[]{:S(2)}) collective-permute-start(f32[16,512]{1,0:T(8,128)S(1)} %get-tuple-element.11), channel_id=1, source_target_pairs={{0,2},{2,4},{4,6},{6,8},{8,10},{10,12},{12,14},{14,16},{16,18},{18... | collective-permute-start | bytes 98312 | tf_op jit(solution)/shard_map/ppermute | solution.py:18
  111.2 3.1 %collective-permute-start.5 = (f32[16,512]{1,0:T(8,128)S(1)}, f32[16,512]{1,0:T(8,128)S(1)}, u32[]{:S(2)}, u32[]{:S(2)}) collective-permute-start(f32[16,512]{1,0:T(8,128)S(1)} %get-tuple-element.12), channel_id=1, source_target_pairs={{2,0},{4,2},{6,4},{8,6},{10,8},{12,10},{14,12},{16,14},{18,16},{20... | collective-permute-start | bytes 98312 | tf_op jit(solution)/shard_map/ppermute | solution.py:19
  131.9 2.6 %collective-permute-start.6 = (f32[16,512]{1,0:T(8,128)S(1)}, f32[16,512]{1,0:T(8,128)S(1)}, u32[]{:S(2)}, u32[]{:S(2)}) collective-permute-start(f32[16,512]{1,0:T(8,128)S(1)} %get-tuple-element.9), channel_id=1, source_target_pairs={{0,2},{2,4},{4,6},{6,8},{8,10},{10,12},{12,14},{14,16},{16,18},{18... | collective-permute-start | bytes 98312 | tf_op jit(solution)/shard_map/ppermute | solution.py:18
  133.2 3.1 %collective-permute-start.7 = (f32[16,512]{1,0:T(8,128)S(1)}, f32[16,512]{1,0:T(8,128)S(1)}, u32[]{:S(2)}, u32[]{:S(2)}) collective-permute-start(f32[16,512]{1,0:T(8,128)S(1)} %get-tuple-element.10), channel_id=1, source_target_pairs={{2,0},{4,2},{6,4},{8,6},{10,8},{12,10},{14,12},{16,14},{18,16},{20... | collective-permute-start | bytes 98312 | tf_op jit(solution)/shard_map/ppermute | solution.py:19
where the time goes:
time: 171 us; the launch traced here: 170 us
  blocking collectives  114 us (67%)
  starting transfers between devices  18.8 us (11%)
  waiting for transfers between devices  13 us (8%)
  other arithmetic  9.87 us (6%)
  local copies, waits for them, and re-layouts  9.63 us (6%)
  matrix products  4.63 us (3%)
    psum x1, blocking collectives, local(): gram_matrix, rayleigh = lax.psum((gram_part, rayleigh_part), 'rows')  62.2 us
    psum x1, blocking collectives, local(): squares = lax.psum(jnp.sum(smooth * smooth, axis=1), 'rows')  31.7 us
    all_to_all x1, blocking collectives, local(): lax.all_to_all(to_slots(product, owner_dev, row_devices), 'rows', split_a...  14.6 us
    all_to_all x1, waiting for transfers between devices, local(): lax.all_to_all(to_slots(remain, owner_dev, row_devices), 'rows', split_ax...  7.32 us
    ppermute x4, starting transfers between devices, extended(): before = lax.ppermute(last, axis, up)  6.26 us
    all_gather x1, blocking collectives, local(): all_states = lax.all_gather(states, 'cols', axis=0, tiled=True)  5.51 us
    ppermute x4, starting transfers between devices, extended(): after = lax.ppermute(initial, axis, down)  5.17 us
    scatter x3, local copies, waits for them, and re-layouts, to_slots(): return empty.at[:, owner_dev].set(values)  3.89 us
  transfers between devices with their start and end apart: 10, of which 4 were waited for; matrix products, arithmetic and copies ran while one was open for 5% of the time, Pallas kernels for 0%

commit v1 on v0

--- a/solution.py
+++ b/solution.py
@@ -28,6 +28,25 @@
 
 def from_slots(arrived, owner_dev):
     return arrived[:, owner_dev]
+
+
+def summed(value, axis):
+    peers, stride = (lax.axis_size(axis), 1)
+    while stride < peers:
+        left = peers // stride
+        radix = 4 if left % 4 == 0 else (2 if left % 2 == 0 else left)
+        total = value
+        for step in range(1, radix):
+            pairs = []
+            for i in range(peers):
+                digit = (i // stride) % radix
+                pairs.append((i, i + ((digit + step) % radix - digit) * stride))
+            if radix in (2, 4):
+                pairs = [(i, i ^ (step * stride)) for i in range(peers)]
+            total = total + lax.ppermute(value, axis, pairs)
+        value = total
+        stride *= radix
+    return value
 
 
 def solve_ritz(gram_matrix, rayleigh):
@@ -63,7 +82,9 @@
     all_states = lax.all_gather(states, "cols", axis=0, tiled=True)
     gram_part = jnp.einsum("cv,dv->cd", all_states * degree, all_states, precision=EXACT)
     rayleigh_part = jnp.einsum("cv,dv->cd", all_states, applied, precision=EXACT)
-    gram_matrix, rayleigh = lax.psum((gram_part, rayleigh_part), "rows")
+    both = summed(jnp.concatenate([gram_part, rayleigh_part], axis=1), "rows")
+    columns = gram_part.shape[1]
+    gram_matrix, rayleigh = both[:, :columns], both[:, columns:]
     ritz_matrix = solve_ritz(gram_matrix, rayleigh)
     residual = applied - degree * jnp.einsum("cd,cv->dv", ritz_matrix, all_states, precision=EXACT)
     presmooth = DAMPING * residual / degree
@@ -95,7 +116,7 @@
     coarse_fix = coarse_fix + DAMPING * (coarse - coarse_image) / coarse_degree
     second = presmooth + coarse_fix
     smooth = second + DAMPING * (residual - operate(second)) / degree
-    squares = lax.psum(jnp.sum(smooth * smooth, axis=1), "rows")
+    squares = summed(jnp.sum(smooth * smooth, axis=1), "rows")
     return smooth / jnp.sqrt(squares / (vertices * row_devices) + EPSILON)[:, None]
 
 

time: 171 us -> 112 us (0.65)
  blocking collectives: 114 us -> 20.1 us
  starting transfers between devices: 18.8 us -> 40.8 us
  waiting for transfers between devices: 13 us -> 25.8 us
    psum x2 -> x0, blocking collectives: 94 us -> none  [the longest x1 62.2 us: local(): gram_matrix, rayleigh = lax.psum((gram_part, rayleigh_part), 'rows')]
    ppermute x0 -> x12, starting transfers between devices: none -> 18.2 us  [summed(): total = total + lax.ppermute(value, axis, pairs)]
    ppermute x0 -> x12, waiting for transfers between devices: none -> 12.8 us  [summed(): total = total + lax.ppermute(value, axis, pairs)]
    all_to_all x1, starting transfers between devices: 3.47 us -> 7.28 us  [local(): lax.all_to_all(to_slots(degree_blocks, owner_dev, row_devices), 'rows', s...]
  transfers between devices with their start and end apart: 10 -> 22, of which waited for: 4 -> 12; matrix products, arithmetic and copies ran while one was open for 5% -> 8% of each run, Pallas kernels for 0% -> 0%
where the time goes in v1:
time: 112 us; the launch traced here: 111 us
  starting transfers between devices  40.8 us (36%)
  waiting for transfers between devices  25.8 us (23%)
  blocking collectives  20.1 us (18%)
  other arithmetic  9.94 us (9%)
  local copies, waits for them, and re-layouts  9.64 us (9%)
  matrix products  4.63 us (4%)
    ppermute x12, starting transfers between devices, summed(): total = total + lax.ppermute(value, axis, pairs)  18.2 us
    all_to_all x1, blocking collectives, local(): lax.all_to_all(to_slots(product, owner_dev, row_devices), 'rows', split_a...  14.6 us
    ppermute x12, waiting for transfers between devices, summed(): total = total + lax.ppermute(value, axis, pairs)  12.8 us
    all_to_all x1, waiting for transfers between devices, local(): lax.all_to_all(to_slots(remain, owner_dev, row_devices), 'rows', split_ax...  7.32 us
    all_to_all x1, starting transfers between devices, local(): lax.all_to_all(to_slots(degree_blocks, owner_dev, row_devices), 'rows', s...  7.28 us
    ppermute x4, starting transfers between devices, extended(): before = lax.ppermute(last, axis, up)  6.26 us
    all_gather x1, blocking collectives, local(): all_states = lax.all_gather(states, 'cols', axis=0, tiled=True)  5.51 us
    ppermute x4, starting transfers between devices, extended(): after = lax.ppermute(initial, axis, down)  5.17 us
  transfers between devices with their start and end apart: 22, of which 12 were waited for; matrix products, arithmetic and copies ran while one was open for 8% of the time, Pallas kernels for 0%

profile of v1, /device:TPU:0, one launch (start us, length us, event | category | flops | bytes accessed | tf_op | source)
XLA Modules:
  0.0 111.4 jit_solution(8021162609525432681)
XLA Ops:
  0.8 2.4 %collective-permute-start = (f32[16,512]{1,0:T(8,128)S(1)}, f32[16,512]{1,0:T(8,128)S(1)}, u32[]{:S(2)}, u32[]{:S(2)}) collective-permute-start(f32[16,512]{1,0:T(8,128)S(1)} %get-tuple-element.13), channel_id=1, source_target_pairs={{0,2},{2,4},{4,6},{6,8},{8,10},{10,12},{12,14},{14,16},{16,18},{18... | collective-permute-start | bytes 98312 | tf_op jit(solution)/shard_map/ppermute | solution.py:18
  3.2 1.3 %collective-permute-start.1 = (f32[16,512]{1,0:T(8,128)S(1)}, f32[16,512]{1,0:T(8,128)S(1)}, u32[]{:S(2)}, u32[]{:S(2)}) collective-permute-start(f32[16,512]{1,0:T(8,128)S(1)} %get-tuple-element.14), channel_id=1, source_target_pairs={{2,0},{4,2},{6,4},{8,6},{10,8},{12,10},{14,12},{16,14},{18,16},{20... | collective-permute-start | bytes 98312 | tf_op jit(solution)/shard_map/ppermute | solution.py:19
  4.5 5.5 %all_gather.3 = f32[32,1024]{1,0:T(8,128)S(1)} all-gather(f32[16,1024]{1,0:T(8,128)} %param.4), channel_id=1, replica_groups=mesh['rows'=16,'cols'=2] {'cols'}, dimensions={0}, use_global_device_ids=true | all-gather | bytes 196608 | tf_op jit(solution)/shard_map/all_gather | solution.py:82
  10.9 1.4 %convert_reduce_fusion = f32[8,128]{1,0:T(8,128)S(1)} fusion(bf16[8,3,128,128]{3,2,1,0:T(8,128)(2,1)} %param.5), kind=kLoop, calls=%fused_computation.10 | loop fusion | flops 785408 | bytes 790528 | tf_op jit(solution)/shard_map/reduce_sum | solution.py:65
  14.4 4.5 %collective-permute-start.3 = (f32[32,48]{0,1:T(8,128)S(1)}, f32[32,48]{0,1:T(8,128)S(1)}, u32[]{:S(2)}, u32[]{:S(2)}) collective-permute-start(f32[32,48]{0,1:T(8,128)S(1)} %pad_maximum_fusion), channel_id=1, source_target_pairs={{0,4},{2,6},{4,0},{6,2},{8,12},{10,14},{12,8},{14,10},{16,20},{18,... | collective-permute-start | bytes 18440 | tf_op jit(solution)/shard_map/ppermute | solution.py:46
  19.1 1.6 %collective-permute-done.3 = f32[32,48]{0,1:T(8,128)S(1)} collective-permute-done((f32[32,48]{0,1:T(8,128)S(1)}, f32[32,48]{0,1:T(8,128)S(1)}, u32[]{:S(2)}, u32[]{:S(2)}) %collective-permute-start.3) | collective-permute-done | bytes 6176 | tf_op jit(solution)/shard_map/ppermute | solution.py:46
  20.8 1.4 %collective-permute-done.4 = f32[32,48]{0,1:T(8,128)S(1)} collective-permute-done((f32[32,48]{0,1:T(8,128)S(1)}, f32[32,48]{0,1:T(8,128)S(1)}, u32[]{:S(2)}, u32[]{:S(2)}) %collective-permute-start.4) | collective-permute-done | bytes 6176 | tf_op jit(solution)/shard_map/ppermute | solution.py:46
  22.2 3.9 %collective-permute-start.7 = (f32[32,48]{0,1:T(8,128)S(1)}, f32[32,48]{0,1:T(8,128)S(1)}, u32[]{:S(2)}, u32[]{:S(2)}) collective-permute-start(f32[32,48]{0,1:T(8,128)S(1)} %add_add_fusion.1), channel_id=1, source_target_pairs={{0,24},{2,26},{4,28},{6,30},{8,16},{10,18},{12,20},{14,22},{16,8},... | collective-permute-start | bytes 18440 | tf_op jit(solution)/shard_map/ppermute | solution.py:46
  26.8 1.2 %collective-permute-done.7 = f32[32,48]{0,1:T(8,128)S(1)} collective-permute-done((f32[32,48]{0,1:T(8,128)S(1)}, f32[32,48]{0,1:T(8,128)S(1)}, u32[]{:S(2)}, u32[]{:S(2)}) %collective-permute-start.7) | collective-permute-done | bytes 6176 | tf_op jit(solution)/shard_map/ppermute | solution.py:46
  28.0 2.9 %collective-permute-done.6 = f32[32,48]{0,1:T(8,128)S(1)} collective-permute-done((f32[32,48]{0,1:T(8,128)S(1)}, f32[32,48]{0,1:T(8,128)S(1)}, u32[]{:S(2)}, u32[]{:S(2)}) %collective-permute-start.6) | collective-permute-done | bytes 6176 | tf_op jit(solution)/shard_map/ppermute | solution.py:46
  31.0 2.9 %cholesky.16 = f32[32,32]{1,0:T(8,128)S(1)} custom-call(f32[32,32]{1,0:T(8,128)S(1)} %fusion.20), custom_call_target="Cholesky" | custom-call | tf_op jit(solution)/shard_map/jit(cholesky)/cholesky | solution.py:53
  35.2 2.4 %custom-call.10 = f32[1,32,32]{1,2,0:T(8,128)S(1)} custom-call(f32[1,32,32]{2,1,0:T(8,128)S(1)} %fusion.15), custom_call_target="InvertDiagBlocksLowerTriangular" | custom-call | tf_op jit(solution)/shard_map/jit(_cho_solve)/triangular_solve | solution.py:54
  38.2 1.3 %collective-permute-start.8 = (f32[16,512]{1,0:T(8,128)S(1)}, f32[16,512]{1,0:T(8,128)S(1)}, u32[]{:S(2)}, u32[]{:S(2)}) collective-permute-start(f32[16,512]{1,0:T(8,128)S(1)} %get-tuple-element.11), channel_id=1, source_target_pairs={{0,2},{2,4},{4,6},{6,8},{8,10},{10,12},{12,14},{14,16},{16,18},{18... | collective-permute-start | bytes 98312 | tf_op jit(solution)/shard_map/ppermute | solution.py:18
  39.5 1.3 %collective-permute-start.9 = (f32[16,512]{1,0:T(8,128)S(1)}, f32[16,512]{1,0:T(8,128)S(1)}, u32[]{:S(2)}, u32[]{:S(2)}) collective-permute-start(f32[16,512]{1,0:T(8,128)S(1)} %get-tuple-element.12), channel_id=1, source_target_pairs={{2,0},{4,2},{6,4},{8,6},{10,8},{12,10},{14,12},{16,14},{18,16},{20... | collective-permute-start | bytes 98312 | tf_op jit(solution)/shard_map/ppermute | solution.py:19
  40.9 1.2 %scatter_custom_fusion.1 = f32[16,128]{1,0:T(8,128)} fusion(s32[8]{0:T(128)S(1)} %compare_select_fusion.1, f32[8,128]{1,0:T(8,128)S(1)} %convert_reduce_fusion, f32[]{:T(128)} %constant.73.clone.1), kind=kCustom, calls=%fused_computation.71 | custom fusion | bytes 8196 | tf_op jit(solution)/shard_map/scatter | solution.py:26
  42.0 7.3 %all-to-all-start.1 = ((f32[1,16,128]{2,0,1:T(1,128)}), f32[1,16,128]{2,0,1:T(1,128)S(1)}, u32[]{:S(2)}, u32[]{:S(2)}) async-start(f32[1,16,128]{2,0,1:T(1,128)} %bitcast.17), calls=%async_computation.1 | async-start | bytes 16384 | tf_op jit(solution)/shard_map/all_to_all | solution.py:100
  51.6 2.0 %scatter_fusion = f32[16,16,128]{2,0,1:T(8,128)} fusion(f32[16,16,128]{2,0,1:T(8,128)} %broadcast.109.clone, s32[8]{0:T(128)S(1)} %compare_select_fusion.1, f32[8,16,128]{2,1,0:T(8,128)S(1)} %bitcast_bitcast_fusion.1), kind=kCustom, calls=%fused_computation.7 | custom fusion | bytes 196640 | tf_op jit(solution)/shard_map/scatter | solution.py:26
  53.6 2.1 %all-to-all-done.1 = f32[1,16,128]{2,0,1:T(1,128)S(1)} async-done(((f32[1,16,128]{2,0,1:T(1,128)}), f32[1,16,128]{2,0,1:T(1,128)S(1)}, u32[]{:S(2)}, u32[]{:S(2)}) %all-to-all-start.1) | async-done | bytes 8224 | tf_op jit(solution)/shard_map/all_to_all | solution.py:100
  55.7 3.9 %all-to-all-start = ((f32[16,16,128]{2,0,1:T(8,128)}), f32[16,16,128]{2,0,1:T(8,128)S(1)}, u32[]{:S(2)}, u32[]{:S(2)}) async-start(f32[16,16,128]{2,0,1:T(8,128)} %scatter_fusion), calls=%async_computation | async-start | bytes 262144 | tf_op jit(solution)/shard_map/all_to_all | solution.py:93
  60.2 7.3 %all-to-all-done = f32[16,16,128]{2,0,1:T(8,128)S(1)} async-done(((f32[16,16,128]{2,0,1:T(8,128)}), f32[16,16,128]{2,0,1:T(8,128)S(1)}, u32[]{:S(2)}, u32[]{:S(2)}) %all-to-all-start) | async-done | bytes 131104 | tf_op jit(solution)/shard_map/all_to_all | solution.py:93
  68.1 1.3 %collective-permute-start.10 = (f32[16,512]{1,0:T(8,128)S(1)}, f32[16,512]{1,0:T(8,128)S(1)}, u32[]{:S(2)}, u32[]{:S(2)}) collective-permute-start(f32[16,512]{1,0:T(8,128)S(1)} %get-tuple-element.9), channel_id=1, source_target_pairs={{0,2},{2,4},{4,6},{6,8},{8,10},{10,12},{12,14},{14,16},{16,18},{18... | collective-permute-start | bytes 98312 | tf_op jit(solution)/shard_map/ppermute | solution.py:18
  69.4 1.3 %collective-permute-start.11 = (f32[16,512]{1,0:T(8,128)S(1)}, f32[16,512]{1,0:T(8,128)S(1)}, u32[]{:S(2)}, u32[]{:S(2)}) collective-permute-start(f32[16,512]{1,0:T(8,128)S(1)} %get-tuple-element.10), channel_id=1, source_target_pairs={{2,0},{4,2},{6,4},{8,6},{10,8},{12,10},{14,12},{16,14},{18,16},{20... | collective-permute-start | bytes 98312 | tf_op jit(solution)/shard_map/ppermute | solution.py:19
  70.7 1.8 %collective-permute-done.11 = f32[16,512]{1,0:T(8,128)S(1)} collective-permute-done((f32[16,512]{1,0:T(8,128)S(1)}, f32[16,512]{1,0:T(8,128)S(1)}, u32[]{:S(2)}, u32[]{:S(2)}) %collective-permute-start.11) | collective-permute-done | bytes 32800 | tf_op jit(solution)/shard_map/ppermute | solution.py:19
  74.8 14.6 %all_to_all.15 = f32[16,16,128]{2,0,1:T(8,128)S(1)} all-to-all(f32[16,16,128]{2,0,1:T(8,128)S(1)} %scatter_fusion.1), channel_id=1, replica_groups=mesh['rows'=16,'cols'=2] {'rows'}, dimensions={1} | all-to-all | bytes 262144 | tf_op jit(solution)/shard_map/all_to_all | solution.py:112
  90.0 1.3 %collective-permute-start.12 = (f32[16,512]{1,0:T(8,128)S(1)}, f32[16,512]{1,0:T(8,128)S(1)}, u32[]{:S(2)}, u32[]{:S(2)}) collective-permute-start(f32[16,512]{1,0:T(8,128)S(1)} %get-tuple-element.7), channel_id=1, source_target_pairs={{0,2},{2,4},{4,6},{6,8},{8,10},{10,12},{12,14},{14,16},{16,18},{18... | collective-permute-start | bytes 98312 | tf_op jit(solution)/shard_map/ppermute | solution.py:18
  91.3 1.3 %collective-permute-start.13 = (f32[16,512]{1,0:T(8,128)S(1)}, f32[16,512]{1,0:T(8,128)S(1)}, u32[]{:S(2)}, u32[]{:S(2)}) collective-permute-start(f32[16,512]{1,0:T(8,128)S(1)} %get-tuple-element.8), channel_id=1, source_target_pairs={{2,0},{4,2},{6,4},{8,6},{10,8},{12,10},{14,12},{16,14},{18,16},{20... | collective-permute-start | bytes 98312 | tf_op jit(solution)/shard_map/ppermute | solution.py:19
  92.6 1.8 %collective-permute-done.13 = f32[16,512]{1,0:T(8,128)S(1)} collective-permute-done((f32[16,512]{1,0:T(8,128)S(1)}, f32[16,512]{1,0:T(8,128)S(1)}, u32[]{:S(2)}, u32[]{:S(2)}) %collective-permute-start.13) | collective-permute-done | bytes 32800 | tf_op jit(solution)/shard_map/ppermute | solution.py:19
  96.1 4.3 %collective-permute-start.16 = (f32[16]{0:T(128)S(1)}, f32[16]{0:T(128)S(1)}, u32[]{:S(2)}, u32[]{:S(2)}) collective-permute-start(f32[16]{0:T(128)S(1)} %get-tuple-element.5), channel_id=1, source_target_pairs={{0,6},{2,4},{4,2},{6,0},{8,14},{10,12},{12,10},{14,8},{16,22},{18,... | collective-permute-start | bytes 200 | tf_op jit(solution)/shard_map/ppermute | solution.py:46
  101.6 2.3 %collective-permute-done.15 = f32[16]{0:T(128)S(1)} collective-permute-done((f32[16]{0:T(128)S(1)}, f32[16]{0:T(128)S(1)}, u32[]{:S(2)}, u32[]{:S(2)}) %collective-permute-start.15) | collective-permute-done | bytes 96 | tf_op jit(solution)/shard_map/ppermute | solution.py:46
  104.2 2.9 %collective-permute-start.18 = (f32[16]{0:T(128)S(1)}, f32[16]{0:T(128)S(1)}, u32[]{:S(2)}, u32[]{:S(2)}) collective-permute-start(f32[16]{0:T(128)S(1)} %add_add_fusion.2), channel_id=1, source_target_pairs={{0,16},{2,18},{4,20},{6,22},{8,24},{10,26},{12,28},{14,30},{16,0},... | collective-permute-start | bytes 200 | tf_op jit(solution)/shard_map/ppermute | solution.py:46
  107.1 1.3 %collective-permute-start.17 = (f32[16]{0:T(128)S(1)}, f32[16]{0:T(128)S(1)}, u32[]{:S(2)}, u32[]{:S(2)}) collective-permute-start(f32[16]{0:T(128)S(1)} %add_add_fusion.2), channel_id=1, source_target_pairs={{0,8},{2,10},{4,12},{6,14},{8,0},{10,2},{12,4},{14,6},{16,24},{18,... | collective-permute-start | bytes 200 | tf_op jit(solution)/shard_map/ppermute | solution.py:46
  109.4 1.3 %collective-permute-done.17 = f32[16]{0:T(128)S(1)} collective-permute-done((f32[16]{0:T(128)S(1)}, f32[16]{0:T(128)S(1)}, u32[]{:S(2)}, u32[]{:S(2)}) %collective-permute-start.17) | collective-permute-done | bytes 96 | tf_op jit(solution)/shard_map/ppermute | solution.py:46
  (76 shorter events, 17.7 us)
Async XLA Ops:
  0.0 12.6 %copy-start.1 = (f32[16,1024]{1,0:T(8,128)S(1)}, f32[16,1024]{1,0:T(8,128)}, u32[]{:S(2)}) copy-start(f32[16,1024]{1,0:T(8,128)} %param.4) | copy-start | bytes 196612
  0.8 11.8 %collective-permute-start = (f32[16,512]{1,0:T(8,128)S(1)}, f32[16,512]{1,0:T(8,128)S(1)}, u32[]{:S(2)}, u32[]{:S(2)}) collective-permute-start(f32[16,512]{1,0:T(8,128)S(1)} %get-tuple-element.13), channel_id=1, source_target_pairs={{0,2},{2,4},{4,6},{6,8},{8,10},{10,12},{12,14},{14,16},{16,18},{18... | collective-permute-start | bytes 98312 | tf_op jit(solution)/shard_map/ppermute | solution.py:18
  3.2 9.4 %collective-permute-start.1 = (f32[16,512]{1,0:T(8,128)S(1)}, f32[16,512]{1,0:T(8,128)S(1)}, u32[]{:S(2)}, u32[]{:S(2)}) collective-permute-start(f32[16,512]{1,0:T(8,128)S(1)} %get-tuple-element.14), channel_id=1, source_target_pairs={{2,0},{4,2},{6,4},{8,6},{10,8},{12,10},{14,12},{16,14},{18,16},{20... | collective-permute-start | bytes 98312 | tf_op jit(solution)/shard_map/ppermute | solution.py:19
  10.9 2.3 %copy-start = (bf16[8,3,128,128]{3,2,1,0:T(8,128)(2,1)S(1)}, bf16[8,3,128,128]{3,2,1,0:T(8,128)(2,1)}, u32[]{:S(2)}) copy-start(bf16[8,3,128,128]{3,2,1,0:T(8,128)(2,1)} %param.5) | copy-start | bytes 2359300
  14.2 26.7 %copy-start.2 = (s32[8]{0:T(128)S(1)}, s32[8]{0:T(128)}, u32[]{:S(2)}) copy-start(s32[8]{0:T(128)} %param.7) | copy-start | bytes 100
  14.4 6.3 %collective-permute-start.3 = (f32[32,48]{0,1:T(8,128)S(1)}, f32[32,48]{0,1:T(8,128)S(1)}, u32[]{:S(2)}, u32[]{:S(2)}) collective-permute-start(f32[32,48]{0,1:T(8,128)S(1)} %pad_maximum_fusion), channel_id=1, source_target_pairs={{0,4},{2,6},{4,0},{6,2},{8,12},{10,14},{12,8},{14,10},{16,20},{18,... | collective-permute-start | bytes 18440 | tf_op jit(solution)/shard_map/ppermute | solution.py:46
  19.0 3.3 %collective-permute-start.4 = (f32[32,48]{0,1:T(8,128)S(1)}, f32[32,48]{0,1:T(8,128)S(1)}, u32[]{:S(2)}, u32[]{:S(2)}) collective-permute-start(f32[32,48]{0,1:T(8,128)S(1)} %pad_maximum_fusion), channel_id=1, source_target_pairs={{0,6},{2,4},{4,2},{6,0},{8,14},{10,12},{12,10},{14,8},{16,22},{18,... | collective-permute-start | bytes 18440 | tf_op jit(solution)/shard_map/ppermute | solution.py:46
  19.0 3.3 %collective-permute-start.2 = (f32[32,48]{0,1:T(8,128)S(1)}, f32[32,48]{0,1:T(8,128)S(1)}, u32[]{:S(2)}, u32[]{:S(2)}) collective-permute-start(f32[32,48]{0,1:T(8,128)S(1)} %pad_maximum_fusion), channel_id=1, source_target_pairs={{0,2},{2,0},{4,6},{6,4},{8,10},{10,8},{12,14},{14,12},{16,18},{18,... | collective-permute-start | bytes 18440 | tf_op jit(solution)/shard_map/ppermute | solution.py:46
  22.2 5.7 %collective-permute-start.7 = (f32[32,48]{0,1:T(8,128)S(1)}, f32[32,48]{0,1:T(8,128)S(1)}, u32[]{:S(2)}, u32[]{:S(2)}) collective-permute-start(f32[32,48]{0,1:T(8,128)S(1)} %add_add_fusion.1), channel_id=1, source_target_pairs={{0,24},{2,26},{4,28},{6,30},{8,16},{10,18},{12,20},{14,22},{16,8},... | collective-permute-start | bytes 18440 | tf_op jit(solution)/shard_map/ppermute | solution.py:46
  26.2 4.7 %collective-permute-start.6 = (f32[32,48]{0,1:T(8,128)S(1)}, f32[32,48]{0,1:T(8,128)S(1)}, u32[]{:S(2)}, u32[]{:S(2)}) collective-permute-start(f32[32,48]{0,1:T(8,128)S(1)} %add_add_fusion.1), channel_id=1, source_target_pairs={{0,16},{2,18},{4,20},{6,22},{8,24},{10,26},{12,28},{14,30},{16,0},... | collective-permute-start | bytes 18440 | tf_op jit(solution)/shard_map/ppermute | solution.py:46
  26.2 4.7 %collective-permute-start.5 = (f32[32,48]{0,1:T(8,128)S(1)}, f32[32,48]{0,1:T(8,128)S(1)}, u32[]{:S(2)}, u32[]{:S(2)}) collective-permute-start(f32[32,48]{0,1:T(8,128)S(1)} %add_add_fusion.1), channel_id=1, source_target_pairs={{0,8},{2,10},{4,12},{6,14},{8,0},{10,2},{12,4},{14,6},{16,24},{18,... | collective-permute-start | bytes 18440 | tf_op jit(solution)/shard_map/ppermute | solution.py:46
  38.2 11.1 %collective-permute-start.8 = (f32[16,512]{1,0:T(8,128)S(1)}, f32[16,512]{1,0:T(8,128)S(1)}, u32[]{:S(2)}, u32[]{:S(2)}) collective-permute-start(f32[16,512]{1,0:T(8,128)S(1)} %get-tuple-element.11), channel_id=1, source_target_pairs={{0,2},{2,4},{4,6},{6,8},{8,10},{10,12},{12,14},{14,16},{16,18},{18... | collective-permute-start | bytes 98312 | tf_op jit(solution)/shard_map/ppermute | solution.py:18
  39.5 9.8 %collective-permute-start.9 = (f32[16,512]{1,0:T(8,128)S(1)}, f32[16,512]{1,0:T(8,128)S(1)}, u32[]{:S(2)}, u32[]{:S(2)}) collective-permute-start(f32[16,512]{1,0:T(8,128)S(1)} %get-tuple-element.12), channel_id=1, source_target_pairs={{2,0},{4,2},{6,4},{8,6},{10,8},{12,10},{14,12},{16,14},{18,16},{20... | collective-permute-start | bytes 98312 | tf_op jit(solution)/shard_map/ppermute | solution.py:19
  42.0 13.6 %all-to-all-start.1 = ((f32[1,16,128]{2,0,1:T(1,128)}), f32[1,16,128]{2,0,1:T(1,128)S(1)}, u32[]{:S(2)}, u32[]{:S(2)}) async-start(f32[1,16,128]{2,0,1:T(1,128)} %bitcast.17), calls=%async_computation.1 | async-start | bytes 16384 | tf_op jit(solution)/shard_map/all_to_all | solution.py:100
  55.7 11.8 %all-to-all-start = ((f32[16,16,128]{2,0,1:T(8,128)}), f32[16,16,128]{2,0,1:T(8,128)S(1)}, u32[]{:S(2)}, u32[]{:S(2)}) async-start(f32[16,16,128]{2,0,1:T(8,128)} %scatter_fusion), calls=%async_computation | async-start | bytes 262144 | tf_op jit(solution)/shard_map/all_to_all | solution.py:93
  68.1 2.6 %collective-permute-start.10 = (f32[16,512]{1,0:T(8,128)S(1)}, f32[16,512]{1,0:T(8,128)S(1)}, u32[]{:S(2)}, u32[]{:S(2)}) collective-permute-start(f32[16,512]{1,0:T(8,128)S(1)} %get-tuple-element.9), channel_id=1, source_target_pairs={{0,2},{2,4},{4,6},{6,8},{8,10},{10,12},{12,14},{14,16},{16,18},{18... | collective-permute-start | bytes 98312 | tf_op jit(solution)/shard_map/ppermute | solution.py:18
  69.4 3.1 %collective-permute-start.11 = (f32[16,512]{1,0:T(8,128)S(1)}, f32[16,512]{1,0:T(8,128)S(1)}, u32[]{:S(2)}, u32[]{:S(2)}) collective-permute-start(f32[16,512]{1,0:T(8,128)S(1)} %get-tuple-element.10), channel_id=1, source_target_pairs={{2,0},{4,2},{6,4},{8,6},{10,8},{12,10},{14,12},{16,14},{18,16},{20... | collective-permute-start | bytes 98312 | tf_op jit(solution)/shard_map/ppermute | solution.py:19
  90.0 2.6 %collective-permute-start.12 = (f32[16,512]{1,0:T(8,128)S(1)}, f32[16,512]{1,0:T(8,128)S(1)}, u32[]{:S(2)}, u32[]{:S(2)}) collective-permute-start(f32[16,512]{1,0:T(8,128)S(1)} %get-tuple-element.7), channel_id=1, source_target_pairs={{0,2},{2,4},{4,6},{6,8},{8,10},{10,12},{12,14},{14,16},{16,18},{18... | collective-permute-start | bytes 98312 | tf_op jit(solution)/shard_map/ppermute | solution.py:18
  91.3 3.1 %collective-permute-start.13 = (f32[16,512]{1,0:T(8,128)S(1)}, f32[16,512]{1,0:T(8,128)S(1)}, u32[]{:S(2)}, u32[]{:S(2)}) collective-permute-start(f32[16,512]{1,0:T(8,128)S(1)} %get-tuple-element.8), channel_id=1, source_target_pairs={{2,0},{4,2},{6,4},{8,6},{10,8},{12,10},{14,12},{16,14},{18,16},{20... | collective-permute-start | bytes 98312 | tf_op jit(solution)/shard_map/ppermute | solution.py:19
  96.1 5.6 %collective-permute-start.16 = (f32[16]{0:T(128)S(1)}, f32[16]{0:T(128)S(1)}, u32[]{:S(2)}, u32[]{:S(2)}) collective-permute-start(f32[16]{0:T(128)S(1)} %get-tuple-element.5), channel_id=1, source_target_pairs={{0,6},{2,4},{4,2},{6,0},{8,14},{10,12},{12,10},{14,8},{16,22},{18,... | collective-permute-start | bytes 200 | tf_op jit(solution)/shard_map/ppermute | solution.py:46
  100.4 3.6 %collective-permute-start.15 = (f32[16]{0:T(128)S(1)}, f32[16]{0:T(128)S(1)}, u32[]{:S(2)}, u32[]{:S(2)}) collective-permute-start(f32[16]{0:T(128)S(1)} %get-tuple-element.5), channel_id=1, source_target_pairs={{0,4},{2,6},{4,0},{6,2},{8,12},{10,14},{12,8},{14,10},{16,20},{18,... | collective-permute-start | bytes 200 | tf_op jit(solution)/shard_map/ppermute | solution.py:46
  100.4 3.6 %collective-permute-start.14 = (f32[16]{0:T(128)S(1)}, f32[16]{0:T(128)S(1)}, u32[]{:S(2)}, u32[]{:S(2)}) collective-permute-start(f32[16]{0:T(128)S(1)} %get-tuple-element.5), channel_id=1, source_target_pairs={{0,2},{2,0},{4,6},{6,4},{8,10},{10,8},{12,14},{14,12},{16,18},{18,... | collective-permute-start | bytes 200 | tf_op jit(solution)/shard_map/ppermute | solution.py:46
  103.9 5.4 %collective-permute-start.19 = (f32[16]{0:T(128)S(1)}, f32[16]{0:T(128)S(1)}, u32[]{:S(2)}, u32[]{:S(2)}) collective-permute-start(f32[16]{0:T(128)S(1)} %add_add_fusion.2), channel_id=1, source_target_pairs={{0,24},{2,26},{4,28},{6,30},{8,16},{10,18},{12,20},{14,22},{16,8},... | collective-permute-start | bytes 200 | tf_op jit(solution)/shard_map/ppermute | solution.py:46
  104.2 5.2 %collective-permute-start.18 = (f32[16]{0:T(128)S(1)}, f32[16]{0:T(128)S(1)}, u32[]{:S(2)}, u32[]{:S(2)}) collective-permute-start(f32[16]{0:T(128)S(1)} %add_add_fusion.2), channel_id=1, source_target_pairs={{0,16},{2,18},{4,20},{6,22},{8,24},{10,26},{12,28},{14,30},{16,0},... | collective-permute-start | bytes 200 | tf_op jit(solution)/shard_map/ppermute | solution.py:46
  107.1 3.6 %collective-permute-start.17 = (f32[16]{0:T(128)S(1)}, f32[16]{0:T(128)S(1)}, u32[]{:S(2)}, u32[]{:S(2)}) collective-permute-start(f32[16]{0:T(128)S(1)} %add_add_fusion.2), channel_id=1, source_target_pairs={{0,8},{2,10},{4,12},{6,14},{8,0},{10,2},{12,4},{14,6},{16,24},{18,... | collective-permute-start | bytes 200 | tf_op jit(solution)/shard_map/ppermute | solution.py:46

commit v2 on v0

v2 whole, which is shorter than its diff:
```python
import jax
import jax.numpy as jnp
from jax import lax
from jax.experimental import pallas as pl
from jax.experimental.pallas import tpu as pltpu
from jax.sharding import PartitionSpec as P

DAMPING = 2.0 / 3.0
KEEP = 1.0 - DAMPING
EPSILON = 1e-06
EXACT = lax.Precision.HIGHEST
PARTS = 3
F32 = jnp.float32
IN_VMEM = pl.BlockSpec(memory_space=pltpu.VMEM)
IN_SMEM = pl.BlockSpec(memory_space=pltpu.SMEM)


def kernel_call(body, name, outs, scalars, arrays, scratch=(), cost=2_000_000):
    return pl.pallas_call(
        body,
        name=name,
        out_shape=[jax.ShapeDtypeStruct(shape, F32) for shape in outs],
        in_specs=[IN_SMEM] * len(scalars) + [IN_VMEM] * len(arrays),
        out_specs=[IN_VMEM] * len(outs),
        scratch_shapes=list(scratch),
        cost_estimate=pl.CostEstimate(flops=cost, bytes_accessed=cost, transcendentals=0),
    )(*scalars, *arrays)


def radices(peers):
    found = []
    while peers > 1:
        found.append(4 if peers % 4 == 0 else 2)
        peers //= found[-1]
    return found


def exchanged(value, axis, stride, radix):
    peers = lax.axis_size(axis)
    return [value] + [
        lax.ppermute(value, axis, [(i, i ^ (mask * stride)) for i in range(peers)])
        for mask in range(1, radix)
    ]


def from_sides(last, first, axis):
    peers = lax.axis_size(axis)
    up = [(i, i + 1) for i in range(peers - 1)]
    return lax.ppermute(last, axis, up), lax.ppermute(first, axis, [(j, i) for i, j in up])


def each(count, body):
    if count <= 8:
        for step in range(count):
            body(step)
    else:
        lax.fori_loop(0, count, lambda step, carry: (body(step), carry)[1], 0)


def lanes(block, length):
    start = block * length
    return pl.ds(start if isinstance(block, int) else pl.multiple_of(start, length), length)


def padded(value, rows):
    if value.shape[0] == rows:
        return value
    return jnp.concatenate([value, jnp.zeros((rows - value.shape[0], value.shape[1]), F32)], axis=0)


def in_parts(value):
    pieces = []
    for _ in range(PARTS):
        piece = value.astype(jnp.bfloat16)
        pieces.append(piece)
        value = value - piece.astype(F32)
    return jnp.concatenate(pieces, axis=0)


def fill(field, base, value, length):
    split = in_parts(value)
    for block in range(value.shape[1] // length):
        field[base + block, : split.shape[0], :] = split[:, block * length : (block + 1) * length]


def fill_extended(field, before, own, after, length):
    count = before.shape[1] // length
    fill(field, 0, before, length)
    fill(field, count, own, length)
    fill(field, count + own.shape[1] // length, after, length)


def neighbours(index, weight, field, block):
    blocks = index.shape[0]
    shift = blocks // 2 - index[0, 0]
    total = None
    for k in range(index.shape[1]):
        term = lax.dot_general(
            field[index[block, k] + shift],
            weight[block, k],
            (((1,), (1,)), ((), ())),
            preferred_element_type=F32,
        )
        total = term if total is None else total + term
    return total


def folded(total, rows):
    return total[:rows] + total[rows : 2 * rows] + total[2 * rows : PARTS * rows]


def solved(matrix, size):
    row_id = lax.broadcasted_iota(jnp.int32, matrix.shape, 0)
    for k in range(0, size, 2):
        left = jnp.broadcast_to(matrix[:, k : k + 1], matrix.shape)
        right = jnp.broadcast_to(matrix[:, k + 1 : k + 2], matrix.shape)
        upper, lower = matrix[k : k + 1], matrix[k + 1 : k + 2]
        pivot, cross = left[k : k + 1], right[k : k + 1]
        ratio = left[k + 1 : k + 2] / pivot
        new_lower = (lower - ratio * upper) / (right[k + 1 : k + 2] - ratio * cross)
        new_upper = (upper - cross * new_lower) / pivot
        rest = matrix - left * new_upper - right * new_lower
        matrix = jnp.where(row_id == k, new_upper, jnp.where(row_id == k + 1, new_lower, rest))
    return matrix


def local(states, adj_weight, adj_index, partner):
    local_cols, vertices = states.shape
    blocks, _, length, _ = adj_weight.shape
    row_devices, col_devices = lax.axis_size("rows"), lax.axis_size("cols")
    total_cols = local_cols * col_devices
    width = (blocks // 2) * length
    rows = -(-local_cols // 16) * 16
    stages = radices(row_devices)
    field_shape = (2 * blocks, PARTS * rows, length)
    field = pltpu.VMEM(field_shape, jnp.bfloat16)
    full, edge, line = (rows, vertices), (rows, width), (1, vertices)
    slots = (row_devices, rows, length)

    def first_body(index, weight, before, after, *refs):
        peers, (payload, image, sent, scaled, last, first, degree, ones_field) = (
            refs[:col_devices],
            refs[col_devices:],
        )
        fill_extended(
            ones_field,
            padded(before[...], rows),
            padded(peers[0][...], rows),
            padded(after[...], rows),
            length,
        )
        ones_field[:, PARTS * rows :, :] = jnp.ones((2 * blocks, 16, length), jnp.bfloat16)
        payload[...] = jnp.zeros(payload.shape, F32)

        def one(block):
            total = neighbours(index, weight, ones_field, block)
            here = total[PARTS * rows : PARTS * rows + 1]
            value = folded(total, rows)
            at = lanes(block, length)
            degree[:, at] = here
            payload[pl.ds(total_cols + block, 1), :] = here
            image[:, at] = value
            scaled[:, at] = value / here

        each(blocks, one)
        everyone = jnp.concatenate([peer[...] for peer in peers], axis=0)
        other = jnp.concatenate([everyone * degree[...], image[...]], axis=0)
        payload[:total_cols, : total_cols + rows] = lax.dot_general(
            everyone, other, (((1,), (1,)), ((), ())), precision=EXACT, preferred_element_type=F32
        )
        sent[...] = image[:local_cols, :]
        last[...] = scaled[:, vertices - width :]
        first[...] = scaled[:, :width]

    def second_body(index, weight, before, after, scaled, image, offset, spread):
        fill_extended(spread, before[...], scaled[...], after[...], length)

        def one(block):
            at = lanes(block, length)
            value = folded(neighbours(index, weight, spread, block), rows)
            offset[:, at] = KEEP * image[:, at] + DAMPING * value

        each(blocks, one)

    def ritz_body(index, mates, *refs):
        pieces, refs = refs[: stages[-1]], refs[stages[-1] :]
        peers, refs = refs[:col_devices], refs[col_devices:]
        images, refs = refs[:col_devices], refs[col_devices:]
        own_image, scaled, offset, degree, out, remain, residual, presmooth, pair_degree, table = refs
        group = row_devices // stages[-1] * blocks
        total = pieces[0][:total_cols, :]
        for piece in pieces[1:]:
            total = total + piece[:total_cols, :]
        for place, piece in enumerate(pieces):
            table[place * group : (place + 1) * group, :] = piece[total_cols:, :]
        ritz = jnp.transpose(solved(total, total_cols))[total_cols : total_cols + rows]
        everyone = jnp.concatenate([peer[...] for peer in peers], axis=0)
        spread = jnp.concatenate([image[...] for image in images], axis=0)
        mixed = jnp.dot(ritz, everyone, precision=EXACT, preferred_element_type=F32)
        mixed_image = jnp.dot(ritz, spread, precision=EXACT, preferred_element_type=F32)
        weighted = degree[...] * mixed
        residual[...] = weighted - own_image[...]
        presmooth[...] = DAMPING * (mixed - scaled[...])
        remain[...] = KEEP * weighted + DAMPING * mixed_image - offset[...]
        me = lax.div(index[0, 0], blocks)

        def one(block):
            at = lanes(block, length)
            owner = lax.div(mates[block], blocks)
            row = lax.bitwise_xor(owner, me) * blocks + (mates[block] - owner * blocks)
            out[owner] = remain[:, at]
            pair_degree[:, at] = degree[:, at] + table[pl.ds(row, 1), :]

        each(blocks, one)

    def coarse_body(mates, arrived, remain, pair_degree, coarse, fix, last, first):
        def one(block):
            at = lanes(block, length)
            value = remain[:, at] + arrived[lax.div(mates[block], blocks)]
            coarse[:, at] = value
            fix[:, at] = DAMPING * value / pair_degree[:, at]

        each(blocks, one)
        last[...] = fix[:, vertices - width :]
        first[...] = fix[:, :width]

    def product_body(index, mates, weight, before, after, fix, degree, out, product, spread):
        fill_extended(spread, before[...], fix[...], after[...], length)

        def one(block):
            at = lanes(block, length)
            value = degree[:, at] * fix[:, at] - folded(neighbours(index, weight, spread, block), rows)
            product[:, at] = value
            out[lax.div(mates[block], blocks)] = value

        each(blocks, one)

    def fix_body(mates, arrived, product, coarse, fix, pair_degree, presmooth, second, last, first):
        def one(block):
            at = lanes(block, length)
            image = product[:, at] + arrived[lax.div(mates[block], blocks)]
            step = DAMPING * (coarse[:, at] - image) / pair_degree[:, at]
            second[:, at] = presmooth[:, at] + (fix[:, at] + step)

        each(blocks, one)
        last[...] = second[:, vertices - width :]
        first[...] = second[:, :width]

    def smooth_body(index, weight, before, after, second, residual, degree, smooth, squares, spread):
        fill_extended(spread, before[...], second[...], after[...], length)

        def one(block):
            at = lanes(block, length)
            value, here = second[:, at], degree[:, at]
            image = here * value - folded(neighbours(index, weight, spread, block), rows)
            smooth[:, at] = value + DAMPING * (residual[:, at] - image) / here

        each(blocks, one)
        value = smooth[...]
        squares[...] = jnp.broadcast_to(jnp.sum(value * value, axis=1, keepdims=True), squares.shape)

    def scale_body(*refs):
        smooth, correction = refs[-2:]
        total = refs[0][...]
        for piece in refs[1:-2]:
            total = total + piece[...]
        norm = jnp.sqrt(total[:local_cols, :1] / (vertices * row_devices) + EPSILON)
        correction[...] = smooth[:local_cols, :] / norm

    before, after = from_sides(states[:, vertices - width :], states[:, :width], "rows")
    peers = exchanged(states, "cols", 1, col_devices)
    payload, image, sent, scaled, last, first, degree = kernel_call(
        first_body,
        "image",
        [(total_cols + blocks, length), full, (local_cols, vertices), full, edge, edge, line],
        [adj_index],
        [adj_weight, before, after, *peers],
        [pltpu.VMEM((2 * blocks, PARTS * rows + 16, length), jnp.bfloat16)],
    )
    stride = 1
    for place, radix in enumerate(stages):
        pieces = exchanged(payload, "rows", stride, radix)
        stride *= radix
        if place + 1 < len(stages):
            summed = pieces[0][:total_cols]
            for piece in pieces[1:]:
                summed = summed + piece[:total_cols]
            payload = jnp.concatenate([summed] + [piece[total_cols:] for piece in pieces], axis=0)
    before, after = from_sides(last, first, "rows")
    images = exchanged(sent, "cols", 1, col_devices)
    (offset,) = kernel_call(
        second_body, "offset", [full], [adj_index], [adj_weight, before, after, scaled, image], [field]
    )
    out, remain, residual, presmooth, pair_degree = kernel_call(
        ritz_body,
        "ritz",
        [slots, full, full, full, line],
        [adj_index, partner],
        [*pieces, *peers, *images, image, scaled, offset, degree],
        [pltpu.VMEM((row_devices * blocks, length), F32)],
    )
    arrived = lax.all_to_all(out, "rows", split_axis=0, concat_axis=0, tiled=True)
    coarse, fix, last, first = kernel_call(
        coarse_body, "coarse", [full, full, edge, edge], [partner], [arrived, remain, pair_degree]
    )
    before, after = from_sides(last, first, "rows")
    out, product = kernel_call(
        product_body,
        "product",
        [slots, full],
        [adj_index, partner],
        [adj_weight, before, after, fix, degree],
        [field],
    )
    arrived = lax.all_to_all(out, "rows", split_axis=0, concat_axis=0, tiled=True)
    second, last, first = kernel_call(
        fix_body,
        "fix",
        [full, edge, edge],
        [partner],
        [arrived, product, coarse, fix, pair_degree, presmooth],
    )
    before, after = from_sides(last, first, "rows")
    smooth, squares = kernel_call(
        smooth_body,
        "smooth",
        [full, (rows, length)],
        [adj_index],
        [adj_weight, before, after, second, residual, degree],
        [field],
    )
    stride = 1
    for place, radix in enumerate(stages):
        pieces = exchanged(squares, "rows", stride, radix)
        stride *= radix
        if place + 1 < len(stages):
            squares = pieces[0]
            for piece in pieces[1:]:
                squares = squares + piece
    (correction,) = kernel_call(scale_body, "scale", [states.shape], [], [*pieces, smooth])
    return correction


def solution(mesh):
    return jax.shard_map(
        local,
        mesh=mesh,
        in_specs=(P("cols", "rows"), P("rows", None, None, None), P("rows", None), P("rows")),
        out_specs=P("cols", "rows"),
        check_vma=False,
    )
```

time: 171 us -> 104 us (0.61)
  blocking collectives: 114 us -> 26.9 us
  Pallas kernels: 0 us -> 19.1 us
  starting transfers between devices: 18.8 us -> 37.8 us
  other arithmetic: 9.87 us -> 1.43 us
  matrix products: 4.63 us -> 0 us
  local copies, waits for them, and re-layouts: 9.63 us -> 6.42 us
    psum x2 -> x0, blocking collectives: 94 us -> none  [the longest x1 62.2 us: local(): gram_matrix, rayleigh = lax.psum((gram_part, rayleigh_part), 'rows')]
    ppermute x8 -> x22, starting transfers between devices: 11.4 us -> 37.8 us  [the longest x14 24.7 us: exchanged(): lax.ppermute(value, axis, [(i, i ^ mask * stride) for i in range(peers)])]
    pallas_call x0 -> x8, Pallas kernels: none -> 19.1 us  [kernel_call(): pl.pallas_call(body, name=name, out_shape=[jax.ShapeDtypeStruct(shape, F3...]
    all_to_all x1 -> x2, blocking collectives: 14.6 us -> 26.9 us  [local(): lax.all_to_all(out, 'rows', split_axis=0, concat_axis=0, tiled=True)]
    all_to_all x2 -> x0, waiting for transfers between devices: 9.41 us -> none  [the longest x1 7.32 us: local(): lax.all_to_all(to_slots(remain, owner_dev, row_devices), 'rows', split_ax...]
    ppermute x8 -> x22, waiting for transfers between devices: 3.6 us -> 11.4 us  [the longest x14 7.22 us: exchanged(): lax.ppermute(value, axis, [(i, i ^ mask * stride) for i in range(peers)])]
    all_to_all x2 -> x0, starting transfers between devices: 7.34 us -> none  [the longest x1 3.87 us: local(): lax.all_to_all(to_slots(remain, owner_dev, row_devices), 'rows', split_ax...]
    another operation x5 -> x0, other arithmetic: 6.68 us -> none  [the longest x3 3.59 us: solve_ritz(): factor = jnp.linalg.cholesky(gram_matrix)]
  transfers between devices with their start and end apart: 10 -> 22, of which waited for: 4 -> 8; matrix products, arithmetic and copies ran while one was open for 5% -> 3% of each run, Pallas kernels for 0% -> 2%
where the time goes in v2:
time: 104 us; the launch traced here: 103 us
  starting transfers between devices  37.8 us (36%)
  blocking collectives  26.9 us (26%)
  Pallas kernels  19.1 us (18%)
  waiting for transfers between devices  11.4 us (11%)
  local copies, waits for them, and re-layouts  6.42 us (6%)
  other arithmetic  1.43 us (1%)
    all_to_all x2, blocking collectives, local(): lax.all_to_all(out, 'rows', split_axis=0, concat_axis=0, tiled=True)  26.9 us
    ppermute x14, starting transfers between devices, exchanged(): lax.ppermute(value, axis, [(i, i ^ mask * stride) for i in range(peers)])  24.7 us
    pallas_call x8, Pallas kernels, kernel_call(): pl.pallas_call(body, name=name, out_shape=[jax.ShapeDtypeStruct(shape, F3...  19.1 us
    ppermute x4, starting transfers between devices, from_sides(): lax.ppermute(last, axis, up)  7.95 us
    ppermute x14, waiting for transfers between devices, exchanged(): lax.ppermute(value, axis, [(i, i ^ mask * stride) for i in range(peers)])  7.22 us
    unnamed x42, local copies, waits for them, and re-layouts  5.62 us
    ppermute x4, starting transfers between devices, from_sides(): lax.ppermute(first, axis, [(j, i) for i, j in up])  5.17 us
    ppermute x4, waiting for transfers between devices, from_sides(): lax.ppermute(first, axis, [(j, i) for i, j in up])  3.99 us
  transfers between devices with their start and end apart: 22, of which 8 were waited for; matrix products, arithmetic and copies ran while one was open for 3% of the time, Pallas kernels for 2%

profile of v2, /device:TPU:0, one launch (start us, length us, event | category | flops | bytes accessed | tf_op | source)
XLA Modules:
  0.0 103.2 jit_solution(773791629431027098)
XLA Ops:
  0.0 3.0 %collective-permute-start.2 = (f32[16,1024]{1,0:T(8,128)}, f32[16,1024]{1,0:T(8,128)S(1)}, u32[]{:S(2)}, u32[]{:S(2)}) collective-permute-start(f32[16,1024]{1,0:T(8,128)} %refs_4_.1), channel_id=1, source_target_pairs={{0,1},{1,0},{2,3},{3,2},{4,5},{5,4},{6,7},{7,6},{8,9},{9,8},{10,11... | collective-permute-start | bytes 196616 | tf_op jit(solution)/shard_map/ppermute | solution.py:41
  3.0 0.8 fusion.1
  3.8 1.3 %collective-permute-start.1 = (f32[16,512]{1,0:T(8,128)S(1)}, f32[16,512]{1,0:T(8,128)S(1)}, u32[]{:S(2)}, u32[]{:S(2)}) collective-permute-start(f32[16,512]{1,0:T(8,128)S(1)} %get-tuple-element.51), channel_id=1, source_target_pairs={{2,0},{4,2},{6,4},{8,6},{10,8},{12,10},{14,12},{16,14},{18,16},{20... | collective-permute-start | bytes 98312 | tf_op jit(solution)/shard_map/ppermute | solution.py:49
  5.1 3.0 %collective-permute-start = (f32[16,512]{1,0:T(8,128)S(1)}, f32[16,512]{1,0:T(8,128)S(1)}, u32[]{:S(2)}, u32[]{:S(2)}) collective-permute-start(f32[16,512]{1,0:T(8,128)S(1)} %get-tuple-element.52), channel_id=1, source_target_pairs={{0,2},{2,4},{4,6},{6,8},{8,10},{10,12},{12,14},{14,16},{16,18},{18... | collective-permute-start | bytes 98312 | tf_op jit(solution)/shard_map/ppermute | solution.py:49
  10.2 2.9 %image.1 = (f32[40,128]{1,0:T(8,128)}, f32[16,1024]{1,0:T(8,128)}, f32[16,1024]{1,0:T(8,128)}, f32[16,1024]{1,0:T(8,128)}, f32[16,512]{1,0:T(8,128)}, /*index=5*/f32[16,512]{1,0:T(8,128)}, f32[1,1024]{1,0:T(1,128)}) custom-call(s32[8,3]{1,0:T(8,128)} %copy.9.index, bf16[8,3,128,128]{3,2,1,0:T(8,128)(2,1)} %weight.7, f32[16,512]{1,0:T(8,128)} %copy-done.6, ...), custom_call_target="tpu_custom_call" | custom-call | flops 2000000 | bytes 2000000 | tf_op jit(solution)/shard_map/image/pallas_call | solution.py:19
  13.1 3.0 %collective-permute-start.5 = (f32[40,128]{1,0:T(8,128)}, f32[40,128]{1,0:T(8,128)S(1)}, u32[]{:S(2)}, u32[]{:S(2)}) collective-permute-start(f32[40,128]{1,0:T(8,128)} %get-tuple-element.28), channel_id=1, source_target_pairs={{0,6},{2,4},{4,2},{6,0},{8,14},{10,12},{12,10},{14,8},{16,22},{18,... | collective-permute-start | bytes 61448 | tf_op jit(solution)/shard_map/ppermute | solution.py:41
  16.7 2.4 %collective-permute-start.10 = (f32[16,512]{1,0:T(8,128)}, f32[16,512]{1,0:T(8,128)S(1)}, u32[]{:S(2)}, u32[]{:S(2)}) collective-permute-start(f32[16,512]{1,0:T(8,128)} %get-tuple-element.32), channel_id=1, source_target_pairs={{0,2},{2,4},{4,6},{6,8},{8,10},{10,12},{12,14},{14,16},{16,18},{18... | collective-permute-start | bytes 98312 | tf_op jit(solution)/shard_map/ppermute | solution.py:49
  19.1 1.3 %collective-permute-start.11 = (f32[16,512]{1,0:T(8,128)}, f32[16,512]{1,0:T(8,128)S(1)}, u32[]{:S(2)}, u32[]{:S(2)}) collective-permute-start(f32[16,512]{1,0:T(8,128)} %get-tuple-element.33), channel_id=1, source_target_pairs={{2,0},{4,2},{6,4},{8,6},{10,8},{12,10},{14,12},{16,14},{18,16},{20... | collective-permute-start | bytes 98312 | tf_op jit(solution)/shard_map/ppermute | solution.py:49
  22.4 8.1 %collective-permute-start.8 = (f32[64,128]{1,0:T(8,128)S(1)}, f32[64,128]{1,0:T(8,128)S(1)}, u32[]{:S(2)}, u32[]{:S(2)}) collective-permute-start(f32[64,128]{1,0:T(8,128)S(1)} %constant_dynamic-update-slice_fusion.refs_0_), channel_id=1, source_target_pairs={{0,24},{2,26},{4,28},{6,30},{8,16},{10,18},{12,20},{14,22},{16,8},... | collective-permute-start | bytes 98312 | tf_op jit(solution)/shard_map/ppermute | solution.py:41
  31.8 2.4 %offset.1.refs_10_ = f32[16,1024]{1,0:T(8,128)} custom-call(s32[8,3]{1,0:T(8,128)} %copy.9.index, bf16[8,3,128,128]{3,2,1,0:T(8,128)(2,1)} %weight.7, f32[16,512]{1,0:T(8,128)} %copy-done.3, f32[16,512]{1,0:T(8,128)} %copy-done.4, f32[16,1024]{1,0:T(8,128)} %get-tuple-element.31.scaled.refs_9_, f32[16,1024]{1,0:T(8,128)} %get-tuple-element.30.image.refs_8_), custom_call_target="tpu_custom_call" | custom-call | flops 2000000 | bytes 2000000 | tf_op jit(solution)/shard_map/offset/pallas_call | solution.py:19
  34.2 1.1 %collective-permute-done.7.refs_2_ = f32[64,128]{1,0:T(8,128)S(1)} collective-permute-done((f32[64,128]{1,0:T(8,128)S(1)}, f32[64,128]{1,0:T(8,128)S(1)}, u32[]{:S(2)}, u32[]{:S(2)}) %collective-permute-start.7) | collective-permute-done | bytes 32800 | tf_op jit(solution)/shard_map/ppermute | solution.py:41
  36.0 3.9 %ritz.1 = (f32[16,16,128]{2,1,0:T(8,128)}, f32[16,1024]{1,0:T(8,128)}, f32[16,1024]{1,0:T(8,128)}, f32[16,1024]{1,0:T(8,128)}, f32[1,1024]{1,0:T(1,128)}) custom-call(s32[8,3]{1,0:T(8,128)} %copy.9.index, s32[8]{0:T(128)} %mates.7, f32[64,128]{1,0:T(8,128)} %copy-done.1, f32[64,128]{1,0:T(8,128)} %copy-done.14, f32[64,128]{1,0:T(8,128)} %copy-done.13, ...), custom_call_target="tpu_custom_call" | custom-call | flops 2000000 | bytes 2000000 | tf_op jit(solution)/shard_map/ritz/pallas_call | solution.py:19
  39.9 12.1 %all_to_all.10.arrived = f32[16,16,128]{2,1,0:T(8,128)} all-to-all(f32[16,16,128]{2,1,0:T(8,128)} %get-tuple-element.35), channel_id=1, replica_groups=mesh['rows'=16,'cols'=2] {'rows'}, dimensions={0} | all-to-all | bytes 262144 | tf_op jit(solution)/shard_map/all_to_all | solution.py:302
  52.0 1.6 %coarse.1 = (f32[16,1024]{1,0:T(8,128)}, f32[16,1024]{1,0:T(8,128)}, f32[16,512]{1,0:T(8,128)}, f32[16,512]{1,0:T(8,128)}) custom-call(s32[8]{0:T(128)} %mates.7, f32[16,16,128]{2,1,0:T(8,128)} %all_to_all.10.arrived, f32[16,1024]{1,0:T(8,128)} %get-tuple-element.36.remain, f32[1,1024]{1,0:T(1,128)} %get-tuple-element.37.pair_degree), custom_call_target="tpu_custom_call" | custom-call | flops 2000000 | bytes 2000000 | tf_op jit(solution)/shard_map/coarse/pallas_call | solution.py:19
  53.6 1.3 %collective-permute-start.12 = (f32[16,512]{1,0:T(8,128)}, f32[16,512]{1,0:T(8,128)S(1)}, u32[]{:S(2)}, u32[]{:S(2)}) collective-permute-start(f32[16,512]{1,0:T(8,128)} %get-tuple-element.38), channel_id=1, source_target_pairs={{0,2},{2,4},{4,6},{6,8},{8,10},{10,12},{12,14},{14,16},{16,18},{18... | collective-permute-start | bytes 98312 | tf_op jit(solution)/shard_map/ppermute | solution.py:49
  54.9 1.3 %collective-permute-start.13 = (f32[16,512]{1,0:T(8,128)}, f32[16,512]{1,0:T(8,128)S(1)}, u32[]{:S(2)}, u32[]{:S(2)}) collective-permute-start(f32[16,512]{1,0:T(8,128)} %get-tuple-element.39), channel_id=1, source_target_pairs={{2,0},{4,2},{6,4},{8,6},{10,8},{12,10},{14,12},{16,14},{18,16},{20... | collective-permute-start | bytes 98312 | tf_op jit(solution)/shard_map/ppermute | solution.py:49
  56.2 2.0 %collective-permute-done.13.after = f32[16,512]{1,0:T(8,128)S(1)} collective-permute-done((f32[16,512]{1,0:T(8,128)}, f32[16,512]{1,0:T(8,128)S(1)}, u32[]{:S(2)}, u32[]{:S(2)}) %collective-permute-start.13) | collective-permute-done | bytes 32800 | tf_op jit(solution)/shard_map/ppermute | solution.py:49
  58.8 2.5 %product.1 = (f32[16,16,128]{2,1,0:T(8,128)}, f32[16,1024]{1,0:T(8,128)}) custom-call(s32[8,3]{1,0:T(8,128)} %copy.9.index, s32[8]{0:T(128)} %mates.7, bf16[8,3,128,128]{3,2,1,0:T(8,128)(2,1)} %weight.7, f32[16,512]{1,0:T(8,128)} %copy-done.9, f32[16,512]{1,0:T(8,128)} %copy-done.10, f32[16,1024]{1,0:T(8,128)} %get-tuple-element.40.fix, ...), custom_call_target="tpu_custom_call" | custom-call | flops 2000000 | bytes 2000000 | tf_op jit(solution)/shard_map/product/pallas_call | solution.py:19
  61.3 14.8 %all_to_all.11.arrived = f32[16,16,128]{2,1,0:T(8,128)} all-to-all(f32[16,16,128]{2,1,0:T(8,128)} %get-tuple-element.41), channel_id=1, replica_groups=mesh['rows'=16,'cols'=2] {'rows'}, dimensions={0} | all-to-all | bytes 262144 | tf_op jit(solution)/shard_map/all_to_all | solution.py:315
  76.1 1.7 %fix.1 = (f32[16,1024]{1,0:T(8,128)}, f32[16,512]{1,0:T(8,128)}, f32[16,512]{1,0:T(8,128)}) custom-call(s32[8]{0:T(128)} %mates.7, f32[16,16,128]{2,1,0:T(8,128)} %all_to_all.11.arrived, f32[16,1024]{1,0:T(8,128)} %get-tuple-element.42.product, f32[16,1024]{1,0:T(8,128)} %get-tuple-element.43.coarse, f32[16,1024]{1,0:T(8,128)} %get-tuple-element.40.fix, ...), custom_call_target="tpu_custom_call" | custom-call | flops 2000000 | bytes 2000000 | tf_op jit(solution)/shard_map/fix/pallas_call | solution.py:19
  77.8 1.3 %collective-permute-start.14 = (f32[16,512]{1,0:T(8,128)}, f32[16,512]{1,0:T(8,128)S(1)}, u32[]{:S(2)}, u32[]{:S(2)}) collective-permute-start(f32[16,512]{1,0:T(8,128)} %get-tuple-element.45), channel_id=1, source_target_pairs={{0,2},{2,4},{4,6},{6,8},{8,10},{10,12},{12,14},{14,16},{16,18},{18... | collective-permute-start | bytes 98312 | tf_op jit(solution)/shard_map/ppermute | solution.py:49
  79.1 1.3 %collective-permute-start.15 = (f32[16,512]{1,0:T(8,128)}, f32[16,512]{1,0:T(8,128)S(1)}, u32[]{:S(2)}, u32[]{:S(2)}) collective-permute-start(f32[16,512]{1,0:T(8,128)} %get-tuple-element.46), channel_id=1, source_target_pairs={{2,0},{4,2},{6,4},{8,6},{10,8},{12,10},{14,12},{16,14},{18,16},{20... | collective-permute-start | bytes 98312 | tf_op jit(solution)/shard_map/ppermute | solution.py:49
  80.4 2.0 %collective-permute-done.15.after = f32[16,512]{1,0:T(8,128)S(1)} collective-permute-done((f32[16,512]{1,0:T(8,128)}, f32[16,512]{1,0:T(8,128)S(1)}, u32[]{:S(2)}, u32[]{:S(2)}) %collective-permute-start.15) | collective-permute-done | bytes 32800 | tf_op jit(solution)/shard_map/ppermute | solution.py:49
  83.0 2.5 %smooth.1 = (f32[16,1024]{1,0:T(8,128)}, f32[16,128]{1,0:T(8,128)}) custom-call(s32[8,3]{1,0:T(8,128)} %copy.9.index, bf16[8,3,128,128]{3,2,1,0:T(8,128)(2,1)} %weight.7, f32[16,512]{1,0:T(8,128)} %copy-done.7, f32[16,512]{1,0:T(8,128)} %copy-done.8, f32[16,1024]{1,0:T(8,128)} %get-tuple-element.47.second, f32[16,1024]{1,0:T(8,128)} %get-tuple-element.48.residual, ...), custom_call_target="tpu_custom_call" | custom-call | flops 2000000 | bytes 2000000 | tf_op jit(solution)/shard_map/smooth/pallas_call | solution.py:19
  85.5 4.2 %collective-permute-start.18 = (f32[16,128]{1,0:T(8,128)}, f32[16,128]{1,0:T(8,128)S(1)}, u32[]{:S(2)}, u32[]{:S(2)}) collective-permute-start(f32[16,128]{1,0:T(8,128)} %get-tuple-element.49), channel_id=1, source_target_pairs={{0,6},{2,4},{4,2},{6,0},{8,14},{10,12},{12,10},{14,8},{16,22},{18,... | collective-permute-start | bytes 24584 | tf_op jit(solution)/shard_map/ppermute | solution.py:41
  89.8 1.5 %collective-permute-done.18 = f32[16,128]{1,0:T(8,128)S(1)} collective-permute-done((f32[16,128]{1,0:T(8,128)}, f32[16,128]{1,0:T(8,128)S(1)}, u32[]{:S(2)}, u32[]{:S(2)}) %collective-permute-start.18) | collective-permute-done | bytes 8224 | tf_op jit(solution)/shard_map/ppermute | solution.py:41
  91.3 2.3 %collective-permute-done.17 = f32[16,128]{1,0:T(8,128)S(1)} collective-permute-done((f32[16,128]{1,0:T(8,128)}, f32[16,128]{1,0:T(8,128)S(1)}, u32[]{:S(2)}, u32[]{:S(2)}) %collective-permute-start.17) | collective-permute-done | bytes 8224 | tf_op jit(solution)/shard_map/ppermute | solution.py:41
  94.5 2.8 %collective-permute-start.20 = (f32[16,128]{1,0:T(8,128)S(1)}, f32[16,128]{1,0:T(8,128)S(1)}, u32[]{:S(2)}, u32[]{:S(2)}) collective-permute-start(f32[16,128]{1,0:T(8,128)S(1)} %add_add_fusion.refs_0_), channel_id=1, source_target_pairs={{0,16},{2,18},{4,20},{6,22},{8,24},{10,26},{12,28},{14,30},{16,0},... | collective-permute-start | bytes 24584 | tf_op jit(solution)/shard_map/ppermute | solution.py:41
  97.4 1.3 %collective-permute-start.19 = (f32[16,128]{1,0:T(8,128)S(1)}, f32[16,128]{1,0:T(8,128)S(1)}, u32[]{:S(2)}, u32[]{:S(2)}) collective-permute-start(f32[16,128]{1,0:T(8,128)S(1)} %add_add_fusion.refs_0_), channel_id=1, source_target_pairs={{0,8},{2,10},{4,12},{6,14},{8,0},{10,2},{12,4},{14,6},{16,24},{18,... | collective-permute-start | bytes 24584 | tf_op jit(solution)/shard_map/ppermute | solution.py:41
  98.7 1.1 %collective-permute-done.21.refs_3_ = f32[16,128]{1,0:T(8,128)S(1)} collective-permute-done((f32[16,128]{1,0:T(8,128)S(1)}, f32[16,128]{1,0:T(8,128)S(1)}, u32[]{:S(2)}, u32[]{:S(2)}) %collective-permute-start.21) | collective-permute-done | bytes 8224 | tf_op jit(solution)/shard_map/ppermute | solution.py:41
  99.7 1.3 %collective-permute-done.19.refs_1_ = f32[16,128]{1,0:T(8,128)S(1)} collective-permute-done((f32[16,128]{1,0:T(8,128)S(1)}, f32[16,128]{1,0:T(8,128)S(1)}, u32[]{:S(2)}, u32[]{:S(2)}) %collective-permute-start.19) | collective-permute-done | bytes 8224 | tf_op jit(solution)/shard_map/ppermute | solution.py:41
  101.6 1.6 %scale.1 = f32[16,1024]{1,0:T(8,128)} custom-call(f32[16,128]{1,0:T(8,128)} %copy-done.11, f32[16,128]{1,0:T(8,128)} %copy-done.17, f32[16,128]{1,0:T(8,128)} %copy-done.16, f32[16,128]{1,0:T(8,128)} %copy-done.15, f32[16,1024]{1,0:T(8,128)} %get-tuple-element.50.refs_4_), custom_call_target="tpu_custom_call" | custom-call | flops 2000000 | bytes 2000000 | tf_op jit(solution)/shard_map/scale/pallas_call | solution.py:19
  (68 shorter events, 9.4 us)
Async XLA Ops:
  0.0 9.0 %collective-permute-start.2 = (f32[16,1024]{1,0:T(8,128)}, f32[16,1024]{1,0:T(8,128)S(1)}, u32[]{:S(2)}, u32[]{:S(2)}) collective-permute-start(f32[16,1024]{1,0:T(8,128)} %refs_4_.1), channel_id=1, source_target_pairs={{0,1},{1,0},{2,3},{3,2},{4,5},{5,4},{6,7},{7,6},{8,9},{9,8},{10,11... | collective-permute-start | bytes 196616 | tf_op jit(solution)/shard_map/ppermute | solution.py:41
  3.8 4.3 %copy-start.18 = (s32[8,3]{0,1:T(4,128)S(1)}, s32[8,3]{0,1:T(4,128)}, u32[]{:S(2)}) copy-start(s32[8,3]{0,1:T(4,128)} %param.6) | copy-start | bytes 292
  3.8 5.0 %collective-permute-start.1 = (f32[16,512]{1,0:T(8,128)S(1)}, f32[16,512]{1,0:T(8,128)S(1)}, u32[]{:S(2)}, u32[]{:S(2)}) collective-permute-start(f32[16,512]{1,0:T(8,128)S(1)} %get-tuple-element.51), channel_id=1, source_target_pairs={{2,0},{4,2},{6,4},{8,6},{10,8},{12,10},{14,12},{16,14},{18,16},{20... | collective-permute-start | bytes 98312 | tf_op jit(solution)/shard_map/ppermute | solution.py:49
  5.1 3.9 %collective-permute-start = (f32[16,512]{1,0:T(8,128)S(1)}, f32[16,512]{1,0:T(8,128)S(1)}, u32[]{:S(2)}, u32[]{:S(2)}) collective-permute-start(f32[16,512]{1,0:T(8,128)S(1)} %get-tuple-element.52), channel_id=1, source_target_pairs={{0,2},{2,4},{4,6},{6,8},{8,10},{10,12},{12,14},{14,16},{16,18},{18... | collective-permute-start | bytes 98312 | tf_op jit(solution)/shard_map/ppermute | solution.py:49
  13.1 7.3 %collective-permute-start.5 = (f32[40,128]{1,0:T(8,128)}, f32[40,128]{1,0:T(8,128)S(1)}, u32[]{:S(2)}, u32[]{:S(2)}) collective-permute-start(f32[40,128]{1,0:T(8,128)} %get-tuple-element.28), channel_id=1, source_target_pairs={{0,6},{2,4},{4,2},{6,0},{8,14},{10,12},{12,10},{14,8},{16,22},{18,... | collective-permute-start | bytes 61448 | tf_op jit(solution)/shard_map/ppermute | solution.py:41
  16.1 4.9 %collective-permute-start.4 = (f32[40,128]{1,0:T(8,128)}, f32[40,128]{1,0:T(8,128)S(1)}, u32[]{:S(2)}, u32[]{:S(2)}) collective-permute-start(f32[40,128]{1,0:T(8,128)} %get-tuple-element.28), channel_id=1, source_target_pairs={{0,4},{2,6},{4,0},{6,2},{8,12},{10,14},{12,8},{14,10},{16,20},{18,... | collective-permute-start | bytes 61448 | tf_op jit(solution)/shard_map/ppermute | solution.py:41
  16.7 4.3 %collective-permute-start.3 = (f32[40,128]{1,0:T(8,128)}, f32[40,128]{1,0:T(8,128)S(1)}, u32[]{:S(2)}, u32[]{:S(2)}) collective-permute-start(f32[40,128]{1,0:T(8,128)} %get-tuple-element.28), channel_id=1, source_target_pairs={{0,2},{2,0},{4,6},{6,4},{8,10},{10,8},{12,14},{14,12},{16,18},{18,... | collective-permute-start | bytes 61448 | tf_op jit(solution)/shard_map/ppermute | solution.py:41
  16.7 13.8 %collective-permute-start.10 = (f32[16,512]{1,0:T(8,128)}, f32[16,512]{1,0:T(8,128)S(1)}, u32[]{:S(2)}, u32[]{:S(2)}) collective-permute-start(f32[16,512]{1,0:T(8,128)} %get-tuple-element.32), channel_id=1, source_target_pairs={{0,2},{2,4},{4,6},{6,8},{8,10},{10,12},{12,14},{14,16},{16,18},{18... | collective-permute-start | bytes 98312 | tf_op jit(solution)/shard_map/ppermute | solution.py:49
  19.1 12.1 %collective-permute-start.11 = (f32[16,512]{1,0:T(8,128)}, f32[16,512]{1,0:T(8,128)S(1)}, u32[]{:S(2)}, u32[]{:S(2)}) collective-permute-start(f32[16,512]{1,0:T(8,128)} %get-tuple-element.33), channel_id=1, source_target_pairs={{2,0},{4,2},{6,4},{8,6},{10,8},{12,10},{14,12},{16,14},{18,16},{20... | collective-permute-start | bytes 98312 | tf_op jit(solution)/shard_map/ppermute | solution.py:49
  20.4 15.0 %collective-permute-start.9 = (f32[16,1024]{1,0:T(8,128)}, f32[16,1024]{1,0:T(8,128)S(1)}, u32[]{:S(2)}, u32[]{:S(2)}) collective-permute-start(f32[16,1024]{1,0:T(8,128)} %get-tuple-element.29.refs_6_), channel_id=1, source_target_pairs={{0,1},{1,0},{2,3},{3,2},{4,5},{5,4},{6,7},{7,6},{8,9},{9,8},{10,11... | collective-permute-start | bytes 196616 | tf_op jit(solution)/shard_map/ppermute | solution.py:41
  22.4 11.8 %copy-start.1 = (f32[64,128]{1,0:T(8,128)}, f32[64,128]{1,0:T(8,128)S(1)}, u32[]{:S(2)}) copy-start(f32[64,128]{1,0:T(8,128)S(1)} %constant_dynamic-update-slice_fusion.refs_0_) | copy-start | bytes 98308
  22.4 11.8 %collective-permute-start.8 = (f32[64,128]{1,0:T(8,128)S(1)}, f32[64,128]{1,0:T(8,128)S(1)}, u32[]{:S(2)}, u32[]{:S(2)}) collective-permute-start(f32[64,128]{1,0:T(8,128)S(1)} %constant_dynamic-update-slice_fusion.refs_0_), channel_id=1, source_target_pairs={{0,24},{2,26},{4,28},{6,30},{8,16},{10,18},{12,20},{14,22},{16,8},... | collective-permute-start | bytes 98312 | tf_op jit(solution)/shard_map/ppermute | solution.py:41
  30.5 4.8 %collective-permute-start.7 = (f32[64,128]{1,0:T(8,128)S(1)}, f32[64,128]{1,0:T(8,128)S(1)}, u32[]{:S(2)}, u32[]{:S(2)}) collective-permute-start(f32[64,128]{1,0:T(8,128)S(1)} %constant_dynamic-update-slice_fusion.refs_0_), channel_id=1, source_target_pairs={{0,16},{2,18},{4,20},{6,22},{8,24},{10,26},{12,28},{14,30},{16,0},... | collective-permute-start | bytes 98312 | tf_op jit(solution)/shard_map/ppermute | solution.py:41
  30.5 0.7 copy-start.3
  30.5 4.8 %collective-permute-start.6 = (f32[64,128]{1,0:T(8,128)S(1)}, f32[64,128]{1,0:T(8,128)S(1)}, u32[]{:S(2)}, u32[]{:S(2)}) collective-permute-start(f32[64,128]{1,0:T(8,128)S(1)} %constant_dynamic-update-slice_fusion.refs_0_), channel_id=1, source_target_pairs={{0,8},{2,10},{4,12},{6,14},{8,0},{10,2},{12,4},{14,6},{16,24},{18,... | collective-permute-start | bytes 98312 | tf_op jit(solution)/shard_map/ppermute | solution.py:41
  34.2 1.2 %copy-start.12 = (f32[64,128]{1,0:T(8,128)}, f32[64,128]{1,0:T(8,128)S(1)}, u32[]{:S(2)}) copy-start(f32[64,128]{1,0:T(8,128)S(1)} %collective-permute-done.8.refs_3_) | copy-start | bytes 98308
  35.4 0.6 copy-start.2
  53.6 2.6 %collective-permute-start.12 = (f32[16,512]{1,0:T(8,128)}, f32[16,512]{1,0:T(8,128)S(1)}, u32[]{:S(2)}, u32[]{:S(2)}) collective-permute-start(f32[16,512]{1,0:T(8,128)} %get-tuple-element.38), channel_id=1, source_target_pairs={{0,2},{2,4},{4,6},{6,8},{8,10},{10,12},{12,14},{14,16},{16,18},{18... | collective-permute-start | bytes 98312 | tf_op jit(solution)/shard_map/ppermute | solution.py:49
  54.9 3.3 %collective-permute-start.13 = (f32[16,512]{1,0:T(8,128)}, f32[16,512]{1,0:T(8,128)S(1)}, u32[]{:S(2)}, u32[]{:S(2)}) collective-permute-start(f32[16,512]{1,0:T(8,128)} %get-tuple-element.39), channel_id=1, source_target_pairs={{2,0},{4,2},{6,4},{8,6},{10,8},{12,10},{14,12},{16,14},{18,16},{20... | collective-permute-start | bytes 98312 | tf_op jit(solution)/shard_map/ppermute | solution.py:49
  56.2 2.0 %copy-start.9 = (f32[16,512]{1,0:T(8,128)}, f32[16,512]{1,0:T(8,128)S(1)}, u32[]{:S(2)}) copy-start(f32[16,512]{1,0:T(8,128)S(1)} %collective-permute-done.12.before) | copy-start | bytes 98308
  77.8 2.6 %collective-permute-start.14 = (f32[16,512]{1,0:T(8,128)}, f32[16,512]{1,0:T(8,128)S(1)}, u32[]{:S(2)}, u32[]{:S(2)}) collective-permute-start(f32[16,512]{1,0:T(8,128)} %get-tuple-element.45), channel_id=1, source_target_pairs={{0,2},{2,4},{4,6},{6,8},{8,10},{10,12},{12,14},{14,16},{16,18},{18... | collective-permute-start | bytes 98312 | tf_op jit(solution)/shard_map/ppermute | solution.py:49
  79.1 3.3 %collective-permute-start.15 = (f32[16,512]{1,0:T(8,128)}, f32[16,512]{1,0:T(8,128)S(1)}, u32[]{:S(2)}, u32[]{:S(2)}) collective-permute-start(f32[16,512]{1,0:T(8,128)} %get-tuple-element.46), channel_id=1, source_target_pairs={{2,0},{4,2},{6,4},{8,6},{10,8},{12,10},{14,12},{16,14},{18,16},{20... | collective-permute-start | bytes 98312 | tf_op jit(solution)/shard_map/ppermute | solution.py:49
  80.4 2.0 %copy-start.7 = (f32[16,512]{1,0:T(8,128)}, f32[16,512]{1,0:T(8,128)S(1)}, u32[]{:S(2)}) copy-start(f32[16,512]{1,0:T(8,128)S(1)} %collective-permute-done.14.before) | copy-start | bytes 98308
  85.5 5.8 %collective-permute-start.18 = (f32[16,128]{1,0:T(8,128)}, f32[16,128]{1,0:T(8,128)S(1)}, u32[]{:S(2)}, u32[]{:S(2)}) collective-permute-start(f32[16,128]{1,0:T(8,128)} %get-tuple-element.49), channel_id=1, source_target_pairs={{0,6},{2,4},{4,2},{6,0},{8,14},{10,12},{12,10},{14,8},{16,22},{18,... | collective-permute-start | bytes 24584 | tf_op jit(solution)/shard_map/ppermute | solution.py:41
  89.7 3.9 %collective-permute-start.17 = (f32[16,128]{1,0:T(8,128)}, f32[16,128]{1,0:T(8,128)S(1)}, u32[]{:S(2)}, u32[]{:S(2)}) collective-permute-start(f32[16,128]{1,0:T(8,128)} %get-tuple-element.49), channel_id=1, source_target_pairs={{0,4},{2,6},{4,0},{6,2},{8,12},{10,14},{12,8},{14,10},{16,20},{18,... | collective-permute-start | bytes 24584 | tf_op jit(solution)/shard_map/ppermute | solution.py:41
  89.7 3.9 %collective-permute-start.16 = (f32[16,128]{1,0:T(8,128)}, f32[16,128]{1,0:T(8,128)S(1)}, u32[]{:S(2)}, u32[]{:S(2)}) collective-permute-start(f32[16,128]{1,0:T(8,128)} %get-tuple-element.49), channel_id=1, source_target_pairs={{0,2},{2,0},{4,6},{6,4},{8,10},{10,8},{12,14},{14,12},{16,18},{18,... | collective-permute-start | bytes 24584 | tf_op jit(solution)/shard_map/ppermute | solution.py:41
  94.3 6.7 %copy-start.11 = (f32[16,128]{1,0:T(8,128)}, f32[16,128]{1,0:T(8,128)S(1)}, u32[]{:S(2)}) copy-start(f32[16,128]{1,0:T(8,128)S(1)} %add_add_fusion.refs_0_) | copy-start | bytes 24580
  94.3 5.4 %collective-permute-start.21 = (f32[16,128]{1,0:T(8,128)S(1)}, f32[16,128]{1,0:T(8,128)S(1)}, u32[]{:S(2)}, u32[]{:S(2)}) collective-permute-start(f32[16,128]{1,0:T(8,128)S(1)} %add_add_fusion.refs_0_), channel_id=1, source_target_pairs={{0,24},{2,26},{4,28},{6,30},{8,16},{10,18},{12,20},{14,22},{16,8},... | collective-permute-start | bytes 24584 | tf_op jit(solution)/shard_map/ppermute | solution.py:41
  94.5 5.2 %collective-permute-start.20 = (f32[16,128]{1,0:T(8,128)S(1)}, f32[16,128]{1,0:T(8,128)S(1)}, u32[]{:S(2)}, u32[]{:S(2)}) collective-permute-start(f32[16,128]{1,0:T(8,128)S(1)} %add_add_fusion.refs_0_), channel_id=1, source_target_pairs={{0,16},{2,18},{4,20},{6,22},{8,24},{10,26},{12,28},{14,30},{16,0},... | collective-permute-start | bytes 24584 | tf_op jit(solution)/shard_map/ppermute | solution.py:41
  97.4 3.7 %collective-permute-start.19 = (f32[16,128]{1,0:T(8,128)S(1)}, f32[16,128]{1,0:T(8,128)S(1)}, u32[]{:S(2)}, u32[]{:S(2)}) collective-permute-start(f32[16,128]{1,0:T(8,128)S(1)} %add_add_fusion.refs_0_), channel_id=1, source_target_pairs={{0,8},{2,10},{4,12},{6,14},{8,0},{10,2},{12,4},{14,6},{16,24},{18,... | collective-permute-start | bytes 24584 | tf_op jit(solution)/shard_map/ppermute | solution.py:41
  99.7 1.3 %copy-start.15 = (f32[16,128]{1,0:T(8,128)}, f32[16,128]{1,0:T(8,128)S(1)}, u32[]{:S(2)}) copy-start(f32[16,128]{1,0:T(8,128)S(1)} %collective-permute-done.21.refs_3_) | copy-start | bytes 24580
  99.7 1.3 %copy-start.16 = (f32[16,128]{1,0:T(8,128)}, f32[16,128]{1,0:T(8,128)S(1)}, u32[]{:S(2)}) copy-start(f32[16,128]{1,0:T(8,128)S(1)} %collective-permute-done.20.refs_2_) | copy-start | bytes 24580
  (9 other events, 5.4 us)

commit v3 on v2

--- a/solution.py
+++ b/solution.py
@@ -10,6 +10,7 @@
 EPSILON = 1e-06
 EXACT = lax.Precision.HIGHEST
 PARTS = 3
+VMEM_GRANT = 16 * 1024 * 1024
 F32 = jnp.float32
 IN_VMEM = pl.BlockSpec(memory_space=pltpu.VMEM)
 IN_SMEM = pl.BlockSpec(memory_space=pltpu.SMEM)
@@ -23,6 +24,7 @@
         in_specs=[IN_SMEM] * len(scalars) + [IN_VMEM] * len(arrays),
         out_specs=[IN_VMEM] * len(outs),
         scratch_shapes=list(scratch),
+        compiler_params=pltpu.CompilerParams(vmem_limit_bytes=VMEM_GRANT),
         cost_estimate=pl.CostEstimate(flops=cost, bytes_accessed=cost, transcendentals=0),
     )(*scalars, *arrays)
 

time: 104 us -> 89.4 us (0.86)
  Pallas kernels: 19.1 us -> 9.82 us
  local copies, waits for them, and re-layouts: 6.42 us -> 2.04 us
  waiting for transfers between devices: 11.4 us -> 13.1 us
  other arithmetic: 1.43 us -> 0.01 us
  blocking collectives: 26.9 us -> 25.7 us
    pallas_call x8, Pallas kernels: 19.1 us -> 9.82 us  [kernel_call(): pl.pallas_call(body, name=name, out_shape=[jax.ShapeDtypeStruct(shape, F3...]
    unnamed x42 -> x14, local copies, waits for them, and re-layouts: 5.62 us -> 1.24 us
    ppermute x14, waiting for transfers between devices: 7.22 us -> 8.79 us  [exchanged(): lax.ppermute(value, axis, [(i, i ^ mask * stride) for i in range(peers)])]
    all_to_all x2, blocking collectives: 26.9 us -> 25.7 us  [local(): lax.all_to_all(out, 'rows', split_axis=0, concat_axis=0, tiled=True)]
  transfers between devices with their start and end apart: 22 -> 22, of which waited for: 8 -> 9; matrix products, arithmetic and copies ran while one was open for 3% -> 1% of each run, Pallas kernels for 2% -> 1%
where the time goes in v3:
time: 89.4 us; the launch traced here: 88.9 us
  starting transfers between devices  38 us (43%)
  blocking collectives  25.7 us (29%)
  waiting for transfers between devices  13.1 us (15%)
  Pallas kernels  9.82 us (11%)
  local copies, waits for them, and re-layouts  2.04 us (2%)
    all_to_all x2, blocking collectives, local(): lax.all_to_all(out, 'rows', split_axis=0, concat_axis=0, tiled=True)  25.7 us
    ppermute x14, starting transfers between devices, exchanged(): lax.ppermute(value, axis, [(i, i ^ mask * stride) for i in range(peers)])  24.9 us
    pallas_call x8, Pallas kernels, kernel_call(): pl.pallas_call(body, name=name, out_shape=[jax.ShapeDtypeStruct(shape, F3...  9.82 us
    ppermute x14, waiting for transfers between devices, exchanged(): lax.ppermute(value, axis, [(i, i ^ mask * stride) for i in range(peers)])  8.79 us
    ppermute x4, starting transfers between devices, from_sides(): lax.ppermute(last, axis, up)  7.97 us
    ppermute x4, starting transfers between devices, from_sides(): lax.ppermute(first, axis, [(j, i) for i, j in up])  5.17 us
    ppermute x4, waiting for transfers between devices, from_sides(): lax.ppermute(first, axis, [(j, i) for i, j in up])  3.59 us
  transfers between devices with their start and end apart: 22, of which 9 were waited for; matrix products, arithmetic and copies ran while one was open for 1% of the time, Pallas kernels for 1%

profile of v3, /device:TPU:0, one launch (start us, length us, event | category | flops | bytes accessed | tf_op | source)
XLA Modules:
  0.0 88.9 jit_solution(11831949387822651339)
XLA Ops:
  0.0 3.0 %collective-permute-start.2 = (f32[16,1024]{1,0:T(8,128)}, f32[16,1024]{1,0:T(8,128)S(1)}, u32[]{:S(2)}, u32[]{:S(2)}) collective-permute-start(f32[16,1024]{1,0:T(8,128)} %refs_4_.1), channel_id=1, source_target_pairs={{0,1},{1,0},{2,3},{3,2},{4,5},{5,4},{6,7},{7,6},{8,9},{9,8},{10,11... | collective-permute-start | bytes 196616 | tf_op jit(solution)/shard_map/ppermute | solution.py:43
  3.0 0.8 fusion.1
  3.8 1.3 %collective-permute-start.1 = (f32[16,512]{1,0:T(8,128)S(1)}, f32[16,512]{1,0:T(8,128)S(1)}, u32[]{:S(2)}, u32[]{:S(2)}) collective-permute-start(f32[16,512]{1,0:T(8,128)S(1)} %get-tuple-element.51), channel_id=1, source_target_pairs={{2,0},{4,2},{6,4},{8,6},{10,8},{12,10},{14,12},{16,14},{18,16},{20... | collective-permute-start | bytes 98312 | tf_op jit(solution)/shard_map/ppermute | solution.py:51
  5.1 3.0 %collective-permute-start = (f32[16,512]{1,0:T(8,128)S(1)}, f32[16,512]{1,0:T(8,128)S(1)}, u32[]{:S(2)}, u32[]{:S(2)}) collective-permute-start(f32[16,512]{1,0:T(8,128)S(1)} %get-tuple-element.52), channel_id=1, source_target_pairs={{0,2},{2,4},{4,6},{6,8},{8,10},{10,12},{12,14},{14,16},{16,18},{18... | collective-permute-start | bytes 98312 | tf_op jit(solution)/shard_map/ppermute | solution.py:51
  8.2 0.7 collective-permute-done.before
  9.0 1.1 %copy-done = bf16[8,3,128,128]{3,2,1,0:T(8,128)(2,1)S(1)} copy-done((bf16[8,3,128,128]{3,2,1,0:T(8,128)(2,1)S(1)}, bf16[8,3,128,128]{3,2,1,0:T(8,128)(2,1)}, u32[]{:S(2)}) %copy-start) | copy-done | bytes 786456
  10.1 1.7 %image.1 = (f32[40,128]{1,0:T(8,128)S(1)}, f32[16,1024]{1,0:T(8,128)S(1)}, f32[16,1024]{1,0:T(8,128)S(1)}, f32[16,1024]{1,0:T(8,128)S(1)}, f32[16,512]{1,0:T(8,1...) custom-call(s32[8,3]{1,0:T(8,128)S(1)} %copy.9.index, bf16[8,3,128,128]{3,2,1,0:T(8,128)(2,1)S(1)} %copy-done, ...), custom_call_target="tpu_custom_call" | custom-call | flops 2000000 | bytes 2000000 | tf_op jit(solution)/shard_map/image/pallas_call | solution.py:20
  11.8 3.0 %collective-permute-start.5 = (f32[40,128]{1,0:T(8,128)S(1)}, f32[40,128]{1,0:T(8,128)S(1)}, u32[]{:S(2)}, u32[]{:S(2)}) collective-permute-start(f32[40,128]{1,0:T(8,128)S(1)} %get-tuple-element.28), channel_id=1, source_target_pairs={{0,6},{2,4},{4,2},{6,0},{8,14},{10,12},{12,10},{14,8},{16,22},{18,... | collective-permute-start | bytes 61448 | tf_op jit(solution)/shard_map/ppermute | solution.py:43
  15.4 2.4 %collective-permute-start.10 = (f32[16,512]{1,0:T(8,128)S(1)}, f32[16,512]{1,0:T(8,128)S(1)}, u32[]{:S(2)}, u32[]{:S(2)}) collective-permute-start(f32[16,512]{1,0:T(8,128)S(1)} %get-tuple-element.32), channel_id=1, source_target_pairs={{0,2},{2,4},{4,6},{6,8},{8,10},{10,12},{12,14},{14,16},{16,18},{18... | collective-permute-start | bytes 98312 | tf_op jit(solution)/shard_map/ppermute | solution.py:51
  17.8 1.3 %collective-permute-start.11 = (f32[16,512]{1,0:T(8,128)S(1)}, f32[16,512]{1,0:T(8,128)S(1)}, u32[]{:S(2)}, u32[]{:S(2)}) collective-permute-start(f32[16,512]{1,0:T(8,128)S(1)} %get-tuple-element.33), channel_id=1, source_target_pairs={{2,0},{4,2},{6,4},{8,6},{10,8},{12,10},{14,12},{16,14},{18,16},{20... | collective-permute-start | bytes 98312 | tf_op jit(solution)/shard_map/ppermute | solution.py:51
  19.7 8.1 %collective-permute-start.8 = (f32[64,128]{1,0:T(8,128)S(1)}, f32[64,128]{1,0:T(8,128)S(1)}, u32[]{:S(2)}, u32[]{:S(2)}) collective-permute-start(f32[64,128]{1,0:T(8,128)S(1)} %constant_dynamic-update-slice_fusion.refs_0_), channel_id=1, source_target_pairs={{0,24},{2,26},{4,28},{6,30},{8,16},{10,18},{12,20},{14,22},{16,8},... | collective-permute-start | bytes 98312 | tf_op jit(solution)/shard_map/ppermute | solution.py:43
  28.5 1.2 %offset.1.refs_10_ = f32[16,1024]{1,0:T(8,128)S(1)} custom-call(s32[8,3]{1,0:T(8,128)S(1)} %copy.9.index, bf16[8,3,128,128]{3,2,1,0:T(8,128)(2,1)S(1)} %copy-done, f32[16,512]{1,0:T(8,128)S(1)} %collective-permute-done.10.before, f32[16,512]{1,0:T(8,128)S(1)} %collective-permute-done.11.after, f32[16,1024]{1,0:T(8,128)S(1)} %get-tuple-element.31.scaled.refs_9_, ...), custom_call_target="tpu_custom_call" | custom-call | flops 2000000 | bytes 2000000 | tf_op jit(solution)/shard_map/offset/pallas_call | solution.py:20
  29.8 2.9 %collective-permute-done.7.refs_2_ = f32[64,128]{1,0:T(8,128)S(1)} collective-permute-done((f32[64,128]{1,0:T(8,128)S(1)}, f32[64,128]{1,0:T(8,128)S(1)}, u32[]{:S(2)}, u32[]{:S(2)}) %collective-permute-start.7) | collective-permute-done | bytes 32800 | tf_op jit(solution)/shard_map/ppermute | solution.py:43
  32.7 2.7 %ritz.1 = (f32[16,16,128]{2,1,0:T(8,128)S(1)}, f32[16,1024]{1,0:T(8,128)S(1)}, f32[16,1024]{1,0:T(8,128)S(1)}, f32[16,1024]{1,0:T(8,128)S(1)}, f32[1,1024]{1,0:T(1,128)S(1)}) custom-call(s32[8,3]{1,0:T(8,128)S(1)} %copy.9.index, s32[8]{0:T(128)S(1)} %copy-done.3, f32[64,128]{1,0:T(8,128)S(1)} %constant_dynamic-update-slice_fusion.refs_0_, ...), custom_call_target="tpu_custom_call" | custom-call | flops 2000000 | bytes 2000000 | tf_op jit(solution)/shard_map/ritz/pallas_call | solution.py:20
  35.4 11.1 %all_to_all.10.arrived = f32[16,16,128]{2,1,0:T(8,128)S(1)} all-to-all(f32[16,16,128]{2,1,0:T(8,128)S(1)} %get-tuple-element.35), channel_id=1, replica_groups=mesh['rows'=16,'cols'=2] {'rows'}, dimensions={0} | all-to-all | bytes 262144 | tf_op jit(solution)/shard_map/all_to_all | solution.py:304
  47.1 1.3 %collective-permute-start.12 = (f32[16,512]{1,0:T(8,128)S(1)}, f32[16,512]{1,0:T(8,128)S(1)}, u32[]{:S(2)}, u32[]{:S(2)}) collective-permute-start(f32[16,512]{1,0:T(8,128)S(1)} %get-tuple-element.38), channel_id=1, source_target_pairs={{0,2},{2,4},{4,6},{6,8},{8,10},{10,12},{12,14},{14,16},{16,18},{18... | collective-permute-start | bytes 98312 | tf_op jit(solution)/shard_map/ppermute | solution.py:51
  48.4 1.3 %collective-permute-start.13 = (f32[16,512]{1,0:T(8,128)S(1)}, f32[16,512]{1,0:T(8,128)S(1)}, u32[]{:S(2)}, u32[]{:S(2)}) collective-permute-start(f32[16,512]{1,0:T(8,128)S(1)} %get-tuple-element.39), channel_id=1, source_target_pairs={{2,0},{4,2},{6,4},{8,6},{10,8},{12,10},{14,12},{16,14},{18,16},{20... | collective-permute-start | bytes 98312 | tf_op jit(solution)/shard_map/ppermute | solution.py:51
  49.7 1.8 %collective-permute-done.13.after = f32[16,512]{1,0:T(8,128)S(1)} collective-permute-done((f32[16,512]{1,0:T(8,128)S(1)}, f32[16,512]{1,0:T(8,128)S(1)}, u32[]{:S(2)}, u32[]{:S(2)}) %collective-permute-start.13) | collective-permute-done | bytes 32800 | tf_op jit(solution)/shard_map/ppermute | solution.py:51
  51.5 1.1 %product.1 = (f32[16,16,128]{2,1,0:T(8,128)S(1)}, f32[16,1024]{1,0:T(8,128)S(1)}) custom-call(s32[8,3]{1,0:T(8,128)S(1)} %copy.9.index, s32[8]{0:T(128)S(1)} %copy-done.3, bf16[8,3,128,128]{3,2,1,0:T(8,128)(2,1)S(1)} %copy-done.1, f32[16,512]{1,0:T(8,128)S(1)} %collective-permute-done.12.before, f32[16,512]{1,0:T(8,128)S(1)} %collective-permute-done.13.after, ...), custom_call_target="tpu_custom_call" | custom-call | flops 2000000 | bytes 2000000 | tf_op jit(solution)/shard_map/product/pallas_call | solution.py:20
  52.6 14.6 %all_to_all.11.arrived = f32[16,16,128]{2,1,0:T(8,128)S(1)} all-to-all(f32[16,16,128]{2,1,0:T(8,128)S(1)} %get-tuple-element.41), channel_id=1, replica_groups=mesh['rows'=16,'cols'=2] {'rows'}, dimensions={0} | all-to-all | bytes 262144 | tf_op jit(solution)/shard_map/all_to_all | solution.py:317
  67.8 1.3 %collective-permute-start.14 = (f32[16,512]{1,0:T(8,128)S(1)}, f32[16,512]{1,0:T(8,128)S(1)}, u32[]{:S(2)}, u32[]{:S(2)}) collective-permute-start(f32[16,512]{1,0:T(8,128)S(1)} %get-tuple-element.45), channel_id=1, source_target_pairs={{0,2},{2,4},{4,6},{6,8},{8,10},{10,12},{12,14},{14,16},{16,18},{18... | collective-permute-start | bytes 98312 | tf_op jit(solution)/shard_map/ppermute | solution.py:51
  69.1 1.3 %collective-permute-start.15 = (f32[16,512]{1,0:T(8,128)S(1)}, f32[16,512]{1,0:T(8,128)S(1)}, u32[]{:S(2)}, u32[]{:S(2)}) collective-permute-start(f32[16,512]{1,0:T(8,128)S(1)} %get-tuple-element.46), channel_id=1, source_target_pairs={{2,0},{4,2},{6,4},{8,6},{10,8},{12,10},{14,12},{16,14},{18,16},{20... | collective-permute-start | bytes 98312 | tf_op jit(solution)/shard_map/ppermute | solution.py:51
  70.5 1.8 %collective-permute-done.15.after = f32[16,512]{1,0:T(8,128)S(1)} collective-permute-done((f32[16,512]{1,0:T(8,128)S(1)}, f32[16,512]{1,0:T(8,128)S(1)}, u32[]{:S(2)}, u32[]{:S(2)}) %collective-permute-start.15) | collective-permute-done | bytes 32800 | tf_op jit(solution)/shard_map/ppermute | solution.py:51
  72.2 1.3 %smooth.1 = (f32[16,1024]{1,0:T(8,128)S(1)}, f32[16,128]{1,0:T(8,128)S(1)}) custom-call(s32[8,3]{1,0:T(8,128)S(1)} %copy.9.index, bf16[8,3,128,128]{3,2,1,0:T(8,128)(2,1)S(1)} %copy-done.1, f32[16,512]{1,0:T(8,128)S(1)} %collective-permute-done.14.before, f32[16,512]{1,0:T(8,128)S(1)} %collective-permute-done.15.after, ...), custom_call_target="tpu_custom_call" | custom-call | flops 2000000 | bytes 2000000 | tf_op jit(solution)/shard_map/smooth/pallas_call | solution.py:20
  73.5 4.2 %collective-permute-start.18 = (f32[16,128]{1,0:T(8,128)S(1)}, f32[16,128]{1,0:T(8,128)S(1)}, u32[]{:S(2)}, u32[]{:S(2)}) collective-permute-start(f32[16,128]{1,0:T(8,128)S(1)} %get-tuple-element.49), channel_id=1, source_target_pairs={{0,6},{2,4},{4,2},{6,0},{8,14},{10,12},{12,10},{14,8},{16,22},{18,... | collective-permute-start | bytes 24584 | tf_op jit(solution)/shard_map/ppermute | solution.py:43
  77.9 1.2 %collective-permute-done.18 = f32[16,128]{1,0:T(8,128)S(1)} collective-permute-done((f32[16,128]{1,0:T(8,128)S(1)}, f32[16,128]{1,0:T(8,128)S(1)}, u32[]{:S(2)}, u32[]{:S(2)}) %collective-permute-start.18) | collective-permute-done | bytes 8224 | tf_op jit(solution)/shard_map/ppermute | solution.py:43
  79.1 2.3 %collective-permute-done.17 = f32[16,128]{1,0:T(8,128)S(1)} collective-permute-done((f32[16,128]{1,0:T(8,128)S(1)}, f32[16,128]{1,0:T(8,128)S(1)}, u32[]{:S(2)}, u32[]{:S(2)}) %collective-permute-start.17) | collective-permute-done | bytes 8224 | tf_op jit(solution)/shard_map/ppermute | solution.py:43
  81.7 2.9 %collective-permute-start.20 = (f32[16,128]{1,0:T(8,128)S(1)}, f32[16,128]{1,0:T(8,128)S(1)}, u32[]{:S(2)}, u32[]{:S(2)}) collective-permute-start(f32[16,128]{1,0:T(8,128)S(1)} %add_add_fusion.refs_0_), channel_id=1, source_target_pairs={{0,16},{2,18},{4,20},{6,22},{8,24},{10,26},{12,28},{14,30},{16,0},... | collective-permute-start | bytes 24584 | tf_op jit(solution)/shard_map/ppermute | solution.py:43
  84.5 1.3 %collective-permute-start.19 = (f32[16,128]{1,0:T(8,128)S(1)}, f32[16,128]{1,0:T(8,128)S(1)}, u32[]{:S(2)}, u32[]{:S(2)}) collective-permute-start(f32[16,128]{1,0:T(8,128)S(1)} %add_add_fusion.refs_0_), channel_id=1, source_target_pairs={{0,8},{2,10},{4,12},{6,14},{8,0},{10,2},{12,4},{14,6},{16,24},{18,... | collective-permute-start | bytes 24584 | tf_op jit(solution)/shard_map/ppermute | solution.py:43
  85.9 1.1 %collective-permute-done.21.refs_3_ = f32[16,128]{1,0:T(8,128)S(1)} collective-permute-done((f32[16,128]{1,0:T(8,128)S(1)}, f32[16,128]{1,0:T(8,128)S(1)}, u32[]{:S(2)}, u32[]{:S(2)}) %collective-permute-start.21) | collective-permute-done | bytes 8224 | tf_op jit(solution)/shard_map/ppermute | solution.py:43
  86.9 1.3 %collective-permute-done.19.refs_1_ = f32[16,128]{1,0:T(8,128)S(1)} collective-permute-done((f32[16,128]{1,0:T(8,128)S(1)}, f32[16,128]{1,0:T(8,128)S(1)}, u32[]{:S(2)}, u32[]{:S(2)}) %collective-permute-start.19) | collective-permute-done | bytes 8224 | tf_op jit(solution)/shard_map/ppermute | solution.py:43
  88.2 0.7 scale.1
  (40 shorter events, 3.7 us)
Async XLA Ops:
  0.0 9.0 %copy-start.2 = (f32[16,1024]{1,0:T(8,128)S(1)}, f32[16,1024]{1,0:T(8,128)}, u32[]{:S(2)}) copy-start(f32[16,1024]{1,0:T(8,128)} %refs_4_.1) | copy-start | bytes 196612
  0.0 9.0 %collective-permute-start.2 = (f32[16,1024]{1,0:T(8,128)}, f32[16,1024]{1,0:T(8,128)S(1)}, u32[]{:S(2)}, u32[]{:S(2)}) collective-permute-start(f32[16,1024]{1,0:T(8,128)} %refs_4_.1), channel_id=1, source_target_pairs={{0,1},{1,0},{2,3},{3,2},{4,5},{5,4},{6,7},{7,6},{8,9},{9,8},{10,11... | collective-permute-start | bytes 196616 | tf_op jit(solution)/shard_map/ppermute | solution.py:43
  3.8 4.3 %copy-start.4 = (s32[8,3]{0,1:T(4,128)S(1)}, s32[8,3]{0,1:T(4,128)}, u32[]{:S(2)}) copy-start(s32[8,3]{0,1:T(4,128)} %param.6) | copy-start | bytes 292
  3.8 4.4 %collective-permute-start.1 = (f32[16,512]{1,0:T(8,128)S(1)}, f32[16,512]{1,0:T(8,128)S(1)}, u32[]{:S(2)}, u32[]{:S(2)}) collective-permute-start(f32[16,512]{1,0:T(8,128)S(1)} %get-tuple-element.51), channel_id=1, source_target_pairs={{2,0},{4,2},{6,4},{8,6},{10,8},{12,10},{14,12},{16,14},{18,16},{20... | collective-permute-start | bytes 98312 | tf_op jit(solution)/shard_map/ppermute | solution.py:51
  5.1 3.9 %collective-permute-start = (f32[16,512]{1,0:T(8,128)S(1)}, f32[16,512]{1,0:T(8,128)S(1)}, u32[]{:S(2)}, u32[]{:S(2)}) collective-permute-start(f32[16,512]{1,0:T(8,128)S(1)} %get-tuple-element.52), channel_id=1, source_target_pairs={{0,2},{2,4},{4,6},{6,8},{8,10},{10,12},{12,14},{14,16},{16,18},{18... | collective-permute-start | bytes 98312 | tf_op jit(solution)/shard_map/ppermute | solution.py:51
  9.0 1.1 %copy-start = (bf16[8,3,128,128]{3,2,1,0:T(8,128)(2,1)S(1)}, bf16[8,3,128,128]{3,2,1,0:T(8,128)(2,1)}, u32[]{:S(2)}) copy-start(bf16[8,3,128,128]{3,2,1,0:T(8,128)(2,1)} %weight.7) | copy-start | bytes 2359300
  11.8 7.3 %collective-permute-start.5 = (f32[40,128]{1,0:T(8,128)S(1)}, f32[40,128]{1,0:T(8,128)S(1)}, u32[]{:S(2)}, u32[]{:S(2)}) collective-permute-start(f32[40,128]{1,0:T(8,128)S(1)} %get-tuple-element.28), channel_id=1, source_target_pairs={{0,6},{2,4},{4,2},{6,0},{8,14},{10,12},{12,10},{14,8},{16,22},{18,... | collective-permute-start | bytes 61448 | tf_op jit(solution)/shard_map/ppermute | solution.py:43
  14.8 4.9 %collective-permute-start.4 = (f32[40,128]{1,0:T(8,128)S(1)}, f32[40,128]{1,0:T(8,128)S(1)}, u32[]{:S(2)}, u32[]{:S(2)}) collective-permute-start(f32[40,128]{1,0:T(8,128)S(1)} %get-tuple-element.28), channel_id=1, source_target_pairs={{0,4},{2,6},{4,0},{6,2},{8,12},{10,14},{12,8},{14,10},{16,20},{18,... | collective-permute-start | bytes 61448 | tf_op jit(solution)/shard_map/ppermute | solution.py:43
  15.4 4.3 %collective-permute-start.3 = (f32[40,128]{1,0:T(8,128)S(1)}, f32[40,128]{1,0:T(8,128)S(1)}, u32[]{:S(2)}, u32[]{:S(2)}) collective-permute-start(f32[40,128]{1,0:T(8,128)S(1)} %get-tuple-element.28), channel_id=1, source_target_pairs={{0,2},{2,0},{4,6},{6,4},{8,10},{10,8},{12,14},{14,12},{16,18},{18,... | collective-permute-start | bytes 61448 | tf_op jit(solution)/shard_map/ppermute | solution.py:43
  15.4 12.5 %collective-permute-start.10 = (f32[16,512]{1,0:T(8,128)S(1)}, f32[16,512]{1,0:T(8,128)S(1)}, u32[]{:S(2)}, u32[]{:S(2)}) collective-permute-start(f32[16,512]{1,0:T(8,128)S(1)} %get-tuple-element.32), channel_id=1, source_target_pairs={{0,2},{2,4},{4,6},{6,8},{8,10},{10,12},{12,14},{14,16},{16,18},{18... | collective-permute-start | bytes 98312 | tf_op jit(solution)/shard_map/ppermute | solution.py:51
  17.8 10.7 %collective-permute-start.11 = (f32[16,512]{1,0:T(8,128)S(1)}, f32[16,512]{1,0:T(8,128)S(1)}, u32[]{:S(2)}, u32[]{:S(2)}) collective-permute-start(f32[16,512]{1,0:T(8,128)S(1)} %get-tuple-element.33), channel_id=1, source_target_pairs={{2,0},{4,2},{6,4},{8,6},{10,8},{12,10},{14,12},{16,14},{18,16},{20... | collective-permute-start | bytes 98312 | tf_op jit(solution)/shard_map/ppermute | solution.py:51
  19.1 13.6 %collective-permute-start.9 = (f32[16,1024]{1,0:T(8,128)S(1)}, f32[16,1024]{1,0:T(8,128)S(1)}, u32[]{:S(2)}, u32[]{:S(2)}) collective-permute-start(f32[16,1024]{1,0:T(8,128)S(1)} %get-tuple-element.29.refs_6_), channel_id=1, source_target_pairs={{0,1},{1,0},{2,3},{3,2},{4,5},{5,4},{6,7},{7,6},{8,9},{9,8},{10,11... | collective-permute-start | bytes 196616 | tf_op jit(solution)/shard_map/ppermute | solution.py:43
  19.7 10.0 %collective-permute-start.8 = (f32[64,128]{1,0:T(8,128)S(1)}, f32[64,128]{1,0:T(8,128)S(1)}, u32[]{:S(2)}, u32[]{:S(2)}) collective-permute-start(f32[64,128]{1,0:T(8,128)S(1)} %constant_dynamic-update-slice_fusion.refs_0_), channel_id=1, source_target_pairs={{0,24},{2,26},{4,28},{6,30},{8,16},{10,18},{12,20},{14,22},{16,8},... | collective-permute-start | bytes 98312 | tf_op jit(solution)/shard_map/ppermute | solution.py:43
  27.9 4.8 %collective-permute-start.7 = (f32[64,128]{1,0:T(8,128)S(1)}, f32[64,128]{1,0:T(8,128)S(1)}, u32[]{:S(2)}, u32[]{:S(2)}) collective-permute-start(f32[64,128]{1,0:T(8,128)S(1)} %constant_dynamic-update-slice_fusion.refs_0_), channel_id=1, source_target_pairs={{0,16},{2,18},{4,20},{6,22},{8,24},{10,26},{12,28},{14,30},{16,0},... | collective-permute-start | bytes 98312 | tf_op jit(solution)/shard_map/ppermute | solution.py:43
  27.9 4.8 %collective-permute-start.6 = (f32[64,128]{1,0:T(8,128)S(1)}, f32[64,128]{1,0:T(8,128)S(1)}, u32[]{:S(2)}, u32[]{:S(2)}) collective-permute-start(f32[64,128]{1,0:T(8,128)S(1)} %constant_dynamic-update-slice_fusion.refs_0_), channel_id=1, source_target_pairs={{0,8},{2,10},{4,12},{6,14},{8,0},{10,2},{12,4},{14,6},{16,24},{18,... | collective-permute-start | bytes 98312 | tf_op jit(solution)/shard_map/ppermute | solution.py:43
  28.5 4.2 %copy-start.3 = (s32[8]{0:T(128)S(1)}, s32[8]{0:T(128)}, u32[]{:S(2)}) copy-start(s32[8]{0:T(128)} %mates.7) | copy-start | bytes 100
  29.7 21.8 %copy-start.1 = (bf16[8,3,128,128]{3,2,1,0:T(8,128)(2,1)S(1)}, bf16[8,3,128,128]{3,2,1,0:T(8,128)(2,1)}, u32[]{:S(2)}) copy-start(bf16[8,3,128,128]{3,2,1,0:T(8,128)(2,1)} %weight.7) | copy-start | bytes 2359300
  47.1 2.6 %collective-permute-start.12 = (f32[16,512]{1,0:T(8,128)S(1)}, f32[16,512]{1,0:T(8,128)S(1)}, u32[]{:S(2)}, u32[]{:S(2)}) collective-permute-start(f32[16,512]{1,0:T(8,128)S(1)} %get-tuple-element.38), channel_id=1, source_target_pairs={{0,2},{2,4},{4,6},{6,8},{8,10},{10,12},{12,14},{14,16},{16,18},{18... | collective-permute-start | bytes 98312 | tf_op jit(solution)/shard_map/ppermute | solution.py:51
  48.4 3.1 %collective-permute-start.13 = (f32[16,512]{1,0:T(8,128)S(1)}, f32[16,512]{1,0:T(8,128)S(1)}, u32[]{:S(2)}, u32[]{:S(2)}) collective-permute-start(f32[16,512]{1,0:T(8,128)S(1)} %get-tuple-element.39), channel_id=1, source_target_pairs={{2,0},{4,2},{6,4},{8,6},{10,8},{12,10},{14,12},{16,14},{18,16},{20... | collective-permute-start | bytes 98312 | tf_op jit(solution)/shard_map/ppermute | solution.py:51
  67.8 2.6 %collective-permute-start.14 = (f32[16,512]{1,0:T(8,128)S(1)}, f32[16,512]{1,0:T(8,128)S(1)}, u32[]{:S(2)}, u32[]{:S(2)}) collective-permute-start(f32[16,512]{1,0:T(8,128)S(1)} %get-tuple-element.45), channel_id=1, source_target_pairs={{0,2},{2,4},{4,6},{6,8},{8,10},{10,12},{12,14},{14,16},{16,18},{18... | collective-permute-start | bytes 98312 | tf_op jit(solution)/shard_map/ppermute | solution.py:51
  69.1 3.1 %collective-permute-start.15 = (f32[16,512]{1,0:T(8,128)S(1)}, f32[16,512]{1,0:T(8,128)S(1)}, u32[]{:S(2)}, u32[]{:S(2)}) collective-permute-start(f32[16,512]{1,0:T(8,128)S(1)} %get-tuple-element.46), channel_id=1, source_target_pairs={{2,0},{4,2},{6,4},{8,6},{10,8},{12,10},{14,12},{16,14},{18,16},{20... | collective-permute-start | bytes 98312 | tf_op jit(solution)/shard_map/ppermute | solution.py:51
  73.5 5.6 %collective-permute-start.18 = (f32[16,128]{1,0:T(8,128)S(1)}, f32[16,128]{1,0:T(8,128)S(1)}, u32[]{:S(2)}, u32[]{:S(2)}) collective-permute-start(f32[16,128]{1,0:T(8,128)S(1)} %get-tuple-element.49), channel_id=1, source_target_pairs={{0,6},{2,4},{4,2},{6,0},{8,14},{10,12},{12,10},{14,8},{16,22},{18,... | collective-permute-start | bytes 24584 | tf_op jit(solution)/shard_map/ppermute | solution.py:43
  77.7 3.7 %collective-permute-start.17 = (f32[16,128]{1,0:T(8,128)S(1)}, f32[16,128]{1,0:T(8,128)S(1)}, u32[]{:S(2)}, u32[]{:S(2)}) collective-permute-start(f32[16,128]{1,0:T(8,128)S(1)} %get-tuple-element.49), channel_id=1, source_target_pairs={{0,4},{2,6},{4,0},{6,2},{8,12},{10,14},{12,8},{14,10},{16,20},{18,... | collective-permute-start | bytes 24584 | tf_op jit(solution)/shard_map/ppermute | solution.py:43
  77.7 3.7 %collective-permute-start.16 = (f32[16,128]{1,0:T(8,128)S(1)}, f32[16,128]{1,0:T(8,128)S(1)}, u32[]{:S(2)}, u32[]{:S(2)}) collective-permute-start(f32[16,128]{1,0:T(8,128)S(1)} %get-tuple-element.49), channel_id=1, source_target_pairs={{0,2},{2,0},{4,6},{6,4},{8,10},{10,8},{12,14},{14,12},{16,18},{18,... | collective-permute-start | bytes 24584 | tf_op jit(solution)/shard_map/ppermute | solution.py:43
  81.4 5.5 %collective-permute-start.21 = (f32[16,128]{1,0:T(8,128)S(1)}, f32[16,128]{1,0:T(8,128)S(1)}, u32[]{:S(2)}, u32[]{:S(2)}) collective-permute-start(f32[16,128]{1,0:T(8,128)S(1)} %add_add_fusion.refs_0_), channel_id=1, source_target_pairs={{0,24},{2,26},{4,28},{6,30},{8,16},{10,18},{12,20},{14,22},{16,8},... | collective-permute-start | bytes 24584 | tf_op jit(solution)/shard_map/ppermute | solution.py:43
  81.7 5.3 %collective-permute-start.20 = (f32[16,128]{1,0:T(8,128)S(1)}, f32[16,128]{1,0:T(8,128)S(1)}, u32[]{:S(2)}, u32[]{:S(2)}) collective-permute-start(f32[16,128]{1,0:T(8,128)S(1)} %add_add_fusion.refs_0_), channel_id=1, source_target_pairs={{0,16},{2,18},{4,20},{6,22},{8,24},{10,26},{12,28},{14,30},{16,0},... | collective-permute-start | bytes 24584 | tf_op jit(solution)/shard_map/ppermute | solution.py:43
  84.5 3.7 %collective-permute-start.19 = (f32[16,128]{1,0:T(8,128)S(1)}, f32[16,128]{1,0:T(8,128)S(1)}, u32[]{:S(2)}, u32[]{:S(2)}) collective-permute-start(f32[16,128]{1,0:T(8,128)S(1)} %add_add_fusion.refs_0_), channel_id=1, source_target_pairs={{0,8},{2,10},{4,12},{6,14},{8,0},{10,2},{12,4},{14,6},{16,24},{18,... | collective-permute-start | bytes 24584 | tf_op jit(solution)/shard_map/ppermute | solution.py:43

commit v4 on v3

--- a/solution.py
+++ b/solution.py
@@ -45,10 +45,13 @@
     ]
 
 
-def from_sides(last, first, axis):
+def from_pairs(inner, outer, axis):
     peers = lax.axis_size(axis)
-    up = [(i, i + 1) for i in range(peers - 1)]
-    return lax.ppermute(last, axis, up), lax.ppermute(first, axis, [(j, i) for i, j in up])
+    up = [(i, i + 1) for i in range(1, peers - 1, 2)]
+    return (
+        lax.ppermute(outer, axis, up + [(j, i) for i, j in up]),
+        lax.ppermute(inner, axis, [(i, i ^ 1) for i in range(peers)]),
+    )
 
 
 def each(count, body):
@@ -85,11 +88,19 @@
         field[base + block, : split.shape[0], :] = split[:, block * length : (block + 1) * length]
 
 
-def fill_extended(field, before, own, after, length):
-    count = before.shape[1] // length
-    fill(field, 0, before, length)
-    fill(field, count, own, length)
-    fill(field, count + own.shape[1] // length, after, length)
+def parity_of(index):
+    return lax.rem(lax.div(index[0, 0], index.shape[0]), 2)
+
+
+def half(parity, vertices, width, length):
+    return pl.ds(pl.multiple_of(parity * (vertices - width), length), width)
+
+
+def fill_extended(field, parity, outer, own, inner, length):
+    margin, blocks = outer.shape[1] // length, own.shape[1] // length
+    fill(field, parity * (margin + blocks), outer, length)
+    fill(field, margin, own, length)
+    fill(field, (1 - parity) * (margin + blocks), inner, length)
 
 
 def neighbours(index, weight, field, block):
@@ -139,16 +150,30 @@
     full, edge, line = (rows, vertices), (rows, width), (1, vertices)
     slots = (row_devices, rows, length)
 
-    def first_body(index, weight, before, after, *refs):
-        peers, (payload, image, sent, scaled, last, first, degree, ones_field) = (
+    def halves(parity):
+        return (
+            half(parity, vertices, width, length),
+            half(1 - parity, vertices, width, length),
+        )
+
+    def edges(index, value, outer, inner):
+        at_outer, at_inner = halves(parity_of(index))
+        outer[...] = value[:, at_outer]
+        inner[...] = value[:, at_inner]
+
+    def first_body(index, weight, outer_states, inner_states, *refs):
+        peers, (payload, image, sent, scaled, outer, inner, degree, ones_field) = (
             refs[:col_devices],
             refs[col_devices:],
         )
+        parity = parity_of(index)
+        at_inner, at_outer = halves(parity)
         fill_extended(
             ones_field,
-            padded(before[...], rows),
+            parity,
+            padded(outer_states[:, at_outer], rows),
             padded(peers[0][...], rows),
-            padded(after[...], rows),
+            padded(inner_states[:, at_inner], rows),
             length,
         )
         ones_field[:, PARTS * rows :, :] = jnp.ones((2 * blocks, 16, length), jnp.bfloat16)
@@ -171,11 +196,10 @@
             everyone, other, (((1,), (1,)), ((), ())), precision=EXACT, preferred_element_type=F32
         )
         sent[...] = image[:local_cols, :]
-        last[...] = scaled[:, vertices - width :]
-        first[...] = scaled[:, :width]
-
-    def second_body(index, weight, before, after, scaled, image, offset, spread):
-        fill_extended(spread, before[...], scaled[...], after[...], length)
+        edges(index, scaled, outer, inner)
+
+    def second_body(index, weight, outer, inner, scaled, image, offset, spread):
+        fill_extended(spread, parity_of(index), outer[...], scaled[...], inner[...], length)
 
         def one(block):
             at = lanes(block, length)
@@ -215,7 +239,7 @@
 
         each(blocks, one)
 
-    def coarse_body(mates, arrived, remain, pair_degree, coarse, fix, last, first):
+    def coarse_body(index, mates, arrived, remain, pair_degree, coarse, fix, outer, inner):
         def one(block):
             at = lanes(block, length)
             value = remain[:, at] + arrived[lax.div(mates[block], blocks)]
@@ -223,11 +247,10 @@
             fix[:, at] = DAMPING * value / pair_degree[:, at]
 
         each(blocks, one)
-        last[...] = fix[:, vertices - width :]
-        first[...] = fix[:, :width]
-
-    def product_body(index, mates, weight, before, after, fix, degree, out, product, spread):
-        fill_extended(spread, before[...], fix[...], after[...], length)
+        edges(index, fix, outer, inner)
+
+    def product_body(index, mates, weight, outer, inner, fix, degree, out, product, spread):
+        fill_extended(spread, parity_of(index), outer[...], fix[...], inner[...], length)
 
         def one(block):
             at = lanes(block, length)
@@ -237,7 +260,9 @@
 
         each(blocks, one)
 
-    def fix_body(mates, arrived, product, coarse, fix, pair_degree, presmooth, second, last, first):
+    def fix_body(
+        index, mates, arrived, product, coarse, fix, pair_degree, presmooth, second, outer, inner
+    ):
         def one(block):
             at = lanes(block, length)
             image = product[:, at] + arrived[lax.div(mates[block], blocks)]
@@ -245,11 +270,12 @@
             second[:, at] = presmooth[:, at] + (fix[:, at] + step)
 
         each(blocks, one)
-        last[...] = second[:, vertices - width :]
-        first[...] = second[:, :width]
-
-    def smooth_body(index, weight, before, after, second, residual, degree, smooth, squares, spread):
-        fill_extended(spread, before[...], second[...], after[...], length)
+        edges(index, second, outer, inner)
+
+    def smooth_body(
+        index, weight, outer, inner, second, residual, degree, smooth, squares, spread
+    ):
+        fill_extended(spread, parity_of(index), outer[...], second[...], inner[...], length)
 
         def one(block):
             at = lanes(block, length)
@@ -269,14 +295,14 @@
         norm = jnp.sqrt(total[:local_cols, :1] / (vertices * row_devices) + EPSILON)
         correction[...] = smooth[:local_cols, :] / norm
 
-    before, after = from_sides(states[:, vertices - width :], states[:, :width], "rows")
+    outer, inner = from_pairs(states, states, "rows")
     peers = exchanged(states, "cols", 1, col_devices)
-    payload, image, sent, scaled, last, first, degree = kernel_call(
+    payload, image, sent, scaled, outer, inner, degree = kernel_call(
         first_body,
         "image",
         [(total_cols + blocks, length), full, (local_cols, vertices), full, edge, edge, line],
         [adj_index],
-        [adj_weight, before, after, *peers],
+        [adj_weight, outer, inner, *peers],
         [pltpu.VMEM((2 * blocks, PARTS * rows + 16, length), jnp.bfloat16)],
     )
     stride = 1
@@ -288,10 +314,10 @@
             for piece in pieces[1:]:
                 summed = summed + piece[:total_cols]
             payload = jnp.concatenate([summed] + [piece[total_cols:] for piece in pieces], axis=0)
-    before, after = from_sides(last, first, "rows")
+    outer, inner = from_pairs(inner, outer, "rows")
     images = exchanged(sent, "cols", 1, col_devices)
     (offset,) = kernel_call(
-        second_body, "offset", [full], [adj_index], [adj_weight, before, after, scaled, image], [field]
+        second_body, "offset", [full], [adj_index], [adj_weight, outer, inner, scaled, image], [field]
     )
     out, remain, residual, presmooth, pair_degree = kernel_call(
         ritz_body,
@@ -302,33 +328,33 @@
         [pltpu.VMEM((row_devices * blocks, length), F32)],
     )
     arrived = lax.all_to_all(out, "rows", split_axis=0, concat_axis=0, tiled=True)
-    coarse, fix, last, first = kernel_call(
-        coarse_body, "coarse", [full, full, edge, edge], [partner], [arrived, remain, pair_degree]
-    )
-    before, after = from_sides(last, first, "rows")
+    coarse, fix, outer, inner = kernel_call(
+        coarse_body, "coarse", [full, full, edge, edge], [adj_index, partner], [arrived, remain, pair_degree]
+    )
+    outer, inner = from_pairs(inner, outer, "rows")
     out, product = kernel_call(
         product_body,
         "product",
         [slots, full],
         [adj_index, partner],
-        [adj_weight, before, after, fix, degree],
+        [adj_weight, outer, inner, fix, degree],
         [field],
     )
     arrived = lax.all_to_all(out, "rows", split_axis=0, concat_axis=0, tiled=True)
-    second, last, first = kernel_call(
+    second, outer, inner = kernel_call(
         fix_body,
         "fix",
         [full, edge, edge],
-        [partner],
+        [adj_index, partner],
         [arrived, product, coarse, fix, pair_degree, presmooth],
     )
-    before, after = from_sides(last, first, "rows")
+    outer, inner = from_pairs(inner, outer, "rows")
     smooth, squares = kernel_call(
         smooth_body,
         "smooth",
         [full, (rows, length)],
         [adj_index],
-        [adj_weight, before, after, second, residual, degree],
+        [adj_weight, outer, inner, second, residual, degree],
         [field],
     )
     stride = 1

time: 89.4 us -> 78.3 us (0.88)
  starting transfers between devices: 38 us -> 29.8 us
  waiting for transfers between devices: 13.1 us -> 10.5 us
  blocking collectives: 25.7 us -> 24.7 us
    ppermute x8, starting transfers between devices: 13.1 us -> 7.52 us  [the longest x4 4.89 us: from_pairs(): lax.ppermute(inner, axis, [(i, i ^ 1) for i in range(peers)])]
    ppermute x8, waiting for transfers between devices: 4.34 us -> 1.73 us  [the longest x4 1.72 us: from_pairs(): lax.ppermute(inner, axis, [(i, i ^ 1) for i in range(peers)])]
    ppermute x14, starting transfers between devices: 24.9 us -> 22.3 us  [exchanged(): lax.ppermute(value, axis, [(i, i ^ mask * stride) for i in range(peers)])]
    unnamed x14, local copies, waits for them, and re-layouts: 1.24 us -> 2.75 us
    all_to_all x2, blocking collectives: 25.7 us -> 24.7 us  [local(): lax.all_to_all(out, 'rows', split_axis=0, concat_axis=0, tiled=True)]
  transfers between devices with their start and end apart: 22 -> 22, of which waited for: 9 -> 10; matrix products, arithmetic and copies ran while one was open for 1% -> 1% of each run, Pallas kernels for 1% -> 1%
where the time goes in v4:
time: 78.3 us; the launch traced here: 77.9 us
  starting transfers between devices  29.8 us (38%)
  blocking collectives  24.7 us (32%)
  waiting for transfers between devices  10.5 us (13%)
  Pallas kernels  10 us (13%)
  local copies, waits for them, and re-layouts  2.75 us (4%)
    all_to_all x2, blocking collectives, local(): lax.all_to_all(out, 'rows', split_axis=0, concat_axis=0, tiled=True)  24.7 us
    ppermute x14, starting transfers between devices, exchanged(): lax.ppermute(value, axis, [(i, i ^ mask * stride) for i in range(peers)])  22.3 us
    pallas_call x8, Pallas kernels, kernel_call(): pl.pallas_call(body, name=name, out_shape=[jax.ShapeDtypeStruct(shape, F3...  10 us
    ppermute x14, waiting for transfers between devices, exchanged(): lax.ppermute(value, axis, [(i, i ^ mask * stride) for i in range(peers)])  8.77 us
    ppermute x4, starting transfers between devices, from_pairs(): lax.ppermute(inner, axis, [(i, i ^ 1) for i in range(peers)])  4.89 us
    unnamed x14, local copies, waits for them, and re-layouts  2.75 us
    ppermute x4, starting transfers between devices, from_pairs(): lax.ppermute(outer, axis, up + [(j, i) for i, j in up])  2.63 us
    ppermute x4, waiting for transfers between devices, from_pairs(): lax.ppermute(inner, axis, [(i, i ^ 1) for i in range(peers)])  1.72 us
  transfers between devices with their start and end apart: 22, of which 10 were waited for; matrix products, arithmetic and copies ran while one was open for 1% of the time, Pallas kernels for 1%

profile of v4, /device:TPU:0, one launch (start us, length us, event | category | flops | bytes accessed | tf_op | source)
XLA Modules:
  0.0 77.9 jit_solution(4157279439625688712)
XLA Ops:
  0.0 3.0 %collective-permute-start.2 = (f32[16,1024]{1,0:T(8,128)}, f32[16,1024]{1,0:T(8,128)S(1)}, u32[]{:S(2)}, u32[]{:S(2)}) collective-permute-start(f32[16,1024]{1,0:T(8,128)} %refs_4_.1), channel_id=1, source_target_pairs={{0,1},{1,0},{2,3},{3,2},{4,5},{5,4},{6,7},{7,6},{8,9},{9,8},{10,11... | collective-permute-start | bytes 196616 | tf_op jit(solution)/shard_map/ppermute | solution.py:43
  3.0 0.7 collective-permute-start
  3.7 0.8 copy.11.index
  4.4 1.0 %collective-permute-done.2.refs_1_.refs_5_ = f32[16,1024]{1,0:T(8,128)S(1)} collective-permute-done((f32[16,1024]{1,0:T(8,128)}, f32[16,1024]{1,0:T(8,128)S(1)}, u32[]{:S(2)}, u32[]{:S(2)}) %collective-permute-start.2) | collective-permute-done | bytes 65568 | tf_op jit(solution)/shard_map/ppermute | solution.py:43
  5.5 1.1 %copy-done = bf16[8,3,128,128]{3,2,1,0:T(8,128)(2,1)S(1)} copy-done((bf16[8,3,128,128]{3,2,1,0:T(8,128)(2,1)S(1)}, bf16[8,3,128,128]{3,2,1,0:T(8,128)(2,1)}, u32[]{:S(2)}) %copy-start) | copy-done | bytes 786456
  6.6 0.8 %copy-done.2 = f32[16,1024]{1,0:T(8,128)S(1)} copy-done((f32[16,1024]{1,0:T(8,128)S(1)}, f32[16,1024]{1,0:T(8,128)}, u32[]{:S(2)}) %copy-start.2) | copy-done | bytes 65560
  7.4 1.7 %image.1 = (f32[40,128]{1,0:T(8,128)S(1)}, f32[16,1024]{1,0:T(8,128)S(1)}, f32[16,1024]{1,0:T(8,128)S(1)}, f32[16,1024]{1,0:T(8,128)S(1)}, f32[16,512]{1,0:T(8,1...) custom-call(s32[8,3]{1,0:T(8,128)S(1)} %copy.11.index, bf16[8,3,128,128]{3,2,1,0:T(8,128)(2,1)S(1)} %copy-done, ...), custom_call_target="tpu_custom_call" | custom-call | flops 2000000 | bytes 2000000 | tf_op jit(solution)/shard_map/image/pallas_call | solution.py:20
  9.2 5.9 %collective-permute-start.5 = (f32[40,128]{1,0:T(8,128)S(1)}, f32[40,128]{1,0:T(8,128)S(1)}, u32[]{:S(2)}, u32[]{:S(2)}) collective-permute-start(f32[40,128]{1,0:T(8,128)S(1)} %get-tuple-element.28), channel_id=1, source_target_pairs={{0,6},{2,4},{4,2},{6,0},{8,14},{10,12},{12,10},{14,8},{16,22},{18,... | collective-permute-start | bytes 61448 | tf_op jit(solution)/shard_map/ppermute | solution.py:43
  15.9 3.3 %collective-permute-start.11 = (f32[16,512]{1,0:T(8,128)S(1)}, f32[16,512]{1,0:T(8,128)S(1)}, u32[]{:S(2)}, u32[]{:S(2)}) collective-permute-start(f32[16,512]{1,0:T(8,128)S(1)} %get-tuple-element.33), channel_id=1, source_target_pairs={{0,2},{2,0},{4,6},{6,4},{8,10},{10,8},{12,14},{14,12},{16,18},{18,... | collective-permute-start | bytes 98312 | tf_op jit(solution)/shard_map/ppermute | solution.py:53
  19.7 3.6 %collective-permute-start.8 = (f32[64,128]{1,0:T(8,128)S(1)}, f32[64,128]{1,0:T(8,128)S(1)}, u32[]{:S(2)}, u32[]{:S(2)}) collective-permute-start(f32[64,128]{1,0:T(8,128)S(1)} %constant_dynamic-update-slice_fusion.refs_0_), channel_id=1, source_target_pairs={{0,24},{2,26},{4,28},{6,30},{8,16},{10,18},{12,20},{14,22},{16,8},... | collective-permute-start | bytes 98312 | tf_op jit(solution)/shard_map/ppermute | solution.py:43
  23.4 0.8 %collective-permute-start.6 = (f32[64,128]{1,0:T(8,128)S(1)}, f32[64,128]{1,0:T(8,128)S(1)}, u32[]{:S(2)}, u32[]{:S(2)}) collective-permute-start(f32[64,128]{1,0:T(8,128)S(1)} %constant_dynamic-update-slice_fusion.refs_0_), channel_id=1, source_target_pairs={{0,8},{2,10},{4,12},{6,14},{8,0},{10,2},{12,4},{14,6},{16,24},{18,... | collective-permute-start | bytes 98312 | tf_op jit(solution)/shard_map/ppermute | solution.py:43
  24.2 1.1 %offset.1.refs_10_ = f32[16,1024]{1,0:T(8,128)S(1)} custom-call(s32[8,3]{1,0:T(8,128)S(1)} %copy.11.index, bf16[8,3,128,128]{3,2,1,0:T(8,128)(2,1)S(1)} %copy-done, f32[16,512]{1,0:T(8,128)S(1)} %collective-permute-done.10.outer, f32[16,512]{1,0:T(8,128)S(1)} %collective-permute-done.11.inner, f32[16,1024]{1,0:T(8,128)S(1)} %get-tuple-element.31.scaled.refs_9_, ...), custom_call_target="tpu_custom_call" | custom-call | flops 2000000 | bytes 2000000 | tf_op jit(solution)/shard_map/offset/pallas_call | solution.py:20
  25.5 2.7 %collective-permute-done.7.refs_2_ = f32[64,128]{1,0:T(8,128)S(1)} collective-permute-done((f32[64,128]{1,0:T(8,128)S(1)}, f32[64,128]{1,0:T(8,128)S(1)}, u32[]{:S(2)}, u32[]{:S(2)}) %collective-permute-start.7) | collective-permute-done | bytes 32800 | tf_op jit(solution)/shard_map/ppermute | solution.py:43
  28.2 2.7 %ritz.1 = (f32[16,16,128]{2,1,0:T(8,128)S(1)}, f32[16,1024]{1,0:T(8,128)S(1)}, f32[16,1024]{1,0:T(8,128)S(1)}, f32[16,1024]{1,0:T(8,128)S(1)}, f32[1,1024]{1,0:T(1,128)S(1)}) custom-call(s32[8,3]{1,0:T(8,128)S(1)} %copy.11.index, s32[8]{0:T(128)S(1)} %copy-done.4, f32[64,128]{1,0:T(8,128)S(1)} %constant_dynamic-update-slice_fusion.refs_0_, ...), custom_call_target="tpu_custom_call" | custom-call | flops 2000000 | bytes 2000000 | tf_op jit(solution)/shard_map/ritz/pallas_call | solution.py:20
  30.9 11.1 %all_to_all.10.arrived = f32[16,16,128]{2,1,0:T(8,128)S(1)} all-to-all(f32[16,16,128]{2,1,0:T(8,128)S(1)} %get-tuple-element.35), channel_id=1, replica_groups=mesh['rows'=16,'cols'=2] {'rows'}, dimensions={0} | all-to-all | bytes 262144 | tf_op jit(solution)/shard_map/all_to_all | solution.py:330
  42.7 0.7 collective-permute-start.12
  43.4 0.8 %collective-permute-start.13 = (f32[16,512]{1,0:T(8,128)S(1)}, f32[16,512]{1,0:T(8,128)S(1)}, u32[]{:S(2)}, u32[]{:S(2)}) collective-permute-start(f32[16,512]{1,0:T(8,128)S(1)} %get-tuple-element.39), channel_id=1, source_target_pairs={{0,2},{2,0},{4,6},{6,4},{8,10},{10,8},{12,14},{14,12},{16,18},{18,... | collective-permute-start | bytes 98312 | tf_op jit(solution)/shard_map/ppermute | solution.py:53
  44.2 0.9 %collective-permute-done.13.inner = f32[16,512]{1,0:T(8,128)S(1)} collective-permute-done((f32[16,512]{1,0:T(8,128)S(1)}, f32[16,512]{1,0:T(8,128)S(1)}, u32[]{:S(2)}, u32[]{:S(2)}) %collective-permute-start.13) | collective-permute-done | bytes 32800 | tf_op jit(solution)/shard_map/ppermute | solution.py:53
  45.0 1.2 %product.1 = (f32[16,16,128]{2,1,0:T(8,128)S(1)}, f32[16,1024]{1,0:T(8,128)S(1)}) custom-call(s32[8,3]{1,0:T(8,128)S(1)} %copy.11.index, s32[8]{0:T(128)S(1)} %copy-done.4, bf16[8,3,128,128]{3,2,1,0:T(8,128)(2,1)S(1)} %copy-done.1, f32[16,512]{1,0:T(8,128)S(1)} %collective-permute-done.12.outer, f32[16,512]{1,0:T(8,128)S(1)} %collective-permute-done.13.inner, ...), custom_call_target="tpu_custom_call" | custom-call | flops 2000000 | bytes 2000000 | tf_op jit(solution)/shard_map/product/pallas_call | solution.py:20
  46.2 13.6 %all_to_all.11.arrived = f32[16,16,128]{2,1,0:T(8,128)S(1)} all-to-all(f32[16,16,128]{2,1,0:T(8,128)S(1)} %get-tuple-element.41), channel_id=1, replica_groups=mesh['rows'=16,'cols'=2] {'rows'}, dimensions={0} | all-to-all | bytes 262144 | tf_op jit(solution)/shard_map/all_to_all | solution.py:343
  60.4 0.7 collective-permute-start.14
  61.1 0.8 %collective-permute-start.15 = (f32[16,512]{1,0:T(8,128)S(1)}, f32[16,512]{1,0:T(8,128)S(1)}, u32[]{:S(2)}, u32[]{:S(2)}) collective-permute-start(f32[16,512]{1,0:T(8,128)S(1)} %get-tuple-element.46), channel_id=1, source_target_pairs={{0,2},{2,0},{4,6},{6,4},{8,10},{10,8},{12,14},{14,12},{16,18},{18,... | collective-permute-start | bytes 98312 | tf_op jit(solution)/shard_map/ppermute | solution.py:53
  61.9 0.9 %collective-permute-done.15.inner = f32[16,512]{1,0:T(8,128)S(1)} collective-permute-done((f32[16,512]{1,0:T(8,128)S(1)}, f32[16,512]{1,0:T(8,128)S(1)}, u32[]{:S(2)}, u32[]{:S(2)}) %collective-permute-start.15) | collective-permute-done | bytes 32800 | tf_op jit(solution)/shard_map/ppermute | solution.py:53
  62.8 1.3 %smooth.1 = (f32[16,1024]{1,0:T(8,128)S(1)}, f32[16,128]{1,0:T(8,128)S(1)}) custom-call(s32[8,3]{1,0:T(8,128)S(1)} %copy.11.index, bf16[8,3,128,128]{3,2,1,0:T(8,128)(2,1)S(1)} %copy-done.1, f32[16,512]{1,0:T(8,128)S(1)} %collective-permute-done.14.outer, f32[16,512]{1,0:T(8,128)S(1)} %collective-permute-done.15.inner, ...), custom_call_target="tpu_custom_call" | custom-call | flops 2000000 | bytes 2000000 | tf_op jit(solution)/shard_map/smooth/pallas_call | solution.py:20
  64.0 3.4 %collective-permute-start.18 = (f32[16,128]{1,0:T(8,128)S(1)}, f32[16,128]{1,0:T(8,128)S(1)}, u32[]{:S(2)}, u32[]{:S(2)}) collective-permute-start(f32[16,128]{1,0:T(8,128)S(1)} %get-tuple-element.49), channel_id=1, source_target_pairs={{0,6},{2,4},{4,2},{6,0},{8,14},{10,12},{12,10},{14,8},{16,22},{18,... | collective-permute-start | bytes 24584 | tf_op jit(solution)/shard_map/ppermute | solution.py:43
  67.9 1.0 %collective-permute-done.18 = f32[16,128]{1,0:T(8,128)S(1)} collective-permute-done((f32[16,128]{1,0:T(8,128)S(1)}, f32[16,128]{1,0:T(8,128)S(1)}, u32[]{:S(2)}, u32[]{:S(2)}) %collective-permute-start.18) | collective-permute-done | bytes 8224 | tf_op jit(solution)/shard_map/ppermute | solution.py:43
  68.8 2.3 %collective-permute-done.17 = f32[16,128]{1,0:T(8,128)S(1)} collective-permute-done((f32[16,128]{1,0:T(8,128)S(1)}, f32[16,128]{1,0:T(8,128)S(1)}, u32[]{:S(2)}, u32[]{:S(2)}) %collective-permute-start.17) | collective-permute-done | bytes 8224 | tf_op jit(solution)/shard_map/ppermute | solution.py:43
  71.1 1.2 %collective-permute-start.21 = (f32[16,128]{1,0:T(8,128)S(1)}, f32[16,128]{1,0:T(8,128)S(1)}, u32[]{:S(2)}, u32[]{:S(2)}) collective-permute-start(f32[16,128]{1,0:T(8,128)S(1)} %add_add_fusion.refs_0_), channel_id=1, source_target_pairs={{0,24},{2,26},{4,28},{6,30},{8,16},{10,18},{12,20},{14,22},{16,8},... | collective-permute-start | bytes 24584 | tf_op jit(solution)/shard_map/ppermute | solution.py:43
  72.3 1.1 %collective-permute-start.20 = (f32[16,128]{1,0:T(8,128)S(1)}, f32[16,128]{1,0:T(8,128)S(1)}, u32[]{:S(2)}, u32[]{:S(2)}) collective-permute-start(f32[16,128]{1,0:T(8,128)S(1)} %add_add_fusion.refs_0_), channel_id=1, source_target_pairs={{0,16},{2,18},{4,20},{6,22},{8,24},{10,26},{12,28},{14,30},{16,0},... | collective-permute-start | bytes 24584 | tf_op jit(solution)/shard_map/ppermute | solution.py:43
  73.4 2.2 %collective-permute-start.19 = (f32[16,128]{1,0:T(8,128)S(1)}, f32[16,128]{1,0:T(8,128)S(1)}, u32[]{:S(2)}, u32[]{:S(2)}) collective-permute-start(f32[16,128]{1,0:T(8,128)S(1)} %add_add_fusion.refs_0_), channel_id=1, source_target_pairs={{0,8},{2,10},{4,12},{6,14},{8,0},{10,2},{12,4},{14,6},{16,24},{18,... | collective-permute-start | bytes 24584 | tf_op jit(solution)/shard_map/ppermute | solution.py:43
  75.6 1.1 %collective-permute-done.21.refs_3_ = f32[16,128]{1,0:T(8,128)S(1)} collective-permute-done((f32[16,128]{1,0:T(8,128)S(1)}, f32[16,128]{1,0:T(8,128)S(1)}, u32[]{:S(2)}, u32[]{:S(2)}) %collective-permute-start.21) | collective-permute-done | bytes 8224 | tf_op jit(solution)/shard_map/ppermute | solution.py:43
  77.2 0.7 scale.1
  (39 shorter events, 3.8 us)
Async XLA Ops:
  0.0 5.4 %collective-permute-start.2 = (f32[16,1024]{1,0:T(8,128)}, f32[16,1024]{1,0:T(8,128)S(1)}, u32[]{:S(2)}, u32[]{:S(2)}) collective-permute-start(f32[16,1024]{1,0:T(8,128)} %refs_4_.1), channel_id=1, source_target_pairs={{0,1},{1,0},{2,3},{3,2},{4,5},{5,4},{6,7},{7,6},{8,9},{9,8},{10,11... | collective-permute-start | bytes 196616 | tf_op jit(solution)/shard_map/ppermute | solution.py:43
  3.0 2.5 %collective-permute-start.1 = (f32[16,1024]{1,0:T(8,128)}, f32[16,1024]{1,0:T(8,128)S(1)}, u32[]{:S(2)}, u32[]{:S(2)}) collective-permute-start(f32[16,1024]{1,0:T(8,128)} %refs_4_.1), channel_id=1, source_target_pairs={{0,2},{2,0},{4,6},{6,4},{8,10},{10,8},{12,14},{14,12},{16,18},{18,... | collective-permute-start | bytes 196616 | tf_op jit(solution)/shard_map/ppermute | solution.py:53
  3.0 2.5 %collective-permute-start = (f32[16,1024]{1,0:T(8,128)}, f32[16,1024]{1,0:T(8,128)S(1)}, u32[]{:S(2)}, u32[]{:S(2)}) collective-permute-start(f32[16,1024]{1,0:T(8,128)} %refs_4_.1), channel_id=1, source_target_pairs={{2,4},{6,8},{10,12},{14,16},{18,20},{22,24},{26,28},{4,2},{8,6},{1... | collective-permute-start | bytes 196616 | tf_op jit(solution)/shard_map/ppermute | solution.py:52
  5.5 1.1 %copy-start = (bf16[8,3,128,128]{3,2,1,0:T(8,128)(2,1)S(1)}, bf16[8,3,128,128]{3,2,1,0:T(8,128)(2,1)}, u32[]{:S(2)}) copy-start(bf16[8,3,128,128]{3,2,1,0:T(8,128)(2,1)} %weight.7) | copy-start | bytes 2359300
  6.6 0.8 %copy-start.2 = (f32[16,1024]{1,0:T(8,128)S(1)}, f32[16,1024]{1,0:T(8,128)}, u32[]{:S(2)}) copy-start(f32[16,1024]{1,0:T(8,128)} %refs_4_.1) | copy-start | bytes 196612
  9.2 10.0 %collective-permute-start.5 = (f32[40,128]{1,0:T(8,128)S(1)}, f32[40,128]{1,0:T(8,128)S(1)}, u32[]{:S(2)}, u32[]{:S(2)}) collective-permute-start(f32[40,128]{1,0:T(8,128)S(1)} %get-tuple-element.28), channel_id=1, source_target_pairs={{0,6},{2,4},{4,2},{6,0},{8,14},{10,12},{12,10},{14,8},{16,22},{18,... | collective-permute-start | bytes 61448 | tf_op jit(solution)/shard_map/ppermute | solution.py:43
  15.0 4.6 %collective-permute-start.4 = (f32[40,128]{1,0:T(8,128)S(1)}, f32[40,128]{1,0:T(8,128)S(1)}, u32[]{:S(2)}, u32[]{:S(2)}) collective-permute-start(f32[40,128]{1,0:T(8,128)S(1)} %get-tuple-element.28), channel_id=1, source_target_pairs={{0,4},{2,6},{4,0},{6,2},{8,12},{10,14},{12,8},{14,10},{16,20},{18,... | collective-permute-start | bytes 61448 | tf_op jit(solution)/shard_map/ppermute | solution.py:43
  15.0 4.6 %collective-permute-start.3 = (f32[40,128]{1,0:T(8,128)S(1)}, f32[40,128]{1,0:T(8,128)S(1)}, u32[]{:S(2)}, u32[]{:S(2)}) collective-permute-start(f32[40,128]{1,0:T(8,128)S(1)} %get-tuple-element.28), channel_id=1, source_target_pairs={{0,2},{2,0},{4,6},{6,4},{8,10},{10,8},{12,14},{14,12},{16,18},{18,... | collective-permute-start | bytes 61448 | tf_op jit(solution)/shard_map/ppermute | solution.py:43
  15.2 8.1 %collective-permute-start.10 = (f32[16,512]{1,0:T(8,128)S(1)}, f32[16,512]{1,0:T(8,128)S(1)}, u32[]{:S(2)}, u32[]{:S(2)}) collective-permute-start(f32[16,512]{1,0:T(8,128)S(1)} %get-tuple-element.32), channel_id=1, source_target_pairs={{2,4},{6,8},{10,12},{14,16},{18,20},{22,24},{26,28},{4,2},{8,6},{1... | collective-permute-start | bytes 98312 | tf_op jit(solution)/shard_map/ppermute | solution.py:52
  15.9 8.3 %collective-permute-start.11 = (f32[16,512]{1,0:T(8,128)S(1)}, f32[16,512]{1,0:T(8,128)S(1)}, u32[]{:S(2)}, u32[]{:S(2)}) collective-permute-start(f32[16,512]{1,0:T(8,128)S(1)} %get-tuple-element.33), channel_id=1, source_target_pairs={{0,2},{2,0},{4,6},{6,4},{8,10},{10,8},{12,14},{14,12},{16,18},{18,... | collective-permute-start | bytes 98312 | tf_op jit(solution)/shard_map/ppermute | solution.py:53
  19.1 9.0 %collective-permute-start.9 = (f32[16,1024]{1,0:T(8,128)S(1)}, f32[16,1024]{1,0:T(8,128)S(1)}, u32[]{:S(2)}, u32[]{:S(2)}) collective-permute-start(f32[16,1024]{1,0:T(8,128)S(1)} %get-tuple-element.29.refs_6_), channel_id=1, source_target_pairs={{0,1},{1,0},{2,3},{3,2},{4,5},{5,4},{6,7},{7,6},{8,9},{9,8},{10,11... | collective-permute-start | bytes 196616 | tf_op jit(solution)/shard_map/ppermute | solution.py:43
  19.7 5.8 %collective-permute-start.8 = (f32[64,128]{1,0:T(8,128)S(1)}, f32[64,128]{1,0:T(8,128)S(1)}, u32[]{:S(2)}, u32[]{:S(2)}) collective-permute-start(f32[64,128]{1,0:T(8,128)S(1)} %constant_dynamic-update-slice_fusion.refs_0_), channel_id=1, source_target_pairs={{0,24},{2,26},{4,28},{6,30},{8,16},{10,18},{12,20},{14,22},{16,8},... | collective-permute-start | bytes 98312 | tf_op jit(solution)/shard_map/ppermute | solution.py:43
  23.4 4.8 %collective-permute-start.7 = (f32[64,128]{1,0:T(8,128)S(1)}, f32[64,128]{1,0:T(8,128)S(1)}, u32[]{:S(2)}, u32[]{:S(2)}) collective-permute-start(f32[64,128]{1,0:T(8,128)S(1)} %constant_dynamic-update-slice_fusion.refs_0_), channel_id=1, source_target_pairs={{0,16},{2,18},{4,20},{6,22},{8,24},{10,26},{12,28},{14,30},{16,0},... | collective-permute-start | bytes 98312 | tf_op jit(solution)/shard_map/ppermute | solution.py:43
  23.4 4.8 %collective-permute-start.6 = (f32[64,128]{1,0:T(8,128)S(1)}, f32[64,128]{1,0:T(8,128)S(1)}, u32[]{:S(2)}, u32[]{:S(2)}) collective-permute-start(f32[64,128]{1,0:T(8,128)S(1)} %constant_dynamic-update-slice_fusion.refs_0_), channel_id=1, source_target_pairs={{0,8},{2,10},{4,12},{6,14},{8,0},{10,2},{12,4},{14,6},{16,24},{18,... | collective-permute-start | bytes 98312 | tf_op jit(solution)/shard_map/ppermute | solution.py:43
  24.2 4.0 %copy-start.3 = (f32[16,1024]{1,0:T(8,128)S(1)}, f32[16,1024]{1,0:T(8,128)}, u32[]{:S(2)}) copy-start(f32[16,1024]{1,0:T(8,128)} %refs_4_.1) | copy-start | bytes 196612
  24.2 4.0 %copy-start.4 = (s32[8]{0:T(128)S(1)}, s32[8]{0:T(128)}, u32[]{:S(2)}) copy-start(s32[8]{0:T(128)} %mates.7) | copy-start | bytes 100
  25.3 19.7 %copy-start.1 = (bf16[8,3,128,128]{3,2,1,0:T(8,128)(2,1)S(1)}, bf16[8,3,128,128]{3,2,1,0:T(8,128)(2,1)}, u32[]{:S(2)}) copy-start(bf16[8,3,128,128]{3,2,1,0:T(8,128)(2,1)} %weight.7) | copy-start | bytes 2359300
  42.7 1.5 %collective-permute-start.12 = (f32[16,512]{1,0:T(8,128)S(1)}, f32[16,512]{1,0:T(8,128)S(1)}, u32[]{:S(2)}, u32[]{:S(2)}) collective-permute-start(f32[16,512]{1,0:T(8,128)S(1)} %get-tuple-element.38), channel_id=1, source_target_pairs={{2,4},{6,8},{10,12},{14,16},{18,20},{22,24},{26,28},{4,2},{8,6},{1... | collective-permute-start | bytes 98312 | tf_op jit(solution)/shard_map/ppermute | solution.py:52
  43.4 1.7 %collective-permute-start.13 = (f32[16,512]{1,0:T(8,128)S(1)}, f32[16,512]{1,0:T(8,128)S(1)}, u32[]{:S(2)}, u32[]{:S(2)}) collective-permute-start(f32[16,512]{1,0:T(8,128)S(1)} %get-tuple-element.39), channel_id=1, source_target_pairs={{0,2},{2,0},{4,6},{6,4},{8,10},{10,8},{12,14},{14,12},{16,18},{18,... | collective-permute-start | bytes 98312 | tf_op jit(solution)/shard_map/ppermute | solution.py:53
  60.4 1.5 %collective-permute-start.14 = (f32[16,512]{1,0:T(8,128)S(1)}, f32[16,512]{1,0:T(8,128)S(1)}, u32[]{:S(2)}, u32[]{:S(2)}) collective-permute-start(f32[16,512]{1,0:T(8,128)S(1)} %get-tuple-element.45), channel_id=1, source_target_pairs={{2,4},{6,8},{10,12},{14,16},{18,20},{22,24},{26,28},{4,2},{8,6},{1... | collective-permute-start | bytes 98312 | tf_op jit(solution)/shard_map/ppermute | solution.py:52
  61.1 1.7 %collective-permute-start.15 = (f32[16,512]{1,0:T(8,128)S(1)}, f32[16,512]{1,0:T(8,128)S(1)}, u32[]{:S(2)}, u32[]{:S(2)}) collective-permute-start(f32[16,512]{1,0:T(8,128)S(1)} %get-tuple-element.46), channel_id=1, source_target_pairs={{0,2},{2,0},{4,6},{6,4},{8,10},{10,8},{12,14},{14,12},{16,18},{18,... | collective-permute-start | bytes 98312 | tf_op jit(solution)/shard_map/ppermute | solution.py:53
  64.0 4.8 %collective-permute-start.18 = (f32[16,128]{1,0:T(8,128)S(1)}, f32[16,128]{1,0:T(8,128)S(1)}, u32[]{:S(2)}, u32[]{:S(2)}) collective-permute-start(f32[16,128]{1,0:T(8,128)S(1)} %get-tuple-element.49), channel_id=1, source_target_pairs={{0,6},{2,4},{4,2},{6,0},{8,14},{10,12},{12,10},{14,8},{16,22},{18,... | collective-permute-start | bytes 24584 | tf_op jit(solution)/shard_map/ppermute | solution.py:43
  67.5 3.7 %collective-permute-start.17 = (f32[16,128]{1,0:T(8,128)S(1)}, f32[16,128]{1,0:T(8,128)S(1)}, u32[]{:S(2)}, u32[]{:S(2)}) collective-permute-start(f32[16,128]{1,0:T(8,128)S(1)} %get-tuple-element.49), channel_id=1, source_target_pairs={{0,4},{2,6},{4,0},{6,2},{8,12},{10,14},{12,8},{14,10},{16,20},{18,... | collective-permute-start | bytes 24584 | tf_op jit(solution)/shard_map/ppermute | solution.py:43
  67.9 3.3 %collective-permute-start.16 = (f32[16,128]{1,0:T(8,128)S(1)}, f32[16,128]{1,0:T(8,128)S(1)}, u32[]{:S(2)}, u32[]{:S(2)}) collective-permute-start(f32[16,128]{1,0:T(8,128)S(1)} %get-tuple-element.49), channel_id=1, source_target_pairs={{0,2},{2,0},{4,6},{6,4},{8,10},{10,8},{12,14},{14,12},{16,18},{18,... | collective-permute-start | bytes 24584 | tf_op jit(solution)/shard_map/ppermute | solution.py:43
  71.1 5.5 %collective-permute-start.21 = (f32[16,128]{1,0:T(8,128)S(1)}, f32[16,128]{1,0:T(8,128)S(1)}, u32[]{:S(2)}, u32[]{:S(2)}) collective-permute-start(f32[16,128]{1,0:T(8,128)S(1)} %add_add_fusion.refs_0_), channel_id=1, source_target_pairs={{0,24},{2,26},{4,28},{6,30},{8,16},{10,18},{12,20},{14,22},{16,8},... | collective-permute-start | bytes 24584 | tf_op jit(solution)/shard_map/ppermute | solution.py:43
  72.3 4.5 %collective-permute-start.20 = (f32[16,128]{1,0:T(8,128)S(1)}, f32[16,128]{1,0:T(8,128)S(1)}, u32[]{:S(2)}, u32[]{:S(2)}) collective-permute-start(f32[16,128]{1,0:T(8,128)S(1)} %add_add_fusion.refs_0_), channel_id=1, source_target_pairs={{0,16},{2,18},{4,20},{6,22},{8,24},{10,26},{12,28},{14,30},{16,0},... | collective-permute-start | bytes 24584 | tf_op jit(solution)/shard_map/ppermute | solution.py:43
  73.4 3.8 %collective-permute-start.19 = (f32[16,128]{1,0:T(8,128)S(1)}, f32[16,128]{1,0:T(8,128)S(1)}, u32[]{:S(2)}, u32[]{:S(2)}) collective-permute-start(f32[16,128]{1,0:T(8,128)S(1)} %add_add_fusion.refs_0_), channel_id=1, source_target_pairs={{0,8},{2,10},{4,12},{6,14},{8,0},{10,2},{12,4},{14,6},{16,24},{18,... | collective-permute-start | bytes 24584 | tf_op jit(solution)/shard_map/ppermute | solution.py:43

commit v5 on v4

v5 whole, which is shorter than its diff:
```python
import jax
import jax.numpy as jnp
from jax import lax
from jax.experimental import pallas as pl
from jax.experimental.pallas import tpu as pltpu
from jax.sharding import PartitionSpec as P

DAMPING = 2.0 / 3.0
KEEP = 1.0 - DAMPING
EPSILON = 1e-06
EXACT = lax.Precision.HIGHEST
PARTS = 3
VMEM_GRANT = 16 * 1024 * 1024
F32 = jnp.float32
IN_VMEM = pl.BlockSpec(memory_space=pltpu.VMEM)
IN_SMEM = pl.BlockSpec(memory_space=pltpu.SMEM)


def kernel_call(body, outs, scalars, arrays, scratch=(), cost=2_000_000):
    return pl.pallas_call(
        body,
        out_shape=[
            out if isinstance(out, jax.ShapeDtypeStruct) else jax.ShapeDtypeStruct(out, F32)
            for out in outs
        ],
        in_specs=[IN_SMEM] * len(scalars) + [IN_VMEM] * len(arrays),
        out_specs=[IN_VMEM] * len(outs),
        scratch_shapes=list(scratch),
        compiler_params=pltpu.CompilerParams(vmem_limit_bytes=VMEM_GRANT),
        cost_estimate=pl.CostEstimate(flops=cost, bytes_accessed=cost, transcendentals=0),
    )(*scalars, *arrays)


def exchanged(value, axis):
    peers = lax.axis_size(axis)
    return [value] + [
        lax.ppermute(value, axis, [(i, i ^ mask) for i in range(peers)]) for mask in range(1, peers)
    ]


def swapped(value, axis):
    return lax.all_to_all(value, axis, split_axis=0, concat_axis=0, tiled=True)


def across_outer(value, axis):
    peers = lax.axis_size(axis)
    up = [(i, i + 1) for i in range(1, peers - 1, 2)]
    return lax.ppermute(value, axis, up + [(j, i) for i, j in up])


def across_inner(value, axis):
    return lax.ppermute(value, axis, [(i, i ^ 1) for i in range(lax.axis_size(axis))])


def each(count, body):
    if count <= 16:
        for step in range(count):
            body(step)
    else:
        lax.fori_loop(0, count, lambda step, carry: (body(step), carry)[1], 0)


def lanes(block, length):
    start = block * length
    return pl.ds(start if isinstance(block, int) else pl.multiple_of(start, length), length)


def padded(value, rows):
    if value.shape[0] == rows:
        return value
    return jnp.concatenate([value, jnp.zeros((rows - value.shape[0], value.shape[1]), F32)], axis=0)


def in_parts(value):
    pieces = []
    for _ in range(PARTS):
        piece = value.astype(jnp.bfloat16)
        pieces.append(piece)
        value = value - piece.astype(F32)
    return jnp.concatenate(pieces, axis=0)


def fill(field, base, value, length):
    split = in_parts(value)
    for block in range(value.shape[1] // length):
        field[base + block, : split.shape[0], :] = split[:, block * length : (block + 1) * length]


def split(block, blocks):
    if blocks & (blocks - 1):
        return lax.div(block, blocks), lax.rem(block, blocks)
    bits = blocks.bit_length() - 1
    return lax.shift_right_logical(block, bits), lax.bitwise_and(block, blocks - 1)


def parity_of(index):
    return lax.bitwise_and(split(index[0, 0], index.shape[1])[0], 1)


def half(parity, vertices, width, length):
    return pl.ds(pl.multiple_of(parity * (vertices - width), length), width)


def fill_extended(field, parity, outer, own, inner, length):
    margin, blocks = outer.shape[1] // length, own.shape[1] // length
    fill(field, parity * (margin + blocks), outer, length)
    fill(field, margin, own, length)
    fill(field, (1 - parity) * (margin + blocks), inner, length)


def neighbours(index, weight, field, block):
    shift = index.shape[1] // 2 - index[0, 0]
    total = None
    for k in range(index.shape[0]):
        term = lax.dot_general(
            field[index[k, block] + shift],
            weight[block, k],
            (((1,), (1,)), ((), ())),
            preferred_element_type=F32,
        )
        total = term if total is None else total + term
    return total


def folded(total, rows):
    return total[:rows] + total[rows : 2 * rows] + total[2 * rows : PARTS * rows]


def solved(matrix, size):
    row_id = lax.broadcasted_iota(jnp.int32, matrix.shape, 0)
    for k in range(0, size, 2):
        left = jnp.broadcast_to(matrix[:, k : k + 1], matrix.shape)
        right = jnp.broadcast_to(matrix[:, k + 1 : k + 2], matrix.shape)
        upper, lower = matrix[k : k + 1], matrix[k + 1 : k + 2]
        pivot, cross = left[k : k + 1], right[k : k + 1]
        ratio = left[k + 1 : k + 2] / pivot
        new_lower = (lower - ratio * upper) / (right[k + 1 : k + 2] - ratio * cross)
        new_upper = (upper - cross * new_lower) / pivot
        rest = matrix - left * new_upper - right * new_lower
        matrix = jnp.where(row_id == k, new_upper, jnp.where(row_id == k + 1, new_lower, rest))
    return matrix


def local(states, adj_weight, adj_index, partner):
    local_cols, vertices = states.shape
    blocks, _, length, _ = adj_weight.shape
    row_devices, col_devices = lax.axis_size("rows"), lax.axis_size("cols")
    total_cols = local_cols * col_devices
    margin = blocks // 2
    width = margin * length
    rows = -(-local_cols // 16) * 16
    packed_rows = total_cols // 2
    field_shape = (2 * blocks, PARTS * rows, length)
    field = pltpu.VMEM(field_shape, jnp.bfloat16)
    full, edge, line = (rows, vertices), (rows, width), (1, vertices)
    slots = (row_devices, 2 * rows, length)

    def halves(parity):
        return (
            half(parity, vertices, width, length),
            half(1 - parity, vertices, width, length),
        )

    def place(out, mate, value):
        owner, position = split(mate, blocks)
        side = lax.bitwise_and(owner, 1)
        beside = owner + 2 * side - 1
        high = lax.select(position >= margin, 1, 0)
        wanted = (high == side) & (beside >= 0) & (beside < row_devices)
        out[owner, :rows, :] = value
        start = lax.select(wanted, rows, 0)
        target = lax.select(wanted, beside, owner)
        out[target, pl.ds(pl.multiple_of(start, rows), rows), :] = value

    def degree_body(weight, degree):
        ones = jnp.ones((16, length), jnp.bfloat16)

        def one(block):
            total = None
            for k in range(weight.shape[1]):
                term = lax.dot_general(
                    ones,
                    weight[block, k],
                    (((1,), (1,)), ((), ())),
                    preferred_element_type=F32,
                )
                total = term if total is None else total + term
            degree[:, lanes(block, length)] = total[:1]

        each(blocks, one)

    def image_body(index, mates, weight, degree, outer_states, inner_states, states, *refs):
        image, sent, scaled, outer, inner, spread = refs
        parity = parity_of(index)
        at_own_outer, at_own_inner = halves(parity)
        fill_extended(
            spread,
            parity,
            padded(outer_states[:, at_own_inner], rows),
            padded(states[...], rows),
            padded(inner_states[:, at_own_outer], rows),
            length,
        )

        def one(block):
            value = folded(neighbours(index, weight, spread, block), rows)
            at = lanes(block, length)
            image[:, at] = value
            scaled[:, at] = value / degree[:, at]

        each(blocks, one)
        sent[...] = image[:local_cols, :]
        inner[...] = scaled[:, at_own_inner]
        outer[:, :width] = scaled[:, at_own_outer]
        lane = lax.broadcasted_iota(jnp.int32, (rows, length), 1)
        listed = jnp.zeros((rows, length), jnp.int32)
        for block in range(blocks):
            listed = jnp.where(lane == block, mates[block], listed)
        outer[:, width:] = listed.astype(F32)

    def products_body(mates, *refs):
        peers, (image, degree, shared) = refs[:col_devices], refs[col_devices:]
        everyone = jnp.concatenate([peer[...] for peer in peers], axis=0)
        other = jnp.concatenate([everyone * degree[...], image[...]], axis=0)
        products = lax.dot_general(
            everyone,
            padded(other, length),
            (((1,), (1,)), ((), ())),
            precision=EXACT,
            preferred_element_type=F32,
        )
        packed = products[:packed_rows] + pltpu.roll(products[packed_rows:], length // 2, 1)
        for device in range(row_devices):
            shared[device, :packed_rows, :] = packed

        def send_degree(block):
            owner = split(mates[block], blocks)[0]
            shared[owner, packed_rows : packed_rows + 1, :] = degree[:, lanes(block, length)]

        each(blocks, send_degree)

    def ritz_body(index, mates, weight, outer, inner, shared, *refs):
        peers, refs = refs[:col_devices], refs[col_devices:]
        images, refs = refs[:col_devices], refs[col_devices:]
        own_image, scaled, degree, *refs = refs
        out, remain, residual, presmooth, pair_degree, beside, spread_field = refs
        parity = parity_of(index)
        fill_extended(spread_field, parity, outer[:, :width], scaled[...], inner[...], length)

        def offset(block):
            at = lanes(block, length)
            value = folded(neighbours(index, weight, spread_field, block), rows)
            remain[:, at] = KEEP * own_image[:, at] + DAMPING * value

        each(blocks, offset)
        total = shared[0, :packed_rows, :]
        for device in range(1, row_devices):
            total = total + shared[device, :packed_rows, :]
        total = jnp.concatenate([total, pltpu.roll(total, length // 2, 1)], axis=0)
        ritz = jnp.transpose(solved(total, total_cols))[total_cols : total_cols + rows]
        everyone = jnp.concatenate([peer[...] for peer in peers], axis=0)
        spread = jnp.concatenate([image[...] for image in images], axis=0)
        mixed = jnp.dot(ritz, everyone, precision=EXACT, preferred_element_type=F32)
        mixed_image = jnp.dot(ritz, spread, precision=EXACT, preferred_element_type=F32)
        weighted = degree[...] * mixed
        residual[...] = weighted - own_image[...]
        presmooth[...] = DAMPING * (mixed - scaled[...])
        remain[...] = KEEP * weighted + DAMPING * mixed_image - remain[...]

        def one(block):
            at = lanes(block, length)
            place(out, mates[block], remain[:, at])
            other = shared[split(mates[block], blocks)[0], packed_rows : packed_rows + 1, :]
            pair_degree[:, at] = degree[:, at] + other

        each(blocks, one)
        at_outer, _ = halves(parity)
        beside[:, :width] = remain[:, at_outer]
        beside[:, width:] = jnp.zeros((rows, length), F32)
        shared_degree = pair_degree[:, at_outer]
        for block in range(margin):
            beside[block : block + 1, width:] = shared_degree[:, block * length : (block + 1) * length]

    def beside_slot(index, outer_mates, block):
        return split(outer_mates[(1 - parity_of(index)) * margin + block], blocks)[0]

    def coarse_body(
        index, mates, outer_mates, arrived, beside, remain, pair_degree, coarse, fix, further, inner
    ):
        def one(block):
            at = lanes(block, length)
            value = remain[:, at] + arrived[split(mates[block], blocks)[0], :rows, :]
            coarse[:, at] = value
            fix[:, at] = DAMPING * value / pair_degree[:, at]

        def other(block):
            at = lanes(block, length)
            source = beside_slot(index, outer_mates, block)
            value = beside[:, at] + arrived[source, rows:, :]
            further[:rows, at] = DAMPING * value / beside[pl.ds(block, 1), width:]
            further[rows:, at] = value

        each(blocks, one)
        each(margin, other)
        inner[...] = fix[:, halves(parity_of(index))[1]]

    def product_body(
        index, mates, weight, further, inner, fix, degree, presmooth, pair_degree, *refs
    ):
        out, product, outer, spread = refs
        fill_extended(spread, parity_of(index), further[:rows, :], fix[...], inner[...], length)

        def one(block):
            at = lanes(block, length)
            value = degree[:, at] * fix[:, at] - folded(neighbours(index, weight, spread, block), rows)
            product[:, at] = value

        each(blocks, one)
        each(blocks, lambda block: place(out, mates[block], product[:, lanes(block, length)]))
        at_outer, _ = halves(parity_of(index))
        step = DAMPING * product[:, at_outer] / pair_degree[:, at_outer]
        outer[...] = presmooth[:, at_outer] - step

    def fix_body(index, mates, outer_mates, arrived, partial, beside, further, *refs):
        product, coarse, fix, pair_degree, presmooth, second, outer, inner = refs

        def one(block):
            at = lanes(block, length)
            image = product[:, at] + arrived[split(mates[block], blocks)[0], :rows, :]
            step = DAMPING * (coarse[:, at] - image) / pair_degree[:, at]
            second[:, at] = presmooth[:, at] + (fix[:, at] + step)

        def other(block):
            at = lanes(block, length)
            source = beside_slot(index, outer_mates, block)
            image = further[rows:, at] - arrived[source, rows:, :]
            step = DAMPING * image / beside[pl.ds(block, 1), width:]
            outer[:, at] = partial[:, at] + (further[:rows, at] + step)

        each(blocks, one)
        each(margin, other)
        inner[...] = second[:, halves(parity_of(index))[1]]

    def smooth_body(
        index, weight, outer, inner, second, residual, degree, smooth, squares, spread
    ):
        fill_extended(spread, parity_of(index), outer[...], second[...], inner[...], length)

        def one(block):
            at = lanes(block, length)
            value, here = second[:, at], degree[:, at]
            image = here * value - folded(neighbours(index, weight, spread, block), rows)
            smooth[:, at] = value + DAMPING * (residual[:, at] - image) / here

        each(blocks, one)
        value = smooth[...]
        total = jnp.broadcast_to(jnp.sum(value * value, axis=1, keepdims=True), (rows, length))
        lane = lax.broadcasted_iota(jnp.int32, (rows // 2, length), 1)
        packed = jnp.where(lane < length // 2, total[: rows // 2], total[rows // 2 :])
        for device in range(row_devices):
            squares[device] = packed

    def scale_body(squares, smooth, correction):
        total = squares[0]
        for device in range(1, row_devices):
            total = total + squares[device]
        total = jnp.concatenate([total, pltpu.roll(total, length // 2, 1)], axis=0)
        norm = jnp.sqrt(total[:local_cols, :1] / (vertices * row_devices) + EPSILON)
        correction[...] = smooth[:local_cols, :] / norm

    adj_index = adj_index.T
    outer = across_outer(states, "rows")
    inner = across_inner(states, "rows")
    peers = exchanged(states, "cols")
    (degree,) = kernel_call(degree_body, [line], [], [adj_weight])
    image, sent, scaled, outer, inner = kernel_call(
        image_body,
        [full, (local_cols, vertices), full, (rows, width + length), edge],
        [adj_index, partner],
        [adj_weight, degree, outer, inner, states],
        [field],
    )
    (shared,) = kernel_call(
        products_body, [(row_devices, packed_rows + 8, length)], [partner], [*peers, image, degree]
    )
    shared = swapped(shared, "rows")
    outer = across_outer(outer, "rows")
    inner = across_inner(inner, "rows")
    images = exchanged(sent, "cols")
    outer_mates = outer[0, width : width + blocks].astype(jnp.int32)
    out, remain, residual, presmooth, pair_degree, beside = kernel_call(
        ritz_body,
        [slots, full, full, full, line, (rows, width + length)],
        [adj_index, partner],
        [adj_weight, outer, inner, shared, *peers, *images, image, scaled, degree],
        [field],
    )
    arrived = swapped(out, "rows")
    beside = across_outer(beside, "rows")
    coarse, fix, further, inner = kernel_call(
        coarse_body,
        [full, full, (2 * rows, width), edge],
        [adj_index, partner, outer_mates],
        [arrived, beside, remain, pair_degree],
    )
    inner = across_inner(inner, "rows")
    out, product, outer = kernel_call(
        product_body,
        [slots, full, edge],
        [adj_index, partner],
        [adj_weight, further, inner, fix, degree, presmooth, pair_degree],
        [field],
    )
    arrived = swapped(out, "rows")
    outer = across_outer(outer, "rows")
    second, outer, inner = kernel_call(
        fix_body,
        [full, edge, edge],
        [adj_index, partner, outer_mates],
        [arrived, outer, beside, further, product, coarse, fix, pair_degree, presmooth],
    )
    inner = across_inner(inner, "rows")
    smooth, squares = kernel_call(
        smooth_body,
        [full, (row_devices, rows // 2, length)],
        [adj_index],
        [adj_weight, outer, inner, second, residual, degree],
        [field],
    )
    squares = swapped(squares, "rows")
    (correction,) = kernel_call(scale_body, [states.shape], [], [squares, smooth])
    return correction


def solution(mesh):
    return jax.shard_map(
        local,
        mesh=mesh,
        in_specs=(P("cols", "rows"), P("rows", None, None, None), P("rows", None), P("rows")),
        out_specs=P("cols", "rows"),
        check_vma=False,
    )
```

time: 78.3 us -> 73.9 us (0.944)
  blocking collectives: 24.7 us -> 9.58 us
  waiting for transfers between devices: 10.5 us -> 25 us
  starting transfers between devices: 29.8 us -> 25.1 us
  Pallas kernels: 10 us -> 11.7 us
  local copies, waits for them, and re-layouts: 2.75 us -> 1.79 us
    all_to_all x0 -> x3, waiting for transfers between devices: none -> 21.7 us  [swapped(): return lax.all_to_all(value, axis, split_axis=0, concat_axis=0, tiled=True)]
    ppermute x22 -> x10, starting transfers between devices: 29.8 us -> 13 us  [the longest x4 7.82 us: across_inner(): lax.ppermute(value, axis, [(i, i ^ 1) for i in range(lax.axis_size(axis))])]
    all_to_all x2 -> x1, blocking collectives: 24.7 us -> 9.58 us  [swapped(): return lax.all_to_all(value, axis, split_axis=0, concat_axis=0, tiled=True)]
    all_to_all x0 -> x3, starting transfers between devices: none -> 12.1 us  [swapped(): return lax.all_to_all(value, axis, split_axis=0, concat_axis=0, tiled=True)]
    ppermute x22 -> x10, waiting for transfers between devices: 10.5 us -> 3.3 us  [the longest x4 3.27 us: across_inner(): lax.ppermute(value, axis, [(i, i ^ 1) for i in range(lax.axis_size(axis))])]
    pallas_call x8 -> x9, Pallas kernels: 10 us -> 11.7 us  [kernel_call(): pl.pallas_call(body, out_shape=[out if isinstance(out, jax.ShapeDtypeStru...]
    unnamed x14 -> x10, local copies, waits for them, and re-layouts: 2.75 us -> 1.79 us
  transfers between devices with their start and end apart: 22 -> 13, of which waited for: 10 -> 6; matrix products, arithmetic and copies ran while one was open for 1% -> 0% of each run, Pallas kernels for 1% -> 2%
where the time goes in v5:
time: 73.9 us; the launch traced here: 73.3 us
  starting transfers between devices  25.1 us (34%)
  waiting for transfers between devices  25 us (34%)
  Pallas kernels  11.7 us (16%)
  blocking collectives  9.58 us (13%)
  local copies, waits for them, and re-layouts  1.79 us (2%)
    all_to_all x3, waiting for transfers between devices, swapped(): return lax.all_to_all(value, axis, split_axis=0, concat_axis=0, tiled=True)  21.7 us
    all_to_all x3, starting transfers between devices, swapped(): return lax.all_to_all(value, axis, split_axis=0, concat_axis=0, tiled=True)  12.1 us
    pallas_call x9, Pallas kernels, kernel_call(): pl.pallas_call(body, out_shape=[out if isinstance(out, jax.ShapeDtypeStru...  11.7 us
    all_to_all x1, blocking collectives, swapped(): return lax.all_to_all(value, axis, split_axis=0, concat_axis=0, tiled=True)  9.58 us
    ppermute x4, starting transfers between devices, across_inner(): lax.ppermute(value, axis, [(i, i ^ 1) for i in range(lax.axis_size(axis))])  7.82 us
    ppermute x4, waiting for transfers between devices, across_inner(): lax.ppermute(value, axis, [(i, i ^ 1) for i in range(lax.axis_size(axis))])  3.27 us
    ppermute x4, starting transfers between devices, across_outer(): return lax.ppermute(value, axis, up + [(j, i) for i, j in up])  2.63 us
    ppermute x2, starting transfers between devices, exchanged(): lax.ppermute(value, axis, [(i, i ^ mask) for i in range(peers)])  2.58 us
  transfers between devices with their start and end apart: 13, of which 6 were waited for; matrix products, arithmetic and copies ran while one was open for 0% of the time, Pallas kernels for 2%

profile of v5, /device:TPU:0, one launch (start us, length us, event | category | flops | bytes accessed | tf_op | source)
XLA Modules:
  0.0 73.3 jit_solution(8175702058273905028)
XLA Ops:
  0.0 0.7 collective-permute-start
  0.7 4.4 %collective-permute-start.1 = (f32[16,1024]{1,0:T(8,128)}, f32[16,1024]{1,0:T(8,128)S(1)}, u32[]{:S(2)}, u32[]{:S(2)}) collective-permute-start(f32[16,1024]{1,0:T(8,128)} %refs_0_.3), channel_id=1, source_target_pairs={{0,2},{2,0},{4,6},{6,4},{8,10},{10,8},{12,14},{14,12},{16,18},{18,... | collective-permute-start | bytes 196616 | tf_op jit(solution)/shard_map/ppermute | solution.py:52
  5.1 1.5 %collective-permute-start.4 = (f32[16,1024]{1,0:T(8,128)}, f32[16,1024]{1,0:T(8,128)S(1)}, u32[]{:S(2)}, u32[]{:S(2)}) collective-permute-start(f32[16,1024]{1,0:T(8,128)} %refs_0_.3), channel_id=1, source_target_pairs={{0,1},{1,0},{2,3},{3,2},{4,5},{5,4},{6,7},{7,6},{8,9},{9,8},{10,11... | collective-permute-start | bytes 196616 | tf_op jit(solution)/shard_map/ppermute | solution.py:37
  6.6 1.1 %copy-done = bf16[8,3,128,128]{3,2,1,0:T(8,128)(2,1)S(1)} copy-done((bf16[8,3,128,128]{3,2,1,0:T(8,128)(2,1)S(1)}, bf16[8,3,128,128]{3,2,1,0:T(8,128)(2,1)}, u32[]{:S(2)}) %copy-start) | copy-done | bytes 786456
  7.7 0.5 shard_map.46.degree.refs_3_.refs_6_
  8.2 0.3 copy-done.2
  8.5 0.3 copy-done.4
  8.9 1.1 %shard_map.47 = (f32[16,1024]{1,0:T(8,128)S(1)}, f32[16,1024]{1,0:T(8,128)S(1)}, f32[16,1024]{1,0:T(8,128)S(1)}, f32[16,640]{1,0:T(8,128)S(1)}, f32[16,512]{1,0:T(8,128)S(1)}) custom-call(s32[3,8]{1,0:T(4,128)S(1)} %bitcast.3, s32[8]{0:T(128)S(1)} %copy-done.4, bf16[8,3,128,128]{3,2,1,0:T(8,128)(2,1)S(1)} %copy-done, ...), custom_call_target="tpu_custom_call" | custom-call | flops 2000000 | bytes 2000000 | tf_op jit(solution)/shard_map/pallas_call | solution.py:20
  10.0 1.6 %shard_map.48 = f32[16,24,128]{2,1,0:T(8,128)} custom-call(s32[8]{0:T(128)S(1)} %copy-done.4, f32[16,1024]{1,0:T(8,128)S(1)} %copy-done.2, f32[16,1024]{1,0:T(8,128)S(1)} %collective-permute-done.4.refs_1_, f32[16,1024]{1,0:T(8,128)S(1)} %get-tuple-element.30.refs_2_.refs_4_, f32[1,1024]{1,0:T(1,128)S(1)} %shard_map.46.degree.refs_3_.refs_6_), custom_call_target="tpu_custom_call" | custom-call | flops 2000000 | bytes 2000000 | tf_op jit(solution)/shard_map/pallas_call | solution.py:20
  11.6 5.0 %all-to-all-start = ((f32[16,24,128]{2,1,0:T(8,128)}), f32[16,24,128]{2,1,0:T(8,128)S(1)}, u32[]{:S(2)}, u32[]{:S(2)}) async-start(f32[16,24,128]{2,1,0:T(8,128)} %shard_map.48), calls=%async_computation | async-start | bytes 393216 | tf_op jit(solution)/shard_map/all_to_all | solution.py:42
  16.6 1.1 %collective-permute-start.5 = (f32[16,1024]{1,0:T(8,128)S(1)}, f32[16,1024]{1,0:T(8,128)S(1)}, u32[]{:S(2)}, u32[]{:S(2)}) collective-permute-start(f32[16,1024]{1,0:T(8,128)S(1)} %get-tuple-element.31.refs_2_), channel_id=1, source_target_pairs={{0,1},{1,0},{2,3},{3,2},{4,5},{5,4},{6,7},{7,6},{8,9},{9,8},{10,11... | collective-permute-start | bytes 196616 | tf_op jit(solution)/shard_map/ppermute | solution.py:37
  17.7 0.7 collective-permute-start.2
  18.4 3.3 %collective-permute-start.3 = (f32[16,512]{1,0:T(8,128)S(1)}, f32[16,512]{1,0:T(8,128)S(1)}, u32[]{:S(2)}, u32[]{:S(2)}) collective-permute-start(f32[16,512]{1,0:T(8,128)S(1)} %get-tuple-element.29), channel_id=1, source_target_pairs={{0,2},{2,0},{4,6},{6,4},{8,10},{10,8},{12,14},{14,12},{16,18},{18,... | collective-permute-start | bytes 98312 | tf_op jit(solution)/shard_map/ppermute | solution.py:52
  21.6 0.9 %collective-permute-done.3.inner = f32[16,512]{1,0:T(8,128)S(1)} collective-permute-done((f32[16,512]{1,0:T(8,128)S(1)}, f32[16,512]{1,0:T(8,128)S(1)}, u32[]{:S(2)}, u32[]{:S(2)}) %collective-permute-start.3) | collective-permute-done | bytes 32800 | tf_op jit(solution)/shard_map/ppermute | solution.py:52
  22.5 3.1 %all-to-all-done.shared = f32[16,24,128]{2,1,0:T(8,128)S(1)} async-done(((f32[16,24,128]{2,1,0:T(8,128)}), f32[16,24,128]{2,1,0:T(8,128)S(1)}, u32[]{:S(2)}, u32[]{:S(2)}) %all-to-all-start) | async-done | bytes 196640 | tf_op jit(solution)/shard_map/all_to_all | solution.py:42
  25.6 3.4 %shard_map.49 = (f32[16,32,128]{2,1,0:T(8,128)}, f32[16,1024]{1,0:T(8,128)S(1)}, f32[16,1024]{1,0:T(8,128)S(1)}, f32[16,1024]{1,0:T(8,128)S(1)}, f32[1,1024]{1,0:T(1,128)S(1)}, /*index=5*/f32[16,640]{1,0:T(8,128)S(1)}) custom-call(s32[3,8]{1,0:T(4,128)S(1)} %bitcast.4, s32[8]{0:T(128)S(1)} %copy-done.4, bf16[8,3,128,128]{3,2,1,0:T(8,128)(2,1)S(1)} %copy-done.1, ...), custom_call_target="tpu_custom_call" | custom-call | flops 2000000 | bytes 2000000 | tf_op jit(solution)/shard_map/pallas_call | solution.py:20
  29.0 3.5 %all-to-all-start.1 = ((f32[16,32,128]{2,1,0:T(8,128)}), f32[16,32,128]{2,1,0:T(8,128)S(1)}, u32[]{:S(2)}, u32[]{:S(2)}) async-start(f32[16,32,128]{2,1,0:T(8,128)} %get-tuple-element.33), calls=%async_computation.1 | async-start | bytes 524288 | tf_op jit(solution)/shard_map/all_to_all | solution.py:42
  32.6 0.7 collective-permute-start.6
  33.3 9.3 %all-to-all-done.1.arrived = f32[16,32,128]{2,1,0:T(8,128)S(1)} async-done(((f32[16,32,128]{2,1,0:T(8,128)}), f32[16,32,128]{2,1,0:T(8,128)S(1)}, u32[]{:S(2)}, u32[]{:S(2)}) %all-to-all-start.1) | async-done | bytes 262176 | tf_op jit(solution)/shard_map/all_to_all | solution.py:42
  42.5 0.6 shard_map.50
  43.2 0.1 collective-permute-start.7
  43.2 1.2 %collective-permute-done.7.inner = f32[16,512]{1,0:T(8,128)S(1)} collective-permute-done((f32[16,512]{1,0:T(8,128)S(1)}, f32[16,512]{1,0:T(8,128)S(1)}, u32[]{:S(2)}, u32[]{:S(2)}) %collective-permute-start.7) | collective-permute-done | bytes 32800 | tf_op jit(solution)/shard_map/ppermute | solution.py:52
  44.4 1.8 %shard_map.51 = (f32[16,32,128]{2,1,0:T(8,128)}, f32[16,1024]{1,0:T(8,128)S(1)}, f32[16,512]{1,0:T(8,128)S(1)}) custom-call(s32[3,8]{1,0:T(4,128)S(1)} %bitcast.6, s32[8]{0:T(128)S(1)} %copy-done.4, bf16[8,3,128,128]{3,2,1,0:T(8,128)(2,1)S(1)} %copy-done.1, f32[32,512]{1,0:T(8,128)S(1)} %get-tuple-element.37.further, ...), custom_call_target="tpu_custom_call" | custom-call | flops 2000000 | bytes 2000000 | tf_op jit(solution)/shard_map/pallas_call | solution.py:20
  46.3 3.5 %all-to-all-start.2 = ((f32[16,32,128]{2,1,0:T(8,128)}), f32[16,32,128]{2,1,0:T(8,128)S(1)}, u32[]{:S(2)}, u32[]{:S(2)}) async-start(f32[16,32,128]{2,1,0:T(8,128)} %get-tuple-element.41), calls=%async_computation.2 | async-start | bytes 524288 | tf_op jit(solution)/shard_map/all_to_all | solution.py:42
  49.8 0.7 collective-permute-start.8
  50.5 9.3 %all-to-all-done.2.arrived = f32[16,32,128]{2,1,0:T(8,128)S(1)} async-done(((f32[16,32,128]{2,1,0:T(8,128)}), f32[16,32,128]{2,1,0:T(8,128)S(1)}, u32[]{:S(2)}, u32[]{:S(2)}) %all-to-all-start.2) | async-done | bytes 262176 | tf_op jit(solution)/shard_map/all_to_all | solution.py:42
  59.8 0.6 shard_map.52
  60.4 0.1 collective-permute-start.9
  60.5 1.2 %collective-permute-done.9.inner = f32[16,512]{1,0:T(8,128)S(1)} collective-permute-done((f32[16,512]{1,0:T(8,128)S(1)}, f32[16,512]{1,0:T(8,128)S(1)}, u32[]{:S(2)}, u32[]{:S(2)}) %collective-permute-start.9) | collective-permute-done | bytes 32800 | tf_op jit(solution)/shard_map/ppermute | solution.py:52
  61.7 1.2 %shard_map.53 = (f32[16,1024]{1,0:T(8,128)S(1)}, f32[16,8,128]{2,1,0:T(8,128)S(1)}) custom-call(s32[3,8]{1,0:T(4,128)S(1)} %bitcast.8, bf16[8,3,128,128]{3,2,1,0:T(8,128)(2,1)S(1)} %copy-done.1, f32[16,512]{1,0:T(8,128)S(1)} %get-tuple-element.45.outer, f32[16,512]{1,0:T(8,128)S(1)} %collective-permute-done.9.inner, ...), custom_call_target="tpu_custom_call" | custom-call | flops 2000000 | bytes 2000000 | tf_op jit(solution)/shard_map/pallas_call | solution.py:20
  62.9 9.6 %all_to_all.20.squares = f32[16,8,128]{2,1,0:T(8,128)S(1)} all-to-all(f32[16,8,128]{2,1,0:T(8,128)S(1)} %get-tuple-element.49), channel_id=1, replica_groups=mesh['rows'=16,'cols'=2] {'rows'}, dimensions={0} | all-to-all | bytes 131072 | tf_op jit(solution)/shard_map/all_to_all | solution.py:42
  72.5 0.8 %shard_map.54 = f32[16,1024]{1,0:T(8,128)} custom-call(f32[16,8,128]{2,1,0:T(8,128)S(1)} %all_to_all.20.squares, f32[16,1024]{1,0:T(8,128)S(1)} %get-tuple-element.50.smooth), custom_call_target="tpu_custom_call" | custom-call | flops 2000000 | bytes 2000000 | tf_op jit(solution)/shard_map/pallas_call | solution.py:20
  (15 shorter events, 0.1 us)
Async XLA Ops:
  0.0 8.2 %collective-permute-start = (f32[16,1024]{1,0:T(8,128)}, f32[16,1024]{1,0:T(8,128)S(1)}, u32[]{:S(2)}, u32[]{:S(2)}) collective-permute-start(f32[16,1024]{1,0:T(8,128)} %refs_0_.3), channel_id=1, source_target_pairs={{2,4},{6,8},{10,12},{14,16},{18,20},{22,24},{26,28},{4,2},{8,6},{1... | collective-permute-start | bytes 196616 | tf_op jit(solution)/shard_map/ppermute | solution.py:48
  0.7 7.6 %collective-permute-start.1 = (f32[16,1024]{1,0:T(8,128)}, f32[16,1024]{1,0:T(8,128)S(1)}, u32[]{:S(2)}, u32[]{:S(2)}) collective-permute-start(f32[16,1024]{1,0:T(8,128)} %refs_0_.3), channel_id=1, source_target_pairs={{0,2},{2,0},{4,6},{6,4},{8,10},{10,8},{12,14},{14,12},{16,18},{18,... | collective-permute-start | bytes 196616 | tf_op jit(solution)/shard_map/ppermute | solution.py:52
  5.1 5.0 %collective-permute-start.4 = (f32[16,1024]{1,0:T(8,128)}, f32[16,1024]{1,0:T(8,128)S(1)}, u32[]{:S(2)}, u32[]{:S(2)}) collective-permute-start(f32[16,1024]{1,0:T(8,128)} %refs_0_.3), channel_id=1, source_target_pairs={{0,1},{1,0},{2,3},{3,2},{4,5},{5,4},{6,7},{7,6},{8,9},{9,8},{10,11... | collective-permute-start | bytes 196616 | tf_op jit(solution)/shard_map/ppermute | solution.py:37
  6.6 1.1 %copy-start = (bf16[8,3,128,128]{3,2,1,0:T(8,128)(2,1)S(1)}, bf16[8,3,128,128]{3,2,1,0:T(8,128)(2,1)}, u32[]{:S(2)}) copy-start(bf16[8,3,128,128]{3,2,1,0:T(8,128)(2,1)} %weight.9) | copy-start | bytes 2359300
  7.7 0.8 %copy-start.2 = (f32[16,1024]{1,0:T(8,128)S(1)}, f32[16,1024]{1,0:T(8,128)}, u32[]{:S(2)}) copy-start(f32[16,1024]{1,0:T(8,128)} %refs_0_.3) | copy-start | bytes 196612
  7.7 0.8 %copy-start.3 = (s32[8,3]{0,1:T(4,128)S(1)}, s32[8,3]{0,1:T(4,128)}, u32[]{:S(2)}) copy-start(s32[8,3]{0,1:T(4,128)} %param.6) | copy-start | bytes 292
  8.2 0.7 copy-start.4
  8.9 16.7 %copy-start.1 = (bf16[8,3,128,128]{3,2,1,0:T(8,128)(2,1)S(1)}, bf16[8,3,128,128]{3,2,1,0:T(8,128)(2,1)}, u32[]{:S(2)}) copy-start(bf16[8,3,128,128]{3,2,1,0:T(8,128)(2,1)} %weight.9) | copy-start | bytes 2359300
  11.6 14.0 %all-to-all-start = ((f32[16,24,128]{2,1,0:T(8,128)}), f32[16,24,128]{2,1,0:T(8,128)S(1)}, u32[]{:S(2)}, u32[]{:S(2)}) async-start(f32[16,24,128]{2,1,0:T(8,128)} %shard_map.48), calls=%async_computation | async-start | bytes 393216 | tf_op jit(solution)/shard_map/all_to_all | solution.py:42
  16.6 5.9 %collective-permute-start.5 = (f32[16,1024]{1,0:T(8,128)S(1)}, f32[16,1024]{1,0:T(8,128)S(1)}, u32[]{:S(2)}, u32[]{:S(2)}) collective-permute-start(f32[16,1024]{1,0:T(8,128)S(1)} %get-tuple-element.31.refs_2_), channel_id=1, source_target_pairs={{0,1},{1,0},{2,3},{3,2},{4,5},{5,4},{6,7},{7,6},{8,9},{9,8},{10,11... | collective-permute-start | bytes 196616 | tf_op jit(solution)/shard_map/ppermute | solution.py:37
  17.7 4.8 %collective-permute-start.2 = (f32[16,640]{1,0:T(8,128)S(1)}, f32[16,640]{1,0:T(8,128)S(1)}, u32[]{:S(2)}, u32[]{:S(2)}) collective-permute-start(f32[16,640]{1,0:T(8,128)S(1)} %get-tuple-element.28), channel_id=1, source_target_pairs={{2,4},{6,8},{10,12},{14,16},{18,20},{22,24},{26,28},{4,2},{8,6},{1... | collective-permute-start | bytes 122888 | tf_op jit(solution)/shard_map/ppermute | solution.py:48
  18.4 4.1 %collective-permute-start.3 = (f32[16,512]{1,0:T(8,128)S(1)}, f32[16,512]{1,0:T(8,128)S(1)}, u32[]{:S(2)}, u32[]{:S(2)}) collective-permute-start(f32[16,512]{1,0:T(8,128)S(1)} %get-tuple-element.29), channel_id=1, source_target_pairs={{0,2},{2,0},{4,6},{6,4},{8,10},{10,8},{12,14},{14,12},{16,18},{18,... | collective-permute-start | bytes 98312 | tf_op jit(solution)/shard_map/ppermute | solution.py:52
  29.0 13.5 %all-to-all-start.1 = ((f32[16,32,128]{2,1,0:T(8,128)}), f32[16,32,128]{2,1,0:T(8,128)S(1)}, u32[]{:S(2)}, u32[]{:S(2)}) async-start(f32[16,32,128]{2,1,0:T(8,128)} %get-tuple-element.33), calls=%async_computation.1 | async-start | bytes 524288 | tf_op jit(solution)/shard_map/all_to_all | solution.py:42
  32.6 0.7 collective-permute-start.6
  43.2 1.3 %collective-permute-start.7 = (f32[16,512]{1,0:T(8,128)S(1)}, f32[16,512]{1,0:T(8,128)S(1)}, u32[]{:S(2)}, u32[]{:S(2)}) collective-permute-start(f32[16,512]{1,0:T(8,128)S(1)} %get-tuple-element.38), channel_id=1, source_target_pairs={{0,2},{2,0},{4,6},{6,4},{8,10},{10,8},{12,14},{14,12},{16,18},{18,... | collective-permute-start | bytes 98312 | tf_op jit(solution)/shard_map/ppermute | solution.py:52
  46.3 13.5 %all-to-all-start.2 = ((f32[16,32,128]{2,1,0:T(8,128)}), f32[16,32,128]{2,1,0:T(8,128)S(1)}, u32[]{:S(2)}, u32[]{:S(2)}) async-start(f32[16,32,128]{2,1,0:T(8,128)} %get-tuple-element.41), calls=%async_computation.2 | async-start | bytes 524288 | tf_op jit(solution)/shard_map/all_to_all | solution.py:42
  49.8 0.7 collective-permute-start.8
  60.4 1.3 %collective-permute-start.9 = (f32[16,512]{1,0:T(8,128)S(1)}, f32[16,512]{1,0:T(8,128)S(1)}, u32[]{:S(2)}, u32[]{:S(2)}) collective-permute-start(f32[16,512]{1,0:T(8,128)S(1)} %get-tuple-element.46), channel_id=1, source_target_pairs={{0,2},{2,0},{4,6},{6,4},{8,10},{10,8},{12,14},{14,12},{16,18},{18,... | collective-permute-start | bytes 98312 | tf_op jit(solution)/shard_map/ppermute | solution.py:52

commit v6 on v5

--- a/solution.py
+++ b/solution.py
@@ -128,16 +128,30 @@
 
 def solved(matrix, size):
     row_id = lax.broadcasted_iota(jnp.int32, matrix.shape, 0)
-    for k in range(0, size, 2):
-        left = jnp.broadcast_to(matrix[:, k : k + 1], matrix.shape)
-        right = jnp.broadcast_to(matrix[:, k + 1 : k + 2], matrix.shape)
-        upper, lower = matrix[k : k + 1], matrix[k + 1 : k + 2]
-        pivot, cross = left[k : k + 1], right[k : k + 1]
-        ratio = left[k + 1 : k + 2] / pivot
-        new_lower = (lower - ratio * upper) / (right[k + 1 : k + 2] - ratio * cross)
-        new_upper = (upper - cross * new_lower) / pivot
-        rest = matrix - left * new_upper - right * new_lower
-        matrix = jnp.where(row_id == k, new_upper, jnp.where(row_id == k + 1, new_lower, rest))
+    step = 8 if size % 8 == 0 else 1
+    for base in range(0, size, step):
+        ids = range(step)
+        columns = [
+            jnp.broadcast_to(matrix[:, base + j : base + j + 1], matrix.shape) for j in ids
+        ]
+        block = [[columns[j][base + i : base + i + 1] for j in ids] for i in ids]
+        lines = [matrix[base + i : base + i + 1] for i in ids]
+        for i in ids:
+            scale = 1.0 / block[i][i]
+            lines[i] = lines[i] * scale
+            for j in range(i + 1, step):
+                block[i][j] = block[i][j] * scale
+            for other in ids:
+                if other == i:
+                    continue
+                factor = block[other][i]
+                lines[other] = lines[other] - factor * lines[i]
+                for j in range(i + 1, step):
+                    block[other][j] = block[other][j] - factor * block[i][j]
+        for j in ids:
+            matrix = matrix - columns[j] * lines[j]
+        for j in ids:
+            matrix = jnp.where(row_id == base + j, lines[j], matrix)
     return matrix
 
 
@@ -153,7 +167,7 @@
     field_shape = (2 * blocks, PARTS * rows, length)
     field = pltpu.VMEM(field_shape, jnp.bfloat16)
     full, edge, line = (rows, vertices), (rows, width), (1, vertices)
-    slots = (row_devices, 2 * rows, length)
+    slots = (2 * row_devices, rows, length)
 
     def halves(parity):
         return (
@@ -167,25 +181,25 @@
         beside = owner + 2 * side - 1
         high = lax.select(position >= margin, 1, 0)
         wanted = (high == side) & (beside >= 0) & (beside < row_devices)
-        out[owner, :rows, :] = value
-        start = lax.select(wanted, rows, 0)
-        target = lax.select(wanted, beside, owner)
-        out[target, pl.ds(pl.multiple_of(start, rows), rows), :] = value
-
-    def degree_body(weight, degree):
-        ones = jnp.ones((16, length), jnp.bfloat16)
-
+        out[2 * owner] = value
+        out[lax.select(wanted, 2 * beside + 1, 2 * owner)] = value
+
+    def ones_body(ones):
+        ones[...] = jnp.ones(ones.shape, ones.dtype)
+
+    def degree_body(ones, weight, degree, degrees):
         def one(block):
             total = None
             for k in range(weight.shape[1]):
                 term = lax.dot_general(
-                    ones,
+                    ones[...],
                     weight[block, k],
                     (((1,), (1,)), ((), ())),
                     preferred_element_type=F32,
                 )
                 total = term if total is None else total + term
             degree[:, lanes(block, length)] = total[:1]
+            degrees[pl.ds(block, 1), :] = total[:1]
 
         each(blocks, one)
 
@@ -218,26 +232,22 @@
             listed = jnp.where(lane == block, mates[block], listed)
         outer[:, width:] = listed.astype(F32)
 
-    def products_body(mates, *refs):
-        peers, (image, degree, shared) = refs[:col_devices], refs[col_devices:]
+    def products_body(*refs):
+        peers, (image, degree, degrees, shared, wide) = refs[:col_devices], refs[col_devices:]
         everyone = jnp.concatenate([peer[...] for peer in peers], axis=0)
         other = jnp.concatenate([everyone * degree[...], image[...]], axis=0)
-        products = lax.dot_general(
+        wide[...] = jnp.zeros(wide.shape, F32)
+        wide[:, : total_cols + rows] = lax.dot_general(
             everyone,
-            padded(other, length),
+            other,
             (((1,), (1,)), ((), ())),
             precision=EXACT,
             preferred_element_type=F32,
         )
-        packed = products[:packed_rows] + pltpu.roll(products[packed_rows:], length // 2, 1)
+        packed = wide[:packed_rows, :] + pltpu.roll(wide[packed_rows:, :], length // 2, 1)
         for device in range(row_devices):
             shared[device, :packed_rows, :] = packed
-
-        def send_degree(block):
-            owner = split(mates[block], blocks)[0]
-            shared[owner, packed_rows : packed_rows + 1, :] = degree[:, lanes(block, length)]
-
-        each(blocks, send_degree)
+            shared[device, packed_rows:, :] = degrees[...]
 
     def ritz_body(index, mates, weight, outer, inner, shared, *refs):
         peers, refs = refs[:col_devices], refs[col_devices:]
@@ -270,8 +280,8 @@
         def one(block):
             at = lanes(block, length)
             place(out, mates[block], remain[:, at])
-            other = shared[split(mates[block], blocks)[0], packed_rows : packed_rows + 1, :]
-            pair_degree[:, at] = degree[:, at] + other
+            owner, position = split(mates[block], blocks)
+            pair_degree[:, at] = degree[:, at] + shared[owner, pl.ds(packed_rows + position, 1), :]
 
         each(blocks, one)
         at_outer, _ = halves(parity)
@@ -289,14 +299,14 @@
     ):
         def one(block):
             at = lanes(block, length)
-            value = remain[:, at] + arrived[split(mates[block], blocks)[0], :rows, :]
+            value = remain[:, at] + arrived[2 * split(mates[block], blocks)[0]]
             coarse[:, at] = value
             fix[:, at] = DAMPING * value / pair_degree[:, at]
 
         def other(block):
             at = lanes(block, length)
             source = beside_slot(index, outer_mates, block)
-            value = beside[:, at] + arrived[source, rows:, :]
+            value = beside[:, at] + arrived[2 * source + 1]
             further[:rows, at] = DAMPING * value / beside[pl.ds(block, 1), width:]
             further[rows:, at] = value
 
@@ -326,14 +336,14 @@
 
         def one(block):
             at = lanes(block, length)
-            image = product[:, at] + arrived[split(mates[block], blocks)[0], :rows, :]
+            image = product[:, at] + arrived[2 * split(mates[block], blocks)[0]]
             step = DAMPING * (coarse[:, at] - image) / pair_degree[:, at]
             second[:, at] = presmooth[:, at] + (fix[:, at] + step)
 
         def other(block):
             at = lanes(block, length)
             source = beside_slot(index, outer_mates, block)
-            image = further[rows:, at] - arrived[source, rows:, :]
+            image = further[rows:, at] - arrived[2 * source + 1]
             step = DAMPING * image / beside[pl.ds(block, 1), width:]
             outer[:, at] = partial[:, at] + (further[:rows, at] + step)
 
@@ -372,7 +382,9 @@
     outer = across_outer(states, "rows")
     inner = across_inner(states, "rows")
     peers = exchanged(states, "cols")
-    (degree,) = kernel_call(degree_body, [line], [], [adj_weight])
+    ones_shape = jax.ShapeDtypeStruct((16, length), jnp.bfloat16)
+    (ones,) = kernel_call(ones_body, [ones_shape], [], [], cost=20_000_000_000)
+    degree, degrees = kernel_call(degree_body, [line, (blocks, length)], [], [ones, adj_weight])
     image, sent, scaled, outer, inner = kernel_call(
         image_body,
         [full, (local_cols, vertices), full, (rows, width + length), edge],
@@ -381,7 +393,11 @@
         [field],
     )
     (shared,) = kernel_call(
-        products_body, [(row_devices, packed_rows + 8, length)], [partner], [*peers, image, degree]
+        products_body,
+        [(row_devices, packed_rows + blocks, length)],
+        [],
+        [*peers, image, degree, degrees],
+        [pltpu.VMEM((total_cols, length), F32)],
     )
     shared = swapped(shared, "rows")
     outer = across_outer(outer, "rows")

time: 73.9 us -> 73 us (0.988)
  starting transfers between devices: 25.1 us -> 26.5 us
  Pallas kernels: 11.7 us -> 10.4 us
  local copies, waits for them, and re-layouts: 1.79 us -> 0.68 us
    pallas_call x9 -> x10, Pallas kernels: 11.7 us -> 10.4 us  [kernel_call(): pl.pallas_call(body, out_shape=[out if isinstance(out, jax.ShapeDtypeStru...]
    unnamed x10 -> x8, local copies, waits for them, and re-layouts: 1.79 us -> 0.68 us
    all_to_all x3, starting transfers between devices: 12.1 us -> 12.9 us  [swapped(): return lax.all_to_all(value, axis, split_axis=0, concat_axis=0, tiled=True)]
  transfers between devices with their start and end apart: 13 -> 13, of which waited for: 6 -> 7; matrix products, arithmetic and copies ran while one was open for 0% -> 0% of each run, Pallas kernels for 2% -> 2%
where the time goes in v6:
time: 73 us; the launch traced here: 72.4 us
  starting transfers between devices  26.5 us (36%)
  waiting for transfers between devices  25.1 us (34%)
  Pallas kernels  10.4 us (14%)
  blocking collectives  9.58 us (13%)
    all_to_all x3, waiting for transfers between devices, swapped(): return lax.all_to_all(value, axis, split_axis=0, concat_axis=0, tiled=True)  21.2 us
    all_to_all x3, starting transfers between devices, swapped(): return lax.all_to_all(value, axis, split_axis=0, concat_axis=0, tiled=True)  12.9 us
    pallas_call x10, Pallas kernels, kernel_call(): pl.pallas_call(body, out_shape=[out if isinstance(out, jax.ShapeDtypeStru...  10.4 us
    all_to_all x1, blocking collectives, swapped(): return lax.all_to_all(value, axis, split_axis=0, concat_axis=0, tiled=True)  9.58 us
    ppermute x4, starting transfers between devices, across_inner(): lax.ppermute(value, axis, [(i, i ^ 1) for i in range(lax.axis_size(axis))])  7.82 us
    ppermute x4, waiting for transfers between devices, across_inner(): lax.ppermute(value, axis, [(i, i ^ 1) for i in range(lax.axis_size(axis))])  3.27 us
    ppermute x2, starting transfers between devices, exchanged(): lax.ppermute(value, axis, [(i, i ^ mask) for i in range(peers)])  3.1 us
    ppermute x4, starting transfers between devices, across_outer(): return lax.ppermute(value, axis, up + [(j, i) for i, j in up])  2.76 us
  transfers between devices with their start and end apart: 13, of which 7 were waited for; matrix products, arithmetic and copies ran while one was open for 0% of the time, Pallas kernels for 2%

profile of v6, /device:TPU:0, one launch (start us, length us, event | category | flops | bytes accessed | tf_op | source)
XLA Modules:
  0.0 72.4 jit_solution(5186850580803703247)
XLA Ops:
  0.0 0.8 %collective-permute-start = (f32[16,1024]{1,0:T(8,128)}, f32[16,1024]{1,0:T(8,128)S(1)}, u32[]{:S(2)}, u32[]{:S(2)}) collective-permute-start(f32[16,1024]{1,0:T(8,128)} %refs_0_.3), channel_id=1, source_target_pairs={{2,4},{6,8},{10,12},{14,16},{18,20},{22,24},{26,28},{4,2},{8,6},{1... | collective-permute-start | bytes 196616 | tf_op jit(solution)/shard_map/ppermute | solution.py:48
  0.8 4.4 %collective-permute-start.1 = (f32[16,1024]{1,0:T(8,128)}, f32[16,1024]{1,0:T(8,128)S(1)}, u32[]{:S(2)}, u32[]{:S(2)}) collective-permute-start(f32[16,1024]{1,0:T(8,128)} %refs_0_.3), channel_id=1, source_target_pairs={{0,2},{2,0},{4,6},{6,4},{8,10},{10,8},{12,14},{14,12},{16,18},{18,... | collective-permute-start | bytes 196616 | tf_op jit(solution)/shard_map/ppermute | solution.py:52
  5.2 1.5 %collective-permute-start.4 = (f32[16,1024]{1,0:T(8,128)}, f32[16,1024]{1,0:T(8,128)S(1)}, u32[]{:S(2)}, u32[]{:S(2)}) collective-permute-start(f32[16,1024]{1,0:T(8,128)} %refs_0_.3), channel_id=1, source_target_pairs={{0,1},{1,0},{2,3},{3,2},{4,5},{5,4},{6,7},{7,6},{8,9},{9,8},{10,11... | collective-permute-start | bytes 196616 | tf_op jit(solution)/shard_map/ppermute | solution.py:37
  6.7 0.5 shard_map.47
  7.3 0.3 copy-done.1
  7.6 0.3 copy-done.2
  7.9 1.1 %shard_map.48 = (f32[16,1024]{1,0:T(8,128)S(1)}, f32[16,1024]{1,0:T(8,128)S(1)}, f32[16,1024]{1,0:T(8,128)S(1)}, f32[16,640]{1,0:T(8,128)S(1)}, f32[16,512]{1,0:T(8,128)S(1)}) custom-call(s32[3,8]{1,0:T(4,128)S(1)} %bitcast.3, s32[8]{0:T(128)S(1)} %copy-done.3, bf16[8,3,128,128]{3,2,1,0:T(8,128)(2,1)S(1)} %copy-done, ...), custom_call_target="tpu_custom_call" | custom-call | flops 2000000 | bytes 2000000 | tf_op jit(solution)/shard_map/pallas_call | solution.py:20
  9.0 0.6 collective-permute-done.4.refs_1_
  9.7 1.1 %shard_map.49 = f32[16,24,128]{2,1,0:T(8,128)} custom-call(f32[16,1024]{1,0:T(8,128)S(1)} %copy-done.1, f32[16,1024]{1,0:T(8,128)S(1)} %collective-permute-done.4.refs_1_, f32[16,1024]{1,0:T(8,128)S(1)} %get-tuple-element.33.refs_2_.refs_4_, f32[1,1024]{1,0:T(1,128)S(1)} %get-tuple-element.30.degree.refs_3_.refs_6_, f32[8,128]{1,0:T(8,128)S(1)} %get-tuple-element.34.refs_4_), custom_call_target="tpu_custom_call" | custom-call | flops 2000000 | bytes 2000000 | tf_op jit(solution)/shard_map/pallas_call | solution.py:20
  10.7 5.4 %all-to-all-start = ((f32[16,24,128]{2,1,0:T(8,128)}), f32[16,24,128]{2,1,0:T(8,128)S(1)}, u32[]{:S(2)}, u32[]{:S(2)}) async-start(f32[16,24,128]{2,1,0:T(8,128)} %shard_map.49), calls=%async_computation | async-start | bytes 393216 | tf_op jit(solution)/shard_map/all_to_all | solution.py:42
  16.2 1.6 %collective-permute-start.5 = (f32[16,1024]{1,0:T(8,128)S(1)}, f32[16,1024]{1,0:T(8,128)S(1)}, u32[]{:S(2)}, u32[]{:S(2)}) collective-permute-start(f32[16,1024]{1,0:T(8,128)S(1)} %get-tuple-element.35.refs_2_), channel_id=1, source_target_pairs={{0,1},{1,0},{2,3},{3,2},{4,5},{5,4},{6,7},{7,6},{8,9},{9,8},{10,11... | collective-permute-start | bytes 196616 | tf_op jit(solution)/shard_map/ppermute | solution.py:37
  17.8 0.7 collective-permute-start.2
  18.4 3.3 %collective-permute-start.3 = (f32[16,512]{1,0:T(8,128)S(1)}, f32[16,512]{1,0:T(8,128)S(1)}, u32[]{:S(2)}, u32[]{:S(2)}) collective-permute-start(f32[16,512]{1,0:T(8,128)S(1)} %get-tuple-element.32), channel_id=1, source_target_pairs={{0,2},{2,0},{4,6},{6,4},{8,10},{10,8},{12,14},{14,12},{16,18},{18,... | collective-permute-start | bytes 98312 | tf_op jit(solution)/shard_map/ppermute | solution.py:52
  21.7 0.9 %collective-permute-done.3.inner = f32[16,512]{1,0:T(8,128)S(1)} collective-permute-done((f32[16,512]{1,0:T(8,128)S(1)}, f32[16,512]{1,0:T(8,128)S(1)}, u32[]{:S(2)}, u32[]{:S(2)}) %collective-permute-start.3) | collective-permute-done | bytes 32800 | tf_op jit(solution)/shard_map/ppermute | solution.py:52
  22.6 2.6 %all-to-all-done.shared = f32[16,24,128]{2,1,0:T(8,128)S(1)} async-done(((f32[16,24,128]{2,1,0:T(8,128)}), f32[16,24,128]{2,1,0:T(8,128)S(1)}, u32[]{:S(2)}, u32[]{:S(2)}) %all-to-all-start) | async-done | bytes 196640 | tf_op jit(solution)/shard_map/all_to_all | solution.py:42
  25.1 2.6 %shard_map.50 = (f32[32,16,128]{2,1,0:T(8,128)}, f32[16,1024]{1,0:T(8,128)S(1)}, f32[16,1024]{1,0:T(8,128)S(1)}, f32[16,1024]{1,0:T(8,128)S(1)}, f32[1,1024]{1,0:T(1,128)S(1)}, /*index=5*/f32[16,640]{1,0:T(8,128)S(1)}) custom-call(s32[3,8]{1,0:T(4,128)S(1)} %bitcast.4, s32[8]{0:T(128)S(1)} %copy-done.3, bf16[8,3,128,128]{3,2,1,0:T(8,128)(2,1)S(1)} %copy-done, ...), custom_call_target="tpu_custom_call" | custom-call | flops 2000000 | bytes 2000000 | tf_op jit(solution)/shard_map/pallas_call | solution.py:20
  27.8 3.9 %all-to-all-start.1 = ((f32[32,16,128]{2,1,0:T(8,128)}), f32[32,16,128]{2,1,0:T(8,128)S(1)}, u32[]{:S(2)}, u32[]{:S(2)}) async-start(f32[32,16,128]{2,1,0:T(8,128)} %get-tuple-element.37), calls=%async_computation.1 | async-start | bytes 524288 | tf_op jit(solution)/shard_map/all_to_all | solution.py:42
  31.7 0.7 collective-permute-start.6
  32.4 9.3 %all-to-all-done.1.arrived = f32[32,16,128]{2,1,0:T(8,128)S(1)} async-done(((f32[32,16,128]{2,1,0:T(8,128)}), f32[32,16,128]{2,1,0:T(8,128)S(1)}, u32[]{:S(2)}, u32[]{:S(2)}) %all-to-all-start.1) | async-done | bytes 262176 | tf_op jit(solution)/shard_map/all_to_all | solution.py:42
  41.7 0.6 shard_map.51
  42.3 0.1 collective-permute-start.7
  42.4 1.2 %collective-permute-done.7.inner = f32[16,512]{1,0:T(8,128)S(1)} collective-permute-done((f32[16,512]{1,0:T(8,128)S(1)}, f32[16,512]{1,0:T(8,128)S(1)}, u32[]{:S(2)}, u32[]{:S(2)}) %collective-permute-start.7) | collective-permute-done | bytes 32800 | tf_op jit(solution)/shard_map/ppermute | solution.py:52
  43.6 1.8 %shard_map.52 = (f32[32,16,128]{2,1,0:T(8,128)}, f32[16,1024]{1,0:T(8,128)S(1)}, f32[16,512]{1,0:T(8,128)S(1)}) custom-call(s32[3,8]{1,0:T(4,128)S(1)} %bitcast.6, s32[8]{0:T(128)S(1)} %copy-done.3, bf16[8,3,128,128]{3,2,1,0:T(8,128)(2,1)S(1)} %copy-done, f32[32,512]{1,0:T(8,128)S(1)} %get-tuple-element.41.further, ...), custom_call_target="tpu_custom_call" | custom-call | flops 2000000 | bytes 2000000 | tf_op jit(solution)/shard_map/pallas_call | solution.py:20
  45.4 3.5 %all-to-all-start.2 = ((f32[32,16,128]{2,1,0:T(8,128)}), f32[32,16,128]{2,1,0:T(8,128)S(1)}, u32[]{:S(2)}, u32[]{:S(2)}) async-start(f32[32,16,128]{2,1,0:T(8,128)} %get-tuple-element.45), calls=%async_computation.2 | async-start | bytes 524288 | tf_op jit(solution)/shard_map/all_to_all | solution.py:42
  49.0 0.7 collective-permute-start.8
  49.6 9.3 %all-to-all-done.2.arrived = f32[32,16,128]{2,1,0:T(8,128)S(1)} async-done(((f32[32,16,128]{2,1,0:T(8,128)}), f32[32,16,128]{2,1,0:T(8,128)S(1)}, u32[]{:S(2)}, u32[]{:S(2)}) %all-to-all-start.2) | async-done | bytes 262176 | tf_op jit(solution)/shard_map/all_to_all | solution.py:42
  58.9 0.6 shard_map.53
  59.5 0.1 collective-permute-start.9
  59.6 1.2 %collective-permute-done.9.inner = f32[16,512]{1,0:T(8,128)S(1)} collective-permute-done((f32[16,512]{1,0:T(8,128)S(1)}, f32[16,512]{1,0:T(8,128)S(1)}, u32[]{:S(2)}, u32[]{:S(2)}) %collective-permute-start.9) | collective-permute-done | bytes 32800 | tf_op jit(solution)/shard_map/ppermute | solution.py:52
  60.8 1.2 %shard_map.54 = (f32[16,1024]{1,0:T(8,128)S(1)}, f32[16,8,128]{2,1,0:T(8,128)S(1)}) custom-call(s32[3,8]{1,0:T(4,128)S(1)} %bitcast.8, bf16[8,3,128,128]{3,2,1,0:T(8,128)(2,1)S(1)} %copy-done, f32[16,512]{1,0:T(8,128)S(1)} %get-tuple-element.49.outer, f32[16,512]{1,0:T(8,128)S(1)} %collective-permute-done.9.inner, f32[16,1024]{1,0:T(8,128)S(1)} %get-tuple-element.51.second, ...), custom_call_target="tpu_custom_call" | custom-call | flops 2000000 | bytes 2000000 | tf_op jit(solution)/shard_map/pallas_call | solution.py:20
  62.0 9.6 %all_to_all.20.squares = f32[16,8,128]{2,1,0:T(8,128)S(1)} all-to-all(f32[16,8,128]{2,1,0:T(8,128)S(1)} %get-tuple-element.53), channel_id=1, replica_groups=mesh['rows'=16,'cols'=2] {'rows'}, dimensions={0} | all-to-all | bytes 131072 | tf_op jit(solution)/shard_map/all_to_all | solution.py:42
  71.6 0.8 %shard_map.55 = f32[16,1024]{1,0:T(8,128)} custom-call(f32[16,8,128]{2,1,0:T(8,128)S(1)} %all_to_all.20.squares, f32[16,1024]{1,0:T(8,128)S(1)} %get-tuple-element.54.smooth), custom_call_target="tpu_custom_call" | custom-call | flops 2000000 | bytes 2000000 | tf_op jit(solution)/shard_map/pallas_call | solution.py:20
  (14 shorter events, 0.1 us)
Async XLA Ops:
  0.0 6.7 %copy-start = (bf16[8,3,128,128]{3,2,1,0:T(8,128)(2,1)S(1)}, bf16[8,3,128,128]{3,2,1,0:T(8,128)(2,1)}, u32[]{:S(2)}) copy-start(bf16[8,3,128,128]{3,2,1,0:T(8,128)(2,1)} %weight.9) | copy-start | bytes 2359300
  0.0 7.2 %collective-permute-start = (f32[16,1024]{1,0:T(8,128)}, f32[16,1024]{1,0:T(8,128)S(1)}, u32[]{:S(2)}, u32[]{:S(2)}) collective-permute-start(f32[16,1024]{1,0:T(8,128)} %refs_0_.3), channel_id=1, source_target_pairs={{2,4},{6,8},{10,12},{14,16},{18,20},{22,24},{26,28},{4,2},{8,6},{1... | collective-permute-start | bytes 196616 | tf_op jit(solution)/shard_map/ppermute | solution.py:48
  0.8 6.4 %collective-permute-start.1 = (f32[16,1024]{1,0:T(8,128)}, f32[16,1024]{1,0:T(8,128)S(1)}, u32[]{:S(2)}, u32[]{:S(2)}) collective-permute-start(f32[16,1024]{1,0:T(8,128)} %refs_0_.3), channel_id=1, source_target_pairs={{0,2},{2,0},{4,6},{6,4},{8,10},{10,8},{12,14},{14,12},{16,18},{18,... | collective-permute-start | bytes 196616 | tf_op jit(solution)/shard_map/ppermute | solution.py:52
  5.2 4.5 %collective-permute-start.4 = (f32[16,1024]{1,0:T(8,128)}, f32[16,1024]{1,0:T(8,128)S(1)}, u32[]{:S(2)}, u32[]{:S(2)}) collective-permute-start(f32[16,1024]{1,0:T(8,128)} %refs_0_.3), channel_id=1, source_target_pairs={{0,1},{1,0},{2,3},{3,2},{4,5},{5,4},{6,7},{7,6},{8,9},{9,8},{10,11... | collective-permute-start | bytes 196616 | tf_op jit(solution)/shard_map/ppermute | solution.py:37
  6.7 0.9 %copy-start.1 = (f32[16,1024]{1,0:T(8,128)S(1)}, f32[16,1024]{1,0:T(8,128)}, u32[]{:S(2)}) copy-start(f32[16,1024]{1,0:T(8,128)} %refs_0_.3) | copy-start | bytes 196612
  7.2 0.7 copy-start.2
  7.2 0.7 copy-start.3
  10.7 14.4 %all-to-all-start = ((f32[16,24,128]{2,1,0:T(8,128)}), f32[16,24,128]{2,1,0:T(8,128)S(1)}, u32[]{:S(2)}, u32[]{:S(2)}) async-start(f32[16,24,128]{2,1,0:T(8,128)} %shard_map.49), calls=%async_computation | async-start | bytes 393216 | tf_op jit(solution)/shard_map/all_to_all | solution.py:42
  16.2 6.4 %collective-permute-start.5 = (f32[16,1024]{1,0:T(8,128)S(1)}, f32[16,1024]{1,0:T(8,128)S(1)}, u32[]{:S(2)}, u32[]{:S(2)}) collective-permute-start(f32[16,1024]{1,0:T(8,128)S(1)} %get-tuple-element.35.refs_2_), channel_id=1, source_target_pairs={{0,1},{1,0},{2,3},{3,2},{4,5},{5,4},{6,7},{7,6},{8,9},{9,8},{10,11... | collective-permute-start | bytes 196616 | tf_op jit(solution)/shard_map/ppermute | solution.py:37
  17.8 4.8 %collective-permute-start.2 = (f32[16,640]{1,0:T(8,128)S(1)}, f32[16,640]{1,0:T(8,128)S(1)}, u32[]{:S(2)}, u32[]{:S(2)}) collective-permute-start(f32[16,640]{1,0:T(8,128)S(1)} %get-tuple-element.31), channel_id=1, source_target_pairs={{2,4},{6,8},{10,12},{14,16},{18,20},{22,24},{26,28},{4,2},{8,6},{1... | collective-permute-start | bytes 122888 | tf_op jit(solution)/shard_map/ppermute | solution.py:48
  18.4 4.1 %collective-permute-start.3 = (f32[16,512]{1,0:T(8,128)S(1)}, f32[16,512]{1,0:T(8,128)S(1)}, u32[]{:S(2)}, u32[]{:S(2)}) collective-permute-start(f32[16,512]{1,0:T(8,128)S(1)} %get-tuple-element.32), channel_id=1, source_target_pairs={{0,2},{2,0},{4,6},{6,4},{8,10},{10,8},{12,14},{14,12},{16,18},{18,... | collective-permute-start | bytes 98312 | tf_op jit(solution)/shard_map/ppermute | solution.py:52
  27.8 13.9 %all-to-all-start.1 = ((f32[32,16,128]{2,1,0:T(8,128)}), f32[32,16,128]{2,1,0:T(8,128)S(1)}, u32[]{:S(2)}, u32[]{:S(2)}) async-start(f32[32,16,128]{2,1,0:T(8,128)} %get-tuple-element.37), calls=%async_computation.1 | async-start | bytes 524288 | tf_op jit(solution)/shard_map/all_to_all | solution.py:42
  31.7 0.7 collective-permute-start.6
  42.3 1.3 %collective-permute-start.7 = (f32[16,512]{1,0:T(8,128)S(1)}, f32[16,512]{1,0:T(8,128)S(1)}, u32[]{:S(2)}, u32[]{:S(2)}) collective-permute-start(f32[16,512]{1,0:T(8,128)S(1)} %get-tuple-element.42), channel_id=1, source_target_pairs={{0,2},{2,0},{4,6},{6,4},{8,10},{10,8},{12,14},{14,12},{16,18},{18,... | collective-permute-start | bytes 98312 | tf_op jit(solution)/shard_map/ppermute | solution.py:52
  45.4 13.5 %all-to-all-start.2 = ((f32[32,16,128]{2,1,0:T(8,128)}), f32[32,16,128]{2,1,0:T(8,128)S(1)}, u32[]{:S(2)}, u32[]{:S(2)}) async-start(f32[32,16,128]{2,1,0:T(8,128)} %get-tuple-element.45), calls=%async_computation.2 | async-start | bytes 524288 | tf_op jit(solution)/shard_map/all_to_all | solution.py:42
  49.0 0.7 collective-permute-start.8
  59.5 1.3 %collective-permute-start.9 = (f32[16,512]{1,0:T(8,128)S(1)}, f32[16,512]{1,0:T(8,128)S(1)}, u32[]{:S(2)}, u32[]{:S(2)}) collective-permute-start(f32[16,512]{1,0:T(8,128)S(1)} %get-tuple-element.50), channel_id=1, source_target_pairs={{0,2},{2,0},{4,6},{6,4},{8,10},{10,8},{12,14},{14,12},{16,18},{18,... | collective-permute-start | bytes 98312 | tf_op jit(solution)/shard_map/ppermute | solution.py:52

commit v7 on v6

--- a/solution.py
+++ b/solution.py
@@ -187,7 +187,7 @@
     def ones_body(ones):
         ones[...] = jnp.ones(ones.shape, ones.dtype)
 
-    def degree_body(ones, weight, degree, degrees):
+    def degree_body(ones, weight, index, mates, degree, degrees):
         def one(block):
             total = None
             for k in range(weight.shape[1]):
@@ -249,7 +249,14 @@
             shared[device, :packed_rows, :] = packed
             shared[device, packed_rows:, :] = degrees[...]
 
-    def ritz_body(index, mates, weight, outer, inner, shared, *refs):
+    def solve_body(shared, ritz):
+        total = shared[0, :packed_rows, :]
+        for device in range(1, row_devices):
+            total = total + shared[device, :packed_rows, :]
+        total = jnp.concatenate([total, pltpu.roll(total, length // 2, 1)], axis=0)
+        ritz[...] = jnp.transpose(solved(total, total_cols))[total_cols : total_cols + rows]
+
+    def remain_body(index, mates, weight, outer, inner, shared, ritz, *refs):
         peers, refs = refs[:col_devices], refs[col_devices:]
         images, refs = refs[:col_devices], refs[col_devices:]
         own_image, scaled, degree, *refs = refs
@@ -263,15 +270,10 @@
             remain[:, at] = KEEP * own_image[:, at] + DAMPING * value
 
         each(blocks, offset)
-        total = shared[0, :packed_rows, :]
-        for device in range(1, row_devices):
-            total = total + shared[device, :packed_rows, :]
-        total = jnp.concatenate([total, pltpu.roll(total, length // 2, 1)], axis=0)
-        ritz = jnp.transpose(solved(total, total_cols))[total_cols : total_cols + rows]
         everyone = jnp.concatenate([peer[...] for peer in peers], axis=0)
         spread = jnp.concatenate([image[...] for image in images], axis=0)
-        mixed = jnp.dot(ritz, everyone, precision=EXACT, preferred_element_type=F32)
-        mixed_image = jnp.dot(ritz, spread, precision=EXACT, preferred_element_type=F32)
+        mixed = jnp.dot(ritz[...], everyone, precision=EXACT, preferred_element_type=F32)
+        mixed_image = jnp.dot(ritz[...], spread, precision=EXACT, preferred_element_type=F32)
         weighted = degree[...] * mixed
         residual[...] = weighted - own_image[...]
         presmooth[...] = DAMPING * (mixed - scaled[...])
@@ -384,7 +386,9 @@
     peers = exchanged(states, "cols")
     ones_shape = jax.ShapeDtypeStruct((16, length), jnp.bfloat16)
     (ones,) = kernel_call(ones_body, [ones_shape], [], [], cost=20_000_000_000)
-    degree, degrees = kernel_call(degree_body, [line, (blocks, length)], [], [ones, adj_weight])
+    degree, degrees = kernel_call(
+        degree_body, [line, (blocks, length)], [], [ones, adj_weight, adj_index, partner]
+    )
     image, sent, scaled, outer, inner = kernel_call(
         image_body,
         [full, (local_cols, vertices), full, (rows, width + length), edge],
@@ -404,11 +408,12 @@
     inner = across_inner(inner, "rows")
     images = exchanged(sent, "cols")
     outer_mates = outer[0, width : width + blocks].astype(jnp.int32)
+    (ritz,) = kernel_call(solve_body, [(rows, total_cols)], [], [shared])
     out, remain, residual, presmooth, pair_degree, beside = kernel_call(
-        ritz_body,
+        remain_body,
         [slots, full, full, full, line, (rows, width + length)],
         [adj_index, partner],
-        [adj_weight, outer, inner, shared, *peers, *images, image, scaled, degree],
+        [adj_weight, outer, inner, shared, ritz, *peers, *images, image, scaled, degree],
         [field],
     )
     arrived = swapped(out, "rows")

time: 73 us -> 72.6 us (level)
  starting transfers between devices: 26.5 us -> 25.7 us
    ppermute x4, waiting for transfers between devices: 3.27 us -> 2.39 us  [across_inner(): lax.ppermute(value, axis, [(i, i ^ 1) for i in range(lax.axis_size(axis))])]
    all_to_all x3, waiting for transfers between devices: 21.2 us -> 22 us  [swapped(): return lax.all_to_all(value, axis, split_axis=0, concat_axis=0, tiled=True)]
    all_to_all x3, starting transfers between devices: 12.9 us -> 12 us  [swapped(): return lax.all_to_all(value, axis, split_axis=0, concat_axis=0, tiled=True)]
    pallas_call x10 -> x11, Pallas kernels: 10.4 us -> 10.7 us  [kernel_call(): pl.pallas_call(body, out_shape=[out if isinstance(out, jax.ShapeDtypeStru...]
  transfers between devices with their start and end apart: 13 -> 13, of which waited for: 7 -> 7; matrix products, arithmetic and copies ran while one was open for 0% -> 0% of each run, Pallas kernels for 2% -> 4%
where the time goes in v7:
time: 72.6 us; the launch traced here: 72 us
  starting transfers between devices  25.7 us (35%)
  waiting for transfers between devices  24.8 us (34%)
  Pallas kernels  10.7 us (15%)
  blocking collectives  9.58 us (13%)
  local copies, waits for them, and re-layouts  1.01 us (1%)
    all_to_all x3, waiting for transfers between devices, swapped(): return lax.all_to_all(value, axis, split_axis=0, concat_axis=0, tiled=True)  22 us
    all_to_all x3, starting transfers between devices, swapped(): return lax.all_to_all(value, axis, split_axis=0, concat_axis=0, tiled=True)  12 us
    pallas_call x11, Pallas kernels, kernel_call(): pl.pallas_call(body, out_shape=[out if isinstance(out, jax.ShapeDtypeStru...  10.7 us
    all_to_all x1, blocking collectives, swapped(): return lax.all_to_all(value, axis, split_axis=0, concat_axis=0, tiled=True)  9.58 us
    ppermute x4, starting transfers between devices, across_inner(): lax.ppermute(value, axis, [(i, i ^ 1) for i in range(lax.axis_size(axis))])  7.82 us
    ppermute x2, starting transfers between devices, exchanged(): lax.ppermute(value, axis, [(i, i ^ mask) for i in range(peers)])  3.11 us
    ppermute x4, starting transfers between devices, across_outer(): return lax.ppermute(value, axis, up + [(j, i) for i, j in up])  2.76 us
    ppermute x4, waiting for transfers between devices, across_inner(): lax.ppermute(value, axis, [(i, i ^ 1) for i in range(lax.axis_size(axis))])  2.39 us
  transfers between devices with their start and end apart: 13, of which 7 were waited for; matrix products, arithmetic and copies ran while one was open for 0% of the time, Pallas kernels for 4%

profile of v7, /device:TPU:0, one launch (start us, length us, event | category | flops | bytes accessed | tf_op | source)
XLA Modules:
  0.0 72.0 jit_solution(17700642087717091866)
XLA Ops:
  0.0 0.8 %collective-permute-start = (f32[16,1024]{1,0:T(8,128)}, f32[16,1024]{1,0:T(8,128)S(1)}, u32[]{:S(2)}, u32[]{:S(2)}) collective-permute-start(f32[16,1024]{1,0:T(8,128)} %refs_0_.3), channel_id=1, source_target_pairs={{2,4},{6,8},{10,12},{14,16},{18,20},{22,24},{26,28},{4,2},{8,6},{1... | collective-permute-start | bytes 196616 | tf_op jit(solution)/shard_map/ppermute | solution.py:48
  0.8 4.4 %collective-permute-start.1 = (f32[16,1024]{1,0:T(8,128)}, f32[16,1024]{1,0:T(8,128)S(1)}, u32[]{:S(2)}, u32[]{:S(2)}) collective-permute-start(f32[16,1024]{1,0:T(8,128)} %refs_0_.3), channel_id=1, source_target_pairs={{0,2},{2,0},{4,6},{6,4},{8,10},{10,8},{12,14},{14,12},{16,18},{18,... | collective-permute-start | bytes 196616 | tf_op jit(solution)/shard_map/ppermute | solution.py:52
  5.2 1.5 %collective-permute-start.4 = (f32[16,1024]{1,0:T(8,128)}, f32[16,1024]{1,0:T(8,128)S(1)}, u32[]{:S(2)}, u32[]{:S(2)}) collective-permute-start(f32[16,1024]{1,0:T(8,128)} %refs_0_.3), channel_id=1, source_target_pairs={{0,1},{1,0},{2,3},{3,2},{4,5},{5,4},{6,7},{7,6},{8,9},{9,8},{10,11... | collective-permute-start | bytes 196616 | tf_op jit(solution)/shard_map/ppermute | solution.py:37
  6.7 0.7 copy-done.2
  7.4 0.5 shard_map.47
  7.9 0.3 copy-done.1
  8.2 1.1 %shard_map.48 = (f32[16,1024]{1,0:T(8,128)S(1)}, f32[16,1024]{1,0:T(8,128)S(1)}, f32[16,1024]{1,0:T(8,128)S(1)}, f32[16,640]{1,0:T(8,128)S(1)}, f32[16,512]{1,0:T(8,128)S(1)}) custom-call(s32[3,8]{1,0:T(4,128)S(1)} %bitcast.4, s32[8]{0:T(128)S(1)} %copy-done.3, bf16[8,3,128,128]{3,2,1,0:T(8,128)(2,1)S(1)} %copy-done, ...), custom_call_target="tpu_custom_call" | custom-call | flops 2000000 | bytes 2000000 | tf_op jit(solution)/shard_map/pallas_call | solution.py:20
  9.3 0.3 collective-permute-done.4.refs_1_
  9.7 1.1 %shard_map.49 = f32[16,24,128]{2,1,0:T(8,128)} custom-call(f32[16,1024]{1,0:T(8,128)S(1)} %copy-done.1, f32[16,1024]{1,0:T(8,128)S(1)} %collective-permute-done.4.refs_1_, f32[16,1024]{1,0:T(8,128)S(1)} %get-tuple-element.33.refs_2_.refs_4_, f32[1,1024]{1,0:T(1,128)S(1)} %get-tuple-element.30.degree.refs_3_.refs_6_, f32[8,128]{1,0:T(8,128)S(1)} %get-tuple-element.34.refs_4_), custom_call_target="tpu_custom_call" | custom-call | flops 2000000 | bytes 2000000 | tf_op jit(solution)/shard_map/pallas_call | solution.py:20
  10.7 5.0 %all-to-all-start = ((f32[16,24,128]{2,1,0:T(8,128)}), f32[16,24,128]{2,1,0:T(8,128)S(1)}, u32[]{:S(2)}, u32[]{:S(2)}) async-start(f32[16,24,128]{2,1,0:T(8,128)} %shard_map.49), calls=%async_computation | async-start | bytes 393216 | tf_op jit(solution)/shard_map/all_to_all | solution.py:42
  15.7 1.6 %collective-permute-start.5 = (f32[16,1024]{1,0:T(8,128)S(1)}, f32[16,1024]{1,0:T(8,128)S(1)}, u32[]{:S(2)}, u32[]{:S(2)}) collective-permute-start(f32[16,1024]{1,0:T(8,128)S(1)} %get-tuple-element.35.refs_2_), channel_id=1, source_target_pairs={{0,1},{1,0},{2,3},{3,2},{4,5},{5,4},{6,7},{7,6},{8,9},{9,8},{10,11... | collective-permute-start | bytes 196616 | tf_op jit(solution)/shard_map/ppermute | solution.py:37
  17.3 0.7 collective-permute-start.2
  18.0 3.3 %collective-permute-start.3 = (f32[16,512]{1,0:T(8,128)S(1)}, f32[16,512]{1,0:T(8,128)S(1)}, u32[]{:S(2)}, u32[]{:S(2)}) collective-permute-start(f32[16,512]{1,0:T(8,128)S(1)} %get-tuple-element.32), channel_id=1, source_target_pairs={{0,2},{2,0},{4,6},{6,4},{8,10},{10,8},{12,14},{14,12},{16,18},{18,... | collective-permute-start | bytes 98312 | tf_op jit(solution)/shard_map/ppermute | solution.py:52
  21.2 3.4 %all-to-all-done.shared = f32[16,24,128]{2,1,0:T(8,128)S(1)} async-done(((f32[16,24,128]{2,1,0:T(8,128)}), f32[16,24,128]{2,1,0:T(8,128)S(1)}, u32[]{:S(2)}, u32[]{:S(2)}) %all-to-all-start) | async-done | bytes 196640 | tf_op jit(solution)/shard_map/all_to_all | solution.py:42
  24.7 0.9 %shard_map.50.ritz = f32[16,32]{1,0:T(8,128)S(1)} custom-call(f32[16,24,128]{2,1,0:T(8,128)S(1)} %all-to-all-done.shared), custom_call_target="tpu_custom_call" | custom-call | flops 2000000 | bytes 2000000 | tf_op jit(solution)/shard_map/pallas_call | solution.py:20
  25.7 2.0 %shard_map.51 = (f32[32,16,128]{2,1,0:T(8,128)}, f32[16,1024]{1,0:T(8,128)S(1)}, f32[16,1024]{1,0:T(8,128)S(1)}, f32[16,1024]{1,0:T(8,128)S(1)}, f32[1,1024]{1,0:T(1,128)S(1)}, /*index=5*/f32[16,640]{1,0:T(8,128)S(1)}) custom-call(s32[3,8]{1,0:T(4,128)S(1)} %bitcast.5, s32[8]{0:T(128)S(1)} %copy-done.3, bf16[8,3,128,128]{3,2,1,0:T(8,128)(2,1)S(1)} %copy-done, ...), custom_call_target="tpu_custom_call" | custom-call | flops 2000000 | bytes 2000000 | tf_op jit(solution)/shard_map/pallas_call | solution.py:20
  27.7 3.5 %all-to-all-start.1 = ((f32[32,16,128]{2,1,0:T(8,128)}), f32[32,16,128]{2,1,0:T(8,128)S(1)}, u32[]{:S(2)}, u32[]{:S(2)}) async-start(f32[32,16,128]{2,1,0:T(8,128)} %get-tuple-element.37), calls=%async_computation.1 | async-start | bytes 524288 | tf_op jit(solution)/shard_map/all_to_all | solution.py:42
  31.3 0.7 collective-permute-start.6
  31.9 9.3 %all-to-all-done.1.arrived = f32[32,16,128]{2,1,0:T(8,128)S(1)} async-done(((f32[32,16,128]{2,1,0:T(8,128)}), f32[32,16,128]{2,1,0:T(8,128)S(1)}, u32[]{:S(2)}, u32[]{:S(2)}) %all-to-all-start.1) | async-done | bytes 262176 | tf_op jit(solution)/shard_map/all_to_all | solution.py:42
  41.2 0.6 shard_map.52
  41.8 0.1 collective-permute-start.7
  41.9 1.2 %collective-permute-done.7.inner = f32[16,512]{1,0:T(8,128)S(1)} collective-permute-done((f32[16,512]{1,0:T(8,128)S(1)}, f32[16,512]{1,0:T(8,128)S(1)}, u32[]{:S(2)}, u32[]{:S(2)}) %collective-permute-start.7) | collective-permute-done | bytes 32800 | tf_op jit(solution)/shard_map/ppermute | solution.py:52
  43.1 1.8 %shard_map.53 = (f32[32,16,128]{2,1,0:T(8,128)}, f32[16,1024]{1,0:T(8,128)S(1)}, f32[16,512]{1,0:T(8,128)S(1)}) custom-call(s32[3,8]{1,0:T(4,128)S(1)} %bitcast.7, s32[8]{0:T(128)S(1)} %copy-done.3, bf16[8,3,128,128]{3,2,1,0:T(8,128)(2,1)S(1)} %copy-done, f32[32,512]{1,0:T(8,128)S(1)} %get-tuple-element.41.further, ...), custom_call_target="tpu_custom_call" | custom-call | flops 2000000 | bytes 2000000 | tf_op jit(solution)/shard_map/pallas_call | solution.py:20
  45.0 3.5 %all-to-all-start.2 = ((f32[32,16,128]{2,1,0:T(8,128)}), f32[32,16,128]{2,1,0:T(8,128)S(1)}, u32[]{:S(2)}, u32[]{:S(2)}) async-start(f32[32,16,128]{2,1,0:T(8,128)} %get-tuple-element.45), calls=%async_computation.2 | async-start | bytes 524288 | tf_op jit(solution)/shard_map/all_to_all | solution.py:42
  48.5 0.7 collective-permute-start.8
  49.2 9.3 %all-to-all-done.2.arrived = f32[32,16,128]{2,1,0:T(8,128)S(1)} async-done(((f32[32,16,128]{2,1,0:T(8,128)}), f32[32,16,128]{2,1,0:T(8,128)S(1)}, u32[]{:S(2)}, u32[]{:S(2)}) %all-to-all-start.2) | async-done | bytes 262176 | tf_op jit(solution)/shard_map/all_to_all | solution.py:42
  58.5 0.6 shard_map.54
  59.1 0.1 collective-permute-start.9
  59.2 1.2 %collective-permute-done.9.inner = f32[16,512]{1,0:T(8,128)S(1)} collective-permute-done((f32[16,512]{1,0:T(8,128)S(1)}, f32[16,512]{1,0:T(8,128)S(1)}, u32[]{:S(2)}, u32[]{:S(2)}) %collective-permute-start.9) | collective-permute-done | bytes 32800 | tf_op jit(solution)/shard_map/ppermute | solution.py:52
  60.4 1.2 %shard_map.55 = (f32[16,1024]{1,0:T(8,128)S(1)}, f32[16,8,128]{2,1,0:T(8,128)S(1)}) custom-call(s32[3,8]{1,0:T(4,128)S(1)} %bitcast.9, bf16[8,3,128,128]{3,2,1,0:T(8,128)(2,1)S(1)} %copy-done, f32[16,512]{1,0:T(8,128)S(1)} %get-tuple-element.49.outer, f32[16,512]{1,0:T(8,128)S(1)} %collective-permute-done.9.inner, f32[16,1024]{1,0:T(8,128)S(1)} %get-tuple-element.51.second, ...), custom_call_target="tpu_custom_call" | custom-call | flops 2000000 | bytes 2000000 | tf_op jit(solution)/shard_map/pallas_call | solution.py:20
  61.6 9.6 %all_to_all.20.squares = f32[16,8,128]{2,1,0:T(8,128)S(1)} all-to-all(f32[16,8,128]{2,1,0:T(8,128)S(1)} %get-tuple-element.53), channel_id=1, replica_groups=mesh['rows'=16,'cols'=2] {'rows'}, dimensions={0} | all-to-all | bytes 131072 | tf_op jit(solution)/shard_map/all_to_all | solution.py:42
  71.2 0.8 %shard_map.56 = f32[16,1024]{1,0:T(8,128)} custom-call(f32[16,8,128]{2,1,0:T(8,128)S(1)} %all_to_all.20.squares, f32[16,1024]{1,0:T(8,128)S(1)} %get-tuple-element.54.smooth), custom_call_target="tpu_custom_call" | custom-call | flops 2000000 | bytes 2000000 | tf_op jit(solution)/shard_map/pallas_call | solution.py:20
  (15 shorter events, 0.1 us)
Async XLA Ops:
  0.0 6.7 %copy-start = (bf16[8,3,128,128]{3,2,1,0:T(8,128)(2,1)S(1)}, bf16[8,3,128,128]{3,2,1,0:T(8,128)(2,1)}, u32[]{:S(2)}) copy-start(bf16[8,3,128,128]{3,2,1,0:T(8,128)(2,1)} %weight.9) | copy-start | bytes 2359300
  0.0 7.9 %collective-permute-start = (f32[16,1024]{1,0:T(8,128)}, f32[16,1024]{1,0:T(8,128)S(1)}, u32[]{:S(2)}, u32[]{:S(2)}) collective-permute-start(f32[16,1024]{1,0:T(8,128)} %refs_0_.3), channel_id=1, source_target_pairs={{2,4},{6,8},{10,12},{14,16},{18,20},{22,24},{26,28},{4,2},{8,6},{1... | collective-permute-start | bytes 196616 | tf_op jit(solution)/shard_map/ppermute | solution.py:48
  0.8 7.1 %collective-permute-start.1 = (f32[16,1024]{1,0:T(8,128)}, f32[16,1024]{1,0:T(8,128)S(1)}, u32[]{:S(2)}, u32[]{:S(2)}) collective-permute-start(f32[16,1024]{1,0:T(8,128)} %refs_0_.3), channel_id=1, source_target_pairs={{0,2},{2,0},{4,6},{6,4},{8,10},{10,8},{12,14},{14,12},{16,18},{18,... | collective-permute-start | bytes 196616 | tf_op jit(solution)/shard_map/ppermute | solution.py:52
  5.2 4.5 %collective-permute-start.4 = (f32[16,1024]{1,0:T(8,128)}, f32[16,1024]{1,0:T(8,128)S(1)}, u32[]{:S(2)}, u32[]{:S(2)}) collective-permute-start(f32[16,1024]{1,0:T(8,128)} %refs_0_.3), channel_id=1, source_target_pairs={{0,1},{1,0},{2,3},{3,2},{4,5},{5,4},{6,7},{7,6},{8,9},{9,8},{10,11... | collective-permute-start | bytes 196616 | tf_op jit(solution)/shard_map/ppermute | solution.py:37
  6.7 0.7 copy-start.2
  6.7 0.7 copy-start.3
  7.4 0.8 %copy-start.1 = (f32[16,1024]{1,0:T(8,128)S(1)}, f32[16,1024]{1,0:T(8,128)}, u32[]{:S(2)}) copy-start(f32[16,1024]{1,0:T(8,128)} %refs_0_.3) | copy-start | bytes 196612
  10.7 13.9 %all-to-all-start = ((f32[16,24,128]{2,1,0:T(8,128)}), f32[16,24,128]{2,1,0:T(8,128)S(1)}, u32[]{:S(2)}, u32[]{:S(2)}) async-start(f32[16,24,128]{2,1,0:T(8,128)} %shard_map.49), calls=%async_computation | async-start | bytes 393216 | tf_op jit(solution)/shard_map/all_to_all | solution.py:42
  15.7 10.0 %collective-permute-start.5 = (f32[16,1024]{1,0:T(8,128)S(1)}, f32[16,1024]{1,0:T(8,128)S(1)}, u32[]{:S(2)}, u32[]{:S(2)}) collective-permute-start(f32[16,1024]{1,0:T(8,128)S(1)} %get-tuple-element.35.refs_2_), channel_id=1, source_target_pairs={{0,1},{1,0},{2,3},{3,2},{4,5},{5,4},{6,7},{7,6},{8,9},{9,8},{10,11... | collective-permute-start | bytes 196616 | tf_op jit(solution)/shard_map/ppermute | solution.py:37
  17.3 8.4 %collective-permute-start.2 = (f32[16,640]{1,0:T(8,128)S(1)}, f32[16,640]{1,0:T(8,128)S(1)}, u32[]{:S(2)}, u32[]{:S(2)}) collective-permute-start(f32[16,640]{1,0:T(8,128)S(1)} %get-tuple-element.31), channel_id=1, source_target_pairs={{2,4},{6,8},{10,12},{14,16},{18,20},{22,24},{26,28},{4,2},{8,6},{1... | collective-permute-start | bytes 122888 | tf_op jit(solution)/shard_map/ppermute | solution.py:48
  18.0 7.7 %collective-permute-start.3 = (f32[16,512]{1,0:T(8,128)S(1)}, f32[16,512]{1,0:T(8,128)S(1)}, u32[]{:S(2)}, u32[]{:S(2)}) collective-permute-start(f32[16,512]{1,0:T(8,128)S(1)} %get-tuple-element.32), channel_id=1, source_target_pairs={{0,2},{2,0},{4,6},{6,4},{8,10},{10,8},{12,14},{14,12},{16,18},{18,... | collective-permute-start | bytes 98312 | tf_op jit(solution)/shard_map/ppermute | solution.py:52
  27.7 13.5 %all-to-all-start.1 = ((f32[32,16,128]{2,1,0:T(8,128)}), f32[32,16,128]{2,1,0:T(8,128)S(1)}, u32[]{:S(2)}, u32[]{:S(2)}) async-start(f32[32,16,128]{2,1,0:T(8,128)} %get-tuple-element.37), calls=%async_computation.1 | async-start | bytes 524288 | tf_op jit(solution)/shard_map/all_to_all | solution.py:42
  31.3 0.7 collective-permute-start.6
  41.8 1.3 %collective-permute-start.7 = (f32[16,512]{1,0:T(8,128)S(1)}, f32[16,512]{1,0:T(8,128)S(1)}, u32[]{:S(2)}, u32[]{:S(2)}) collective-permute-start(f32[16,512]{1,0:T(8,128)S(1)} %get-tuple-element.42), channel_id=1, source_target_pairs={{0,2},{2,0},{4,6},{6,4},{8,10},{10,8},{12,14},{14,12},{16,18},{18,... | collective-permute-start | bytes 98312 | tf_op jit(solution)/shard_map/ppermute | solution.py:52
  45.0 13.5 %all-to-all-start.2 = ((f32[32,16,128]{2,1,0:T(8,128)}), f32[32,16,128]{2,1,0:T(8,128)S(1)}, u32[]{:S(2)}, u32[]{:S(2)}) async-start(f32[32,16,128]{2,1,0:T(8,128)} %get-tuple-element.45), calls=%async_computation.2 | async-start | bytes 524288 | tf_op jit(solution)/shard_map/all_to_all | solution.py:42
  48.5 0.7 collective-permute-start.8
  59.1 1.3 %collective-permute-start.9 = (f32[16,512]{1,0:T(8,128)S(1)}, f32[16,512]{1,0:T(8,128)S(1)}, u32[]{:S(2)}, u32[]{:S(2)}) collective-permute-start(f32[16,512]{1,0:T(8,128)S(1)} %get-tuple-element.50), channel_id=1, source_target_pairs={{0,2},{2,0},{4,6},{6,4},{8,10},{10,8},{12,14},{14,12},{16,18},{18,... | collective-permute-start | bytes 98312 | tf_op jit(solution)/shard_map/ppermute | solution.py:52

commit v8 on v7

--- a/solution.py
+++ b/solution.py
@@ -353,6 +353,10 @@
         each(margin, other)
         inner[...] = second[:, halves(parity_of(index))[1]]
 
+    def diagonal():
+        lane = lax.broadcasted_iota(jnp.int32, (rows, length), 1)
+        return lane == lax.broadcasted_iota(jnp.int32, (rows, length), 0)
+
     def smooth_body(
         index, weight, outer, inner, second, residual, degree, smooth, squares, spread
     ):
@@ -367,8 +371,7 @@
         each(blocks, one)
         value = smooth[...]
         total = jnp.broadcast_to(jnp.sum(value * value, axis=1, keepdims=True), (rows, length))
-        lane = lax.broadcasted_iota(jnp.int32, (rows // 2, length), 1)
-        packed = jnp.where(lane < length // 2, total[: rows // 2], total[rows // 2 :])
+        packed = jnp.sum(jnp.where(diagonal(), total, 0.0), axis=0, keepdims=True)
         for device in range(row_devices):
             squares[device] = packed
 
@@ -376,8 +379,9 @@
         total = squares[0]
         for device in range(1, row_devices):
             total = total + squares[device]
-        total = jnp.concatenate([total, pltpu.roll(total, length // 2, 1)], axis=0)
-        norm = jnp.sqrt(total[:local_cols, :1] / (vertices * row_devices) + EPSILON)
+        total = jnp.where(diagonal(), jnp.broadcast_to(total, (rows, length)), 0.0)
+        total = jnp.sum(total, axis=1, keepdims=True)
+        norm = jnp.sqrt(total[:local_cols] / (vertices * row_devices) + EPSILON)
         correction[...] = smooth[:local_cols, :] / norm
 
     adj_index = adj_index.T
@@ -443,7 +447,7 @@
     inner = across_inner(inner, "rows")
     smooth, squares = kernel_call(
         smooth_body,
-        [full, (row_devices, rows // 2, length)],
+        [full, (row_devices, 1, length)],
         [adj_index],
         [adj_weight, outer, inner, second, residual, degree],
         [field],

time: 72.6 us -> 72.1 us (level)
  no operation moved by 1% of the time
where the time goes in v8:
time: 72.1 us; the launch traced here: 71.5 us
  starting transfers between devices  25.7 us (36%)
  waiting for transfers between devices  24.8 us (34%)
  Pallas kernels  10.7 us (15%)
  blocking collectives  9.12 us (13%)
  local copies, waits for them, and re-layouts  1.01 us (1%)
    all_to_all x3, waiting for transfers between devices, swapped(): return lax.all_to_all(value, axis, split_axis=0, concat_axis=0, tiled=True)  22 us
    all_to_all x3, starting transfers between devices, swapped(): return lax.all_to_all(value, axis, split_axis=0, concat_axis=0, tiled=True)  12 us
    pallas_call x11, Pallas kernels, kernel_call(): pl.pallas_call(body, out_shape=[out if isinstance(out, jax.ShapeDtypeStru...  10.7 us
    all_to_all x1, blocking collectives, swapped(): return lax.all_to_all(value, axis, split_axis=0, concat_axis=0, tiled=True)  9.12 us
    ppermute x4, starting transfers between devices, across_inner(): lax.ppermute(value, axis, [(i, i ^ 1) for i in range(lax.axis_size(axis))])  7.82 us
    ppermute x2, starting transfers between devices, exchanged(): lax.ppermute(value, axis, [(i, i ^ mask) for i in range(peers)])  3.11 us
    ppermute x4, starting transfers between devices, across_outer(): return lax.ppermute(value, axis, up + [(j, i) for i, j in up])  2.76 us
    ppermute x4, waiting for transfers between devices, across_inner(): lax.ppermute(value, axis, [(i, i ^ 1) for i in range(lax.axis_size(axis))])  2.39 us
  transfers between devices with their start and end apart: 13, of which 7 were waited for; matrix products, arithmetic and copies ran while one was open for 0% of the time, Pallas kernels for 4%

profile of v8, /device:TPU:0, one launch (start us, length us, event | category | flops | bytes accessed | tf_op | source)
XLA Modules:
  0.0 71.5 jit_solution(15736176570010154767)
XLA Ops:
  0.0 0.8 %collective-permute-start = (f32[16,1024]{1,0:T(8,128)}, f32[16,1024]{1,0:T(8,128)S(1)}, u32[]{:S(2)}, u32[]{:S(2)}) collective-permute-start(f32[16,1024]{1,0:T(8,128)} %refs_0_.3), channel_id=1, source_target_pairs={{2,4},{6,8},{10,12},{14,16},{18,20},{22,24},{26,28},{4,2},{8,6},{1... | collective-permute-start | bytes 196616 | tf_op jit(solution)/shard_map/ppermute | solution.py:48
  0.8 4.4 %collective-permute-start.1 = (f32[16,1024]{1,0:T(8,128)}, f32[16,1024]{1,0:T(8,128)S(1)}, u32[]{:S(2)}, u32[]{:S(2)}) collective-permute-start(f32[16,1024]{1,0:T(8,128)} %refs_0_.3), channel_id=1, source_target_pairs={{0,2},{2,0},{4,6},{6,4},{8,10},{10,8},{12,14},{14,12},{16,18},{18,... | collective-permute-start | bytes 196616 | tf_op jit(solution)/shard_map/ppermute | solution.py:52
  5.2 1.5 %collective-permute-start.4 = (f32[16,1024]{1,0:T(8,128)}, f32[16,1024]{1,0:T(8,128)S(1)}, u32[]{:S(2)}, u32[]{:S(2)}) collective-permute-start(f32[16,1024]{1,0:T(8,128)} %refs_0_.3), channel_id=1, source_target_pairs={{0,1},{1,0},{2,3},{3,2},{4,5},{5,4},{6,7},{7,6},{8,9},{9,8},{10,11... | collective-permute-start | bytes 196616 | tf_op jit(solution)/shard_map/ppermute | solution.py:37
  6.7 0.7 copy-done.2
  7.4 0.5 shard_map.47
  7.9 0.3 copy-done.1
  8.2 1.1 %shard_map.48 = (f32[16,1024]{1,0:T(8,128)S(1)}, f32[16,1024]{1,0:T(8,128)S(1)}, f32[16,1024]{1,0:T(8,128)S(1)}, f32[16,640]{1,0:T(8,128)S(1)}, f32[16,512]{1,0:T(8,128)S(1)}) custom-call(s32[3,8]{1,0:T(4,128)S(1)} %bitcast.4, s32[8]{0:T(128)S(1)} %copy-done.3, bf16[8,3,128,128]{3,2,1,0:T(8,128)(2,1)S(1)} %copy-done, ...), custom_call_target="tpu_custom_call" | custom-call | flops 2000000 | bytes 2000000 | tf_op jit(solution)/shard_map/pallas_call | solution.py:20
  9.3 0.3 collective-permute-done.4.refs_1_
  9.7 1.1 %shard_map.49 = f32[16,24,128]{2,1,0:T(8,128)} custom-call(f32[16,1024]{1,0:T(8,128)S(1)} %copy-done.1, f32[16,1024]{1,0:T(8,128)S(1)} %collective-permute-done.4.refs_1_, f32[16,1024]{1,0:T(8,128)S(1)} %get-tuple-element.33.refs_2_.refs_4_, f32[1,1024]{1,0:T(1,128)S(1)} %get-tuple-element.30.degree.refs_3_.refs_6_, f32[8,128]{1,0:T(8,128)S(1)} %get-tuple-element.34.refs_4_), custom_call_target="tpu_custom_call" | custom-call | flops 2000000 | bytes 2000000 | tf_op jit(solution)/shard_map/pallas_call | solution.py:20
  10.7 5.0 %all-to-all-start = ((f32[16,24,128]{2,1,0:T(8,128)}), f32[16,24,128]{2,1,0:T(8,128)S(1)}, u32[]{:S(2)}, u32[]{:S(2)}) async-start(f32[16,24,128]{2,1,0:T(8,128)} %shard_map.49), calls=%async_computation | async-start | bytes 393216 | tf_op jit(solution)/shard_map/all_to_all | solution.py:42
  15.7 1.6 %collective-permute-start.5 = (f32[16,1024]{1,0:T(8,128)S(1)}, f32[16,1024]{1,0:T(8,128)S(1)}, u32[]{:S(2)}, u32[]{:S(2)}) collective-permute-start(f32[16,1024]{1,0:T(8,128)S(1)} %get-tuple-element.35.refs_2_), channel_id=1, source_target_pairs={{0,1},{1,0},{2,3},{3,2},{4,5},{5,4},{6,7},{7,6},{8,9},{9,8},{10,11... | collective-permute-start | bytes 196616 | tf_op jit(solution)/shard_map/ppermute | solution.py:37
  17.3 0.7 collective-permute-start.2
  18.0 3.3 %collective-permute-start.3 = (f32[16,512]{1,0:T(8,128)S(1)}, f32[16,512]{1,0:T(8,128)S(1)}, u32[]{:S(2)}, u32[]{:S(2)}) collective-permute-start(f32[16,512]{1,0:T(8,128)S(1)} %get-tuple-element.32), channel_id=1, source_target_pairs={{0,2},{2,0},{4,6},{6,4},{8,10},{10,8},{12,14},{14,12},{16,18},{18,... | collective-permute-start | bytes 98312 | tf_op jit(solution)/shard_map/ppermute | solution.py:52
  21.2 3.4 %all-to-all-done.shared = f32[16,24,128]{2,1,0:T(8,128)S(1)} async-done(((f32[16,24,128]{2,1,0:T(8,128)}), f32[16,24,128]{2,1,0:T(8,128)S(1)}, u32[]{:S(2)}, u32[]{:S(2)}) %all-to-all-start) | async-done | bytes 196640 | tf_op jit(solution)/shard_map/all_to_all | solution.py:42
  24.7 0.9 %shard_map.50.ritz = f32[16,32]{1,0:T(8,128)S(1)} custom-call(f32[16,24,128]{2,1,0:T(8,128)S(1)} %all-to-all-done.shared), custom_call_target="tpu_custom_call" | custom-call | flops 2000000 | bytes 2000000 | tf_op jit(solution)/shard_map/pallas_call | solution.py:20
  25.7 2.0 %shard_map.51 = (f32[32,16,128]{2,1,0:T(8,128)}, f32[16,1024]{1,0:T(8,128)S(1)}, f32[16,1024]{1,0:T(8,128)S(1)}, f32[16,1024]{1,0:T(8,128)S(1)}, f32[1,1024]{1,0:T(1,128)S(1)}, /*index=5*/f32[16,640]{1,0:T(8,128)S(1)}) custom-call(s32[3,8]{1,0:T(4,128)S(1)} %bitcast.5, s32[8]{0:T(128)S(1)} %copy-done.3, bf16[8,3,128,128]{3,2,1,0:T(8,128)(2,1)S(1)} %copy-done, ...), custom_call_target="tpu_custom_call" | custom-call | flops 2000000 | bytes 2000000 | tf_op jit(solution)/shard_map/pallas_call | solution.py:20
  27.7 3.5 %all-to-all-start.1 = ((f32[32,16,128]{2,1,0:T(8,128)}), f32[32,16,128]{2,1,0:T(8,128)S(1)}, u32[]{:S(2)}, u32[]{:S(2)}) async-start(f32[32,16,128]{2,1,0:T(8,128)} %get-tuple-element.37), calls=%async_computation.1 | async-start | bytes 524288 | tf_op jit(solution)/shard_map/all_to_all | solution.py:42
  31.3 0.7 collective-permute-start.6
  31.9 9.3 %all-to-all-done.1.arrived = f32[32,16,128]{2,1,0:T(8,128)S(1)} async-done(((f32[32,16,128]{2,1,0:T(8,128)}), f32[32,16,128]{2,1,0:T(8,128)S(1)}, u32[]{:S(2)}, u32[]{:S(2)}) %all-to-all-start.1) | async-done | bytes 262176 | tf_op jit(solution)/shard_map/all_to_all | solution.py:42
  41.2 0.6 shard_map.52
  41.8 0.1 collective-permute-start.7
  41.9 1.2 %collective-permute-done.7.inner = f32[16,512]{1,0:T(8,128)S(1)} collective-permute-done((f32[16,512]{1,0:T(8,128)S(1)}, f32[16,512]{1,0:T(8,128)S(1)}, u32[]{:S(2)}, u32[]{:S(2)}) %collective-permute-start.7) | collective-permute-done | bytes 32800 | tf_op jit(solution)/shard_map/ppermute | solution.py:52
  43.1 1.8 %shard_map.53 = (f32[32,16,128]{2,1,0:T(8,128)}, f32[16,1024]{1,0:T(8,128)S(1)}, f32[16,512]{1,0:T(8,128)S(1)}) custom-call(s32[3,8]{1,0:T(4,128)S(1)} %bitcast.7, s32[8]{0:T(128)S(1)} %copy-done.3, bf16[8,3,128,128]{3,2,1,0:T(8,128)(2,1)S(1)} %copy-done, f32[32,512]{1,0:T(8,128)S(1)} %get-tuple-element.41.further, ...), custom_call_target="tpu_custom_call" | custom-call | flops 2000000 | bytes 2000000 | tf_op jit(solution)/shard_map/pallas_call | solution.py:20
  45.0 3.5 %all-to-all-start.2 = ((f32[32,16,128]{2,1,0:T(8,128)}), f32[32,16,128]{2,1,0:T(8,128)S(1)}, u32[]{:S(2)}, u32[]{:S(2)}) async-start(f32[32,16,128]{2,1,0:T(8,128)} %get-tuple-element.45), calls=%async_computation.2 | async-start | bytes 524288 | tf_op jit(solution)/shard_map/all_to_all | solution.py:42
  48.5 0.7 collective-permute-start.8
  49.2 9.3 %all-to-all-done.2.arrived = f32[32,16,128]{2,1,0:T(8,128)S(1)} async-done(((f32[32,16,128]{2,1,0:T(8,128)}), f32[32,16,128]{2,1,0:T(8,128)S(1)}, u32[]{:S(2)}, u32[]{:S(2)}) %all-to-all-start.2) | async-done | bytes 262176 | tf_op jit(solution)/shard_map/all_to_all | solution.py:42
  58.5 0.6 shard_map.54
  59.1 0.1 collective-permute-start.9
  59.2 1.2 %collective-permute-done.9.inner = f32[16,512]{1,0:T(8,128)S(1)} collective-permute-done((f32[16,512]{1,0:T(8,128)S(1)}, f32[16,512]{1,0:T(8,128)S(1)}, u32[]{:S(2)}, u32[]{:S(2)}) %collective-permute-start.9) | collective-permute-done | bytes 32800 | tf_op jit(solution)/shard_map/ppermute | solution.py:52
  60.4 1.2 %shard_map.55 = (f32[16,1024]{1,0:T(8,128)S(1)}, f32[16,1,128]{2,1,0:T(1,128)S(1)}) custom-call(s32[3,8]{1,0:T(4,128)S(1)} %bitcast.9, bf16[8,3,128,128]{3,2,1,0:T(8,128)(2,1)S(1)} %copy-done, f32[16,512]{1,0:T(8,128)S(1)} %get-tuple-element.49.outer, f32[16,512]{1,0:T(8,128)S(1)} %collective-permute-done.9.inner, f32[16,1024]{1,0:T(8,128)S(1)} %get-tuple-element.51.second, ...), custom_call_target="tpu_custom_call" | custom-call | flops 2000000 | bytes 2000000 | tf_op jit(solution)/shard_map/pallas_call | solution.py:20
  61.6 9.1 %all_to_all.20.squares = f32[16,1,128]{2,1,0:T(1,128)S(1)} all-to-all(f32[16,1,128]{2,1,0:T(1,128)S(1)} %get-tuple-element.53), channel_id=1, replica_groups=mesh['rows'=16,'cols'=2] {'rows'}, dimensions={0} | all-to-all | bytes 16384 | tf_op jit(solution)/shard_map/all_to_all | solution.py:42
  70.7 0.7 %shard_map.56 = f32[16,1024]{1,0:T(8,128)} custom-call(f32[16,1,128]{2,1,0:T(1,128)S(1)} %all_to_all.20.squares, f32[16,1024]{1,0:T(8,128)S(1)} %get-tuple-element.54.smooth), custom_call_target="tpu_custom_call" | custom-call | flops 2000000 | bytes 2000000 | tf_op jit(solution)/shard_map/pallas_call | solution.py:20
  (15 shorter events, 0.1 us)
Async XLA Ops:
  0.0 6.7 %copy-start = (bf16[8,3,128,128]{3,2,1,0:T(8,128)(2,1)S(1)}, bf16[8,3,128,128]{3,2,1,0:T(8,128)(2,1)}, u32[]{:S(2)}) copy-start(bf16[8,3,128,128]{3,2,1,0:T(8,128)(2,1)} %weight.9) | copy-start | bytes 2359300
  0.0 7.9 %collective-permute-start = (f32[16,1024]{1,0:T(8,128)}, f32[16,1024]{1,0:T(8,128)S(1)}, u32[]{:S(2)}, u32[]{:S(2)}) collective-permute-start(f32[16,1024]{1,0:T(8,128)} %refs_0_.3), channel_id=1, source_target_pairs={{2,4},{6,8},{10,12},{14,16},{18,20},{22,24},{26,28},{4,2},{8,6},{1... | collective-permute-start | bytes 196616 | tf_op jit(solution)/shard_map/ppermute | solution.py:48
  0.8 7.1 %collective-permute-start.1 = (f32[16,1024]{1,0:T(8,128)}, f32[16,1024]{1,0:T(8,128)S(1)}, u32[]{:S(2)}, u32[]{:S(2)}) collective-permute-start(f32[16,1024]{1,0:T(8,128)} %refs_0_.3), channel_id=1, source_target_pairs={{0,2},{2,0},{4,6},{6,4},{8,10},{10,8},{12,14},{14,12},{16,18},{18,... | collective-permute-start | bytes 196616 | tf_op jit(solution)/shard_map/ppermute | solution.py:52
  5.2 4.5 %collective-permute-start.4 = (f32[16,1024]{1,0:T(8,128)}, f32[16,1024]{1,0:T(8,128)S(1)}, u32[]{:S(2)}, u32[]{:S(2)}) collective-permute-start(f32[16,1024]{1,0:T(8,128)} %refs_0_.3), channel_id=1, source_target_pairs={{0,1},{1,0},{2,3},{3,2},{4,5},{5,4},{6,7},{7,6},{8,9},{9,8},{10,11... | collective-permute-start | bytes 196616 | tf_op jit(solution)/shard_map/ppermute | solution.py:37
  6.7 0.7 copy-start.2
  6.7 0.7 copy-start.3
  7.4 0.8 %copy-start.1 = (f32[16,1024]{1,0:T(8,128)S(1)}, f32[16,1024]{1,0:T(8,128)}, u32[]{:S(2)}) copy-start(f32[16,1024]{1,0:T(8,128)} %refs_0_.3) | copy-start | bytes 196612
  10.7 13.9 %all-to-all-start = ((f32[16,24,128]{2,1,0:T(8,128)}), f32[16,24,128]{2,1,0:T(8,128)S(1)}, u32[]{:S(2)}, u32[]{:S(2)}) async-start(f32[16,24,128]{2,1,0:T(8,128)} %shard_map.49), calls=%async_computation | async-start | bytes 393216 | tf_op jit(solution)/shard_map/all_to_all | solution.py:42
  15.7 10.0 %collective-permute-start.5 = (f32[16,1024]{1,0:T(8,128)S(1)}, f32[16,1024]{1,0:T(8,128)S(1)}, u32[]{:S(2)}, u32[]{:S(2)}) collective-permute-start(f32[16,1024]{1,0:T(8,128)S(1)} %get-tuple-element.35.refs_2_), channel_id=1, source_target_pairs={{0,1},{1,0},{2,3},{3,2},{4,5},{5,4},{6,7},{7,6},{8,9},{9,8},{10,11... | collective-permute-start | bytes 196616 | tf_op jit(solution)/shard_map/ppermute | solution.py:37
  17.3 8.4 %collective-permute-start.2 = (f32[16,640]{1,0:T(8,128)S(1)}, f32[16,640]{1,0:T(8,128)S(1)}, u32[]{:S(2)}, u32[]{:S(2)}) collective-permute-start(f32[16,640]{1,0:T(8,128)S(1)} %get-tuple-element.31), channel_id=1, source_target_pairs={{2,4},{6,8},{10,12},{14,16},{18,20},{22,24},{26,28},{4,2},{8,6},{1... | collective-permute-start | bytes 122888 | tf_op jit(solution)/shard_map/ppermute | solution.py:48
  18.0 7.7 %collective-permute-start.3 = (f32[16,512]{1,0:T(8,128)S(1)}, f32[16,512]{1,0:T(8,128)S(1)}, u32[]{:S(2)}, u32[]{:S(2)}) collective-permute-start(f32[16,512]{1,0:T(8,128)S(1)} %get-tuple-element.32), channel_id=1, source_target_pairs={{0,2},{2,0},{4,6},{6,4},{8,10},{10,8},{12,14},{14,12},{16,18},{18,... | collective-permute-start | bytes 98312 | tf_op jit(solution)/shard_map/ppermute | solution.py:52
  27.7 13.5 %all-to-all-start.1 = ((f32[32,16,128]{2,1,0:T(8,128)}), f32[32,16,128]{2,1,0:T(8,128)S(1)}, u32[]{:S(2)}, u32[]{:S(2)}) async-start(f32[32,16,128]{2,1,0:T(8,128)} %get-tuple-element.37), calls=%async_computation.1 | async-start | bytes 524288 | tf_op jit(solution)/shard_map/all_to_all | solution.py:42
  31.3 0.7 collective-permute-start.6
  41.8 1.3 %collective-permute-start.7 = (f32[16,512]{1,0:T(8,128)S(1)}, f32[16,512]{1,0:T(8,128)S(1)}, u32[]{:S(2)}, u32[]{:S(2)}) collective-permute-start(f32[16,512]{1,0:T(8,128)S(1)} %get-tuple-element.42), channel_id=1, source_target_pairs={{0,2},{2,0},{4,6},{6,4},{8,10},{10,8},{12,14},{14,12},{16,18},{18,... | collective-permute-start | bytes 98312 | tf_op jit(solution)/shard_map/ppermute | solution.py:52
  45.0 13.5 %all-to-all-start.2 = ((f32[32,16,128]{2,1,0:T(8,128)}), f32[32,16,128]{2,1,0:T(8,128)S(1)}, u32[]{:S(2)}, u32[]{:S(2)}) async-start(f32[32,16,128]{2,1,0:T(8,128)} %get-tuple-element.45), calls=%async_computation.2 | async-start | bytes 524288 | tf_op jit(solution)/shard_map/all_to_all | solution.py:42
  48.5 0.7 collective-permute-start.8
  59.1 1.3 %collective-permute-start.9 = (f32[16,512]{1,0:T(8,128)S(1)}, f32[16,512]{1,0:T(8,128)S(1)}, u32[]{:S(2)}, u32[]{:S(2)}) collective-permute-start(f32[16,512]{1,0:T(8,128)S(1)} %get-tuple-element.50), channel_id=1, source_target_pairs={{0,2},{2,0},{4,6},{6,4},{8,10},{10,8},{12,14},{14,12},{16,18},{18,... | collective-permute-start | bytes 98312 | tf_op jit(solution)/shard_map/ppermute | solution.py:52

commit v9 on v8

--- a/solution.py
+++ b/solution.py
@@ -187,7 +187,7 @@
     def ones_body(ones):
         ones[...] = jnp.ones(ones.shape, ones.dtype)
 
-    def degree_body(ones, weight, index, mates, degree, degrees):
+    def degree_body(ones, weight, index, mates, degree):
         def one(block):
             total = None
             for k in range(weight.shape[1]):
@@ -199,12 +199,11 @@
                 )
                 total = term if total is None else total + term
             degree[:, lanes(block, length)] = total[:1]
-            degrees[pl.ds(block, 1), :] = total[:1]
 
         each(blocks, one)
 
     def image_body(index, mates, weight, degree, outer_states, inner_states, states, *refs):
-        image, sent, scaled, outer, inner, spread = refs
+        image, sent, scaled, outer, inner, degrees, spread = refs
         parity = parity_of(index)
         at_own_outer, at_own_inner = halves(parity)
         fill_extended(
@@ -223,6 +222,8 @@
             scaled[:, at] = value / degree[:, at]
 
         each(blocks, one)
+        for block in range(blocks):
+            degrees[split(mates[block], blocks)[0]] = degree[:, lanes(block, length)]
         sent[...] = image[:local_cols, :]
         inner[...] = scaled[:, at_own_inner]
         outer[:, :width] = scaled[:, at_own_outer]
@@ -233,7 +234,10 @@
         outer[:, width:] = listed.astype(F32)
 
     def products_body(*refs):
-        peers, (image, degree, degrees, shared, wide) = refs[:col_devices], refs[col_devices:]
+        peers, (image, degree, degrees, shared, wide, flat) = (
+            refs[:col_devices],
+            refs[col_devices:],
+        )
         everyone = jnp.concatenate([peer[...] for peer in peers], axis=0)
         other = jnp.concatenate([everyone * degree[...], image[...]], axis=0)
         wide[...] = jnp.zeros(wide.shape, F32)
@@ -245,14 +249,20 @@
             preferred_element_type=F32,
         )
         packed = wide[:packed_rows, :] + pltpu.roll(wide[packed_rows:, :], length // 2, 1)
+        for row in range(packed_rows):
+            flat[:, lanes(row, length)] = packed[row : row + 1]
+        value = flat[...]
         for device in range(row_devices):
-            shared[device, :packed_rows, :] = packed
-            shared[device, packed_rows:, :] = degrees[...]
-
-    def solve_body(shared, ritz):
-        total = shared[0, :packed_rows, :]
+            shared[device, :, : packed_rows * length] = value
+            shared[device, :, packed_rows * length :] = degrees[device]
+
+    def solve_body(shared, ritz, tall):
+        total = shared[0, :, : packed_rows * length]
         for device in range(1, row_devices):
-            total = total + shared[device, :packed_rows, :]
+            total = total + shared[device, :, : packed_rows * length]
+        for row in range(packed_rows):
+            tall[row : row + 1, :] = total[:, row * length : (row + 1) * length]
+        total = tall[...]
         total = jnp.concatenate([total, pltpu.roll(total, length // 2, 1)], axis=0)
         ritz[...] = jnp.transpose(solved(total, total_cols))[total_cols : total_cols + rows]
 
@@ -282,8 +292,8 @@
         def one(block):
             at = lanes(block, length)
             place(out, mates[block], remain[:, at])
-            owner, position = split(mates[block], blocks)
-            pair_degree[:, at] = degree[:, at] + shared[owner, pl.ds(packed_rows + position, 1), :]
+            owner, _ = split(mates[block], blocks)
+            pair_degree[:, at] = degree[:, at] + shared[owner, :, packed_rows * length :]
 
         each(blocks, one)
         at_outer, _ = halves(parity)
@@ -390,29 +400,36 @@
     peers = exchanged(states, "cols")
     ones_shape = jax.ShapeDtypeStruct((16, length), jnp.bfloat16)
     (ones,) = kernel_call(ones_body, [ones_shape], [], [], cost=20_000_000_000)
-    degree, degrees = kernel_call(
-        degree_body, [line, (blocks, length)], [], [ones, adj_weight, adj_index, partner]
-    )
-    image, sent, scaled, outer, inner = kernel_call(
+    (degree,) = kernel_call(degree_body, [line], [], [ones, adj_weight, adj_index, partner])
+    image, sent, scaled, outer, inner, degrees = kernel_call(
         image_body,
-        [full, (local_cols, vertices), full, (rows, width + length), edge],
+        [
+            full,
+            (local_cols, vertices),
+            full,
+            (rows, width + length),
+            edge,
+            (row_devices, 1, length),
+        ],
         [adj_index, partner],
         [adj_weight, degree, outer, inner, states],
         [field],
     )
     (shared,) = kernel_call(
         products_body,
-        [(row_devices, packed_rows + blocks, length)],
+        [(row_devices, 1, (packed_rows + 1) * length)],
         [],
         [*peers, image, degree, degrees],
-        [pltpu.VMEM((total_cols, length), F32)],
+        [pltpu.VMEM((total_cols, length), F32), pltpu.VMEM((1, packed_rows * length), F32)],
     )
     shared = swapped(shared, "rows")
     outer = across_outer(outer, "rows")
     inner = across_inner(inner, "rows")
     images = exchanged(sent, "cols")
     outer_mates = outer[0, width : width + blocks].astype(jnp.int32)
-    (ritz,) = kernel_call(solve_body, [(rows, total_cols)], [], [shared])
+    (ritz,) = kernel_call(
+        solve_body, [(rows, total_cols)], [], [shared], [pltpu.VMEM((packed_rows, length), F32)]
+    )
     out, remain, residual, presmooth, pair_degree, beside = kernel_call(
         remain_body,
         [slots, full, full, full, line, (rows, width + length)],

time: 72.1 us -> 71.4 us (level)
  waiting for transfers between devices: 24.8 us -> 23.9 us
    all_to_all x3, waiting for transfers between devices: 22 us -> 21.1 us  [swapped(): return lax.all_to_all(value, axis, split_axis=0, concat_axis=0, tiled=True)]
where the time goes in v9:
time: 71.4 us; the launch traced here: 70.8 us
  starting transfers between devices  26 us (36%)
  waiting for transfers between devices  23.9 us (33%)
  Pallas kernels  10.7 us (15%)
  blocking collectives  9.12 us (13%)
  local copies, waits for them, and re-layouts  1.01 us (1%)
    all_to_all x3, waiting for transfers between devices, swapped(): return lax.all_to_all(value, axis, split_axis=0, concat_axis=0, tiled=True)  21.1 us
    all_to_all x3, starting transfers between devices, swapped(): return lax.all_to_all(value, axis, split_axis=0, concat_axis=0, tiled=True)  12.3 us
    pallas_call x11, Pallas kernels, kernel_call(): pl.pallas_call(body, out_shape=[out if isinstance(out, jax.ShapeDtypeStru...  10.7 us
    all_to_all x1, blocking collectives, swapped(): return lax.all_to_all(value, axis, split_axis=0, concat_axis=0, tiled=True)  9.12 us
    ppermute x4, starting transfers between devices, across_inner(): lax.ppermute(value, axis, [(i, i ^ 1) for i in range(lax.axis_size(axis))])  7.82 us
    ppermute x2, starting transfers between devices, exchanged(): lax.ppermute(value, axis, [(i, i ^ mask) for i in range(peers)])  3.11 us
    ppermute x4, starting transfers between devices, across_outer(): return lax.ppermute(value, axis, up + [(j, i) for i, j in up])  2.76 us
    ppermute x4, waiting for transfers between devices, across_inner(): lax.ppermute(value, axis, [(i, i ^ 1) for i in range(lax.axis_size(axis))])  2.39 us
  transfers between devices with their start and end apart: 13, of which 7 were waited for; matrix products, arithmetic and copies ran while one was open for 0% of the time, Pallas kernels for 4%

profile of v9, /device:TPU:0, one launch (start us, length us, event | category | flops | bytes accessed | tf_op | source)
XLA Modules:
  0.0 70.8 jit_solution(1467009475750794297)
XLA Ops:
  0.0 0.8 %collective-permute-start = (f32[16,1024]{1,0:T(8,128)}, f32[16,1024]{1,0:T(8,128)S(1)}, u32[]{:S(2)}, u32[]{:S(2)}) collective-permute-start(f32[16,1024]{1,0:T(8,128)} %refs_0_.3), channel_id=1, source_target_pairs={{2,4},{6,8},{10,12},{14,16},{18,20},{22,24},{26,28},{4,2},{8,6},{1... | collective-permute-start | bytes 196616 | tf_op jit(solution)/shard_map/ppermute | solution.py:48
  0.8 4.4 %collective-permute-start.1 = (f32[16,1024]{1,0:T(8,128)}, f32[16,1024]{1,0:T(8,128)S(1)}, u32[]{:S(2)}, u32[]{:S(2)}) collective-permute-start(f32[16,1024]{1,0:T(8,128)} %refs_0_.3), channel_id=1, source_target_pairs={{0,2},{2,0},{4,6},{6,4},{8,10},{10,8},{12,14},{14,12},{16,18},{18,... | collective-permute-start | bytes 196616 | tf_op jit(solution)/shard_map/ppermute | solution.py:52
  5.2 1.5 %collective-permute-start.4 = (f32[16,1024]{1,0:T(8,128)}, f32[16,1024]{1,0:T(8,128)S(1)}, u32[]{:S(2)}, u32[]{:S(2)}) collective-permute-start(f32[16,1024]{1,0:T(8,128)} %refs_0_.3), channel_id=1, source_target_pairs={{0,1},{1,0},{2,3},{3,2},{4,5},{5,4},{6,7},{7,6},{8,9},{9,8},{10,11... | collective-permute-start | bytes 196616 | tf_op jit(solution)/shard_map/ppermute | solution.py:37
  6.7 0.7 copy-done.2
  7.4 0.5 shard_map.47.degree.refs_3_.refs_6_
  7.9 0.3 copy-done.1
  8.2 1.1 %shard_map.48 = (f32[16,1024]{1,0:T(8,128)S(1)}, f32[16,1024]{1,0:T(8,128)S(1)}, f32[16,1024]{1,0:T(8,128)S(1)}, f32[16,640]{1,0:T(8,128)S(1)}, f32[16,512]{1,0:T(8,128)S(1)}, /*index=5*/f32[16,1,128]{2,1,0:T(1,128)S(1)}) custom-call(s32[3,8]{1,0:T(4,128)S(1)} %bitcast.4, s32[8]{0:T(128)S(1)} %copy-done.3, bf16[8,3,128,128]{3,2,1,0:T(8,128)(2,1)S(1)} %copy-done, ...), custom_call_target="tpu_custom_call" | custom-call | flops 2000000 | bytes 2000000 | tf_op jit(solution)/shard_map/pallas_call | solution.py:20
  9.3 0.3 collective-permute-done.4.refs_1_
  9.7 1.0 %shard_map.49 = f32[16,1,2176]{2,1,0:T(1,128)} custom-call(f32[16,1024]{1,0:T(8,128)S(1)} %copy-done.1, f32[16,1024]{1,0:T(8,128)S(1)} %collective-permute-done.4.refs_1_, f32[16,1024]{1,0:T(8,128)S(1)} %get-tuple-element.31.refs_2_.refs_4_, f32[1,1024]{1,0:T(1,128)S(1)} %shard_map.47.degree.refs_3_.refs_6_, f32[16,1,128]{2,1,0:T(1,128)S(1)} %get-tuple-element.32.refs_4_), custom_call_target="tpu_custom_call" | custom-call | flops 2000000 | bytes 2000000 | tf_op jit(solution)/shard_map/pallas_call | solution.py:20
  10.7 5.0 %all-to-all-start = ((f32[16,1,2176]{2,1,0:T(1,128)}), f32[16,1,2176]{2,1,0:T(1,128)S(1)}, u32[]{:S(2)}, u32[]{:S(2)}) async-start(f32[16,1,2176]{2,1,0:T(1,128)} %shard_map.49), calls=%async_computation | async-start | bytes 278528 | tf_op jit(solution)/shard_map/all_to_all | solution.py:42
  15.7 1.6 %collective-permute-start.5 = (f32[16,1024]{1,0:T(8,128)S(1)}, f32[16,1024]{1,0:T(8,128)S(1)}, u32[]{:S(2)}, u32[]{:S(2)}) collective-permute-start(f32[16,1024]{1,0:T(8,128)S(1)} %get-tuple-element.33.refs_2_), channel_id=1, source_target_pairs={{0,1},{1,0},{2,3},{3,2},{4,5},{5,4},{6,7},{7,6},{8,9},{9,8},{10,11... | collective-permute-start | bytes 196616 | tf_op jit(solution)/shard_map/ppermute | solution.py:37
  17.3 0.7 collective-permute-start.2
  17.9 3.3 %collective-permute-start.3 = (f32[16,512]{1,0:T(8,128)S(1)}, f32[16,512]{1,0:T(8,128)S(1)}, u32[]{:S(2)}, u32[]{:S(2)}) collective-permute-start(f32[16,512]{1,0:T(8,128)S(1)} %get-tuple-element.30), channel_id=1, source_target_pairs={{0,2},{2,0},{4,6},{6,4},{8,10},{10,8},{12,14},{14,12},{16,18},{18,... | collective-permute-start | bytes 98312 | tf_op jit(solution)/shard_map/ppermute | solution.py:52
  21.2 2.5 %all-to-all-done.shared = f32[16,1,2176]{2,1,0:T(1,128)S(1)} async-done(((f32[16,1,2176]{2,1,0:T(1,128)}), f32[16,1,2176]{2,1,0:T(1,128)S(1)}, u32[]{:S(2)}, u32[]{:S(2)}) %all-to-all-start) | async-done | bytes 139296 | tf_op jit(solution)/shard_map/all_to_all | solution.py:42
  23.7 0.9 %shard_map.50.ritz = f32[16,32]{1,0:T(8,128)S(1)} custom-call(f32[16,1,2176]{2,1,0:T(1,128)S(1)} %all-to-all-done.shared), custom_call_target="tpu_custom_call" | custom-call | flops 2000000 | bytes 2000000 | tf_op jit(solution)/shard_map/pallas_call | solution.py:20
  24.8 2.0 %shard_map.51 = (f32[32,16,128]{2,1,0:T(8,128)}, f32[16,1024]{1,0:T(8,128)S(1)}, f32[16,1024]{1,0:T(8,128)S(1)}, f32[16,1024]{1,0:T(8,128)S(1)}, f32[1,1024]{1,0:T(1,128)S(1)}, /*index=5*/f32[16,640]{1,0:T(8,128)S(1)}) custom-call(s32[3,8]{1,0:T(4,128)S(1)} %bitcast.5, s32[8]{0:T(128)S(1)} %copy-done.3, bf16[8,3,128,128]{3,2,1,0:T(8,128)(2,1)S(1)} %copy-done, ...), custom_call_target="tpu_custom_call" | custom-call | flops 2000000 | bytes 2000000 | tf_op jit(solution)/shard_map/pallas_call | solution.py:20
  26.8 3.8 %all-to-all-start.1 = ((f32[32,16,128]{2,1,0:T(8,128)}), f32[32,16,128]{2,1,0:T(8,128)S(1)}, u32[]{:S(2)}, u32[]{:S(2)}) async-start(f32[32,16,128]{2,1,0:T(8,128)} %get-tuple-element.35), calls=%async_computation.1 | async-start | bytes 524288 | tf_op jit(solution)/shard_map/all_to_all | solution.py:42
  30.6 0.7 collective-permute-start.6
  31.3 9.3 %all-to-all-done.1.arrived = f32[32,16,128]{2,1,0:T(8,128)S(1)} async-done(((f32[32,16,128]{2,1,0:T(8,128)}), f32[32,16,128]{2,1,0:T(8,128)S(1)}, u32[]{:S(2)}, u32[]{:S(2)}) %all-to-all-start.1) | async-done | bytes 262176 | tf_op jit(solution)/shard_map/all_to_all | solution.py:42
  40.6 0.6 shard_map.52
  41.2 0.1 collective-permute-start.7
  41.3 1.2 %collective-permute-done.7.inner = f32[16,512]{1,0:T(8,128)S(1)} collective-permute-done((f32[16,512]{1,0:T(8,128)S(1)}, f32[16,512]{1,0:T(8,128)S(1)}, u32[]{:S(2)}, u32[]{:S(2)}) %collective-permute-start.7) | collective-permute-done | bytes 32800 | tf_op jit(solution)/shard_map/ppermute | solution.py:52
  42.5 1.8 %shard_map.53 = (f32[32,16,128]{2,1,0:T(8,128)}, f32[16,1024]{1,0:T(8,128)S(1)}, f32[16,512]{1,0:T(8,128)S(1)}) custom-call(s32[3,8]{1,0:T(4,128)S(1)} %bitcast.7, s32[8]{0:T(128)S(1)} %copy-done.3, bf16[8,3,128,128]{3,2,1,0:T(8,128)(2,1)S(1)} %copy-done, f32[32,512]{1,0:T(8,128)S(1)} %get-tuple-element.39.further, ...), custom_call_target="tpu_custom_call" | custom-call | flops 2000000 | bytes 2000000 | tf_op jit(solution)/shard_map/pallas_call | solution.py:20
  44.3 3.5 %all-to-all-start.2 = ((f32[32,16,128]{2,1,0:T(8,128)}), f32[32,16,128]{2,1,0:T(8,128)S(1)}, u32[]{:S(2)}, u32[]{:S(2)}) async-start(f32[32,16,128]{2,1,0:T(8,128)} %get-tuple-element.43), calls=%async_computation.2 | async-start | bytes 524288 | tf_op jit(solution)/shard_map/all_to_all | solution.py:42
  47.9 0.7 collective-permute-start.8
  48.5 9.3 %all-to-all-done.2.arrived = f32[32,16,128]{2,1,0:T(8,128)S(1)} async-done(((f32[32,16,128]{2,1,0:T(8,128)}), f32[32,16,128]{2,1,0:T(8,128)S(1)}, u32[]{:S(2)}, u32[]{:S(2)}) %all-to-all-start.2) | async-done | bytes 262176 | tf_op jit(solution)/shard_map/all_to_all | solution.py:42
  57.8 0.6 shard_map.54
  58.5 0.1 collective-permute-start.9
  58.5 1.2 %collective-permute-done.9.inner = f32[16,512]{1,0:T(8,128)S(1)} collective-permute-done((f32[16,512]{1,0:T(8,128)S(1)}, f32[16,512]{1,0:T(8,128)S(1)}, u32[]{:S(2)}, u32[]{:S(2)}) %collective-permute-start.9) | collective-permute-done | bytes 32800 | tf_op jit(solution)/shard_map/ppermute | solution.py:52
  59.7 1.2 %shard_map.55 = (f32[16,1024]{1,0:T(8,128)S(1)}, f32[16,1,128]{2,1,0:T(1,128)S(1)}) custom-call(s32[3,8]{1,0:T(4,128)S(1)} %bitcast.9, bf16[8,3,128,128]{3,2,1,0:T(8,128)(2,1)S(1)} %copy-done, f32[16,512]{1,0:T(8,128)S(1)} %get-tuple-element.47.outer, f32[16,512]{1,0:T(8,128)S(1)} %collective-permute-done.9.inner, f32[16,1024]{1,0:T(8,128)S(1)} %get-tuple-element.49.second, ...), custom_call_target="tpu_custom_call" | custom-call | flops 2000000 | bytes 2000000 | tf_op jit(solution)/shard_map/pallas_call | solution.py:20
  61.0 9.1 %all_to_all.20.squares = f32[16,1,128]{2,1,0:T(1,128)S(1)} all-to-all(f32[16,1,128]{2,1,0:T(1,128)S(1)} %get-tuple-element.51), channel_id=1, replica_groups=mesh['rows'=16,'cols'=2] {'rows'}, dimensions={0} | all-to-all | bytes 16384 | tf_op jit(solution)/shard_map/all_to_all | solution.py:42
  70.1 0.7 %shard_map.56 = f32[16,1024]{1,0:T(8,128)} custom-call(f32[16,1,128]{2,1,0:T(1,128)S(1)} %all_to_all.20.squares, f32[16,1024]{1,0:T(8,128)S(1)} %get-tuple-element.52.smooth), custom_call_target="tpu_custom_call" | custom-call | flops 2000000 | bytes 2000000 | tf_op jit(solution)/shard_map/pallas_call | solution.py:20
  (15 shorter events, 0.1 us)
Async XLA Ops:
  0.0 6.7 %copy-start = (bf16[8,3,128,128]{3,2,1,0:T(8,128)(2,1)S(1)}, bf16[8,3,128,128]{3,2,1,0:T(8,128)(2,1)}, u32[]{:S(2)}) copy-start(bf16[8,3,128,128]{3,2,1,0:T(8,128)(2,1)} %weight.9) | copy-start | bytes 2359300
  0.0 7.9 %collective-permute-start = (f32[16,1024]{1,0:T(8,128)}, f32[16,1024]{1,0:T(8,128)S(1)}, u32[]{:S(2)}, u32[]{:S(2)}) collective-permute-start(f32[16,1024]{1,0:T(8,128)} %refs_0_.3), channel_id=1, source_target_pairs={{2,4},{6,8},{10,12},{14,16},{18,20},{22,24},{26,28},{4,2},{8,6},{1... | collective-permute-start | bytes 196616 | tf_op jit(solution)/shard_map/ppermute | solution.py:48
  0.8 7.1 %collective-permute-start.1 = (f32[16,1024]{1,0:T(8,128)}, f32[16,1024]{1,0:T(8,128)S(1)}, u32[]{:S(2)}, u32[]{:S(2)}) collective-permute-start(f32[16,1024]{1,0:T(8,128)} %refs_0_.3), channel_id=1, source_target_pairs={{0,2},{2,0},{4,6},{6,4},{8,10},{10,8},{12,14},{14,12},{16,18},{18,... | collective-permute-start | bytes 196616 | tf_op jit(solution)/shard_map/ppermute | solution.py:52
  5.2 4.5 %collective-permute-start.4 = (f32[16,1024]{1,0:T(8,128)}, f32[16,1024]{1,0:T(8,128)S(1)}, u32[]{:S(2)}, u32[]{:S(2)}) collective-permute-start(f32[16,1024]{1,0:T(8,128)} %refs_0_.3), channel_id=1, source_target_pairs={{0,1},{1,0},{2,3},{3,2},{4,5},{5,4},{6,7},{7,6},{8,9},{9,8},{10,11... | collective-permute-start | bytes 196616 | tf_op jit(solution)/shard_map/ppermute | solution.py:37
  6.7 0.7 copy-start.2
  6.7 0.7 copy-start.3
  7.4 0.8 %copy-start.1 = (f32[16,1024]{1,0:T(8,128)S(1)}, f32[16,1024]{1,0:T(8,128)}, u32[]{:S(2)}) copy-start(f32[16,1024]{1,0:T(8,128)} %refs_0_.3) | copy-start | bytes 196612
  10.7 13.0 %all-to-all-start = ((f32[16,1,2176]{2,1,0:T(1,128)}), f32[16,1,2176]{2,1,0:T(1,128)S(1)}, u32[]{:S(2)}, u32[]{:S(2)}) async-start(f32[16,1,2176]{2,1,0:T(1,128)} %shard_map.49), calls=%async_computation | async-start | bytes 278528 | tf_op jit(solution)/shard_map/all_to_all | solution.py:42
  15.7 9.1 %collective-permute-start.5 = (f32[16,1024]{1,0:T(8,128)S(1)}, f32[16,1024]{1,0:T(8,128)S(1)}, u32[]{:S(2)}, u32[]{:S(2)}) collective-permute-start(f32[16,1024]{1,0:T(8,128)S(1)} %get-tuple-element.33.refs_2_), channel_id=1, source_target_pairs={{0,1},{1,0},{2,3},{3,2},{4,5},{5,4},{6,7},{7,6},{8,9},{9,8},{10,11... | collective-permute-start | bytes 196616 | tf_op jit(solution)/shard_map/ppermute | solution.py:37
  17.3 7.5 %collective-permute-start.2 = (f32[16,640]{1,0:T(8,128)S(1)}, f32[16,640]{1,0:T(8,128)S(1)}, u32[]{:S(2)}, u32[]{:S(2)}) collective-permute-start(f32[16,640]{1,0:T(8,128)S(1)} %get-tuple-element.29), channel_id=1, source_target_pairs={{2,4},{6,8},{10,12},{14,16},{18,20},{22,24},{26,28},{4,2},{8,6},{1... | collective-permute-start | bytes 122888 | tf_op jit(solution)/shard_map/ppermute | solution.py:48
  17.9 6.7 %collective-permute-start.3 = (f32[16,512]{1,0:T(8,128)S(1)}, f32[16,512]{1,0:T(8,128)S(1)}, u32[]{:S(2)}, u32[]{:S(2)}) collective-permute-start(f32[16,512]{1,0:T(8,128)S(1)} %get-tuple-element.30), channel_id=1, source_target_pairs={{0,2},{2,0},{4,6},{6,4},{8,10},{10,8},{12,14},{14,12},{16,18},{18,... | collective-permute-start | bytes 98312 | tf_op jit(solution)/shard_map/ppermute | solution.py:52
  26.8 13.8 %all-to-all-start.1 = ((f32[32,16,128]{2,1,0:T(8,128)}), f32[32,16,128]{2,1,0:T(8,128)S(1)}, u32[]{:S(2)}, u32[]{:S(2)}) async-start(f32[32,16,128]{2,1,0:T(8,128)} %get-tuple-element.35), calls=%async_computation.1 | async-start | bytes 524288 | tf_op jit(solution)/shard_map/all_to_all | solution.py:42
  30.6 0.7 collective-permute-start.6
  41.2 1.3 %collective-permute-start.7 = (f32[16,512]{1,0:T(8,128)S(1)}, f32[16,512]{1,0:T(8,128)S(1)}, u32[]{:S(2)}, u32[]{:S(2)}) collective-permute-start(f32[16,512]{1,0:T(8,128)S(1)} %get-tuple-element.40), channel_id=1, source_target_pairs={{0,2},{2,0},{4,6},{6,4},{8,10},{10,8},{12,14},{14,12},{16,18},{18,... | collective-permute-start | bytes 98312 | tf_op jit(solution)/shard_map/ppermute | solution.py:52
  44.3 13.5 %all-to-all-start.2 = ((f32[32,16,128]{2,1,0:T(8,128)}), f32[32,16,128]{2,1,0:T(8,128)S(1)}, u32[]{:S(2)}, u32[]{:S(2)}) async-start(f32[32,16,128]{2,1,0:T(8,128)} %get-tuple-element.43), calls=%async_computation.2 | async-start | bytes 524288 | tf_op jit(solution)/shard_map/all_to_all | solution.py:42
  47.9 0.7 collective-permute-start.8
  58.5 1.3 %collective-permute-start.9 = (f32[16,512]{1,0:T(8,128)S(1)}, f32[16,512]{1,0:T(8,128)S(1)}, u32[]{:S(2)}, u32[]{:S(2)}) collective-permute-start(f32[16,512]{1,0:T(8,128)S(1)} %get-tuple-element.48), channel_id=1, source_target_pairs={{0,2},{2,0},{4,6},{6,4},{8,10},{10,8},{12,14},{14,12},{16,18},{18,... | collective-permute-start | bytes 98312 | tf_op jit(solution)/shard_map/ppermute | solution.py:52

commit v10 on v9

--- a/solution.py
+++ b/solution.py
@@ -303,28 +303,49 @@
         for block in range(margin):
             beside[block : block + 1, width:] = shared_degree[:, block * length : (block + 1) * length]
 
-    def beside_slot(index, outer_mates, block):
-        return split(outer_mates[(1 - parity_of(index)) * margin + block], blocks)[0]
-
-    def coarse_body(
-        index, mates, outer_mates, arrived, beside, remain, pair_degree, coarse, fix, further, inner
-    ):
-        def one(block):
-            at = lanes(block, length)
-            value = remain[:, at] + arrived[2 * split(mates[block], blocks)[0]]
+    def masks_body(index, mates, outer_mates, masks):
+        parity = parity_of(index)
+        source = lax.broadcasted_iota(jnp.int32, (row_devices, length), 0)
+        for block in range(blocks + margin):
+            if block < blocks:
+                mate = mates[block]
+            else:
+                mate = outer_mates[(1 - parity) * margin + block - blocks]
+            here = source == split(mate, blocks)[0]
+            masks[block * row_devices : (block + 1) * row_devices, :] = jnp.where(here, 1.0, 0.0)
+        masks[(blocks + margin) * row_devices :, :] = jnp.full((8, length), parity, F32)
+
+    def chosen(masks, arrived, block, slot):
+        value = arrived[slot]
+        for device in range(1, row_devices):
+            row = block * row_devices + device
+            here = jnp.broadcast_to(masks[row : row + 1, :], (rows, length)) > 0.5
+            value = jnp.where(here, arrived[2 * device + slot], value)
+        return value
+
+    def inner_half(masks, value):
+        row = (blocks + margin) * row_devices
+        odd = jnp.broadcast_to(masks[row : row + 1, :1], (rows, width)) > 0.5
+        return jnp.where(odd, value[:, :width], value[:, vertices - width :])
+
+    def coarse_body(masks, arrived, beside, remain, pair_degree, coarse, fix, further, inner):
+        def one(block):
+            at = lanes(block, length)
+            value = remain[:, at] + chosen(masks, arrived, block, 0)
             coarse[:, at] = value
             fix[:, at] = DAMPING * value / pair_degree[:, at]
 
         def other(block):
             at = lanes(block, length)
-            source = beside_slot(index, outer_mates, block)
-            value = beside[:, at] + arrived[2 * source + 1]
-            further[:rows, at] = DAMPING * value / beside[pl.ds(block, 1), width:]
+            value = beside[:, at] + chosen(masks, arrived, blocks + block, 1)
+            further[:rows, at] = DAMPING * value / beside[block : block + 1, width:]
             further[rows:, at] = value
 
-        each(blocks, one)
-        each(margin, other)
-        inner[...] = fix[:, halves(parity_of(index))[1]]
+        for block in range(blocks):
+            one(block)
+        for block in range(margin):
+            other(block)
+        inner[...] = inner_half(masks, fix[...])
 
     def product_body(
         index, mates, weight, further, inner, fix, degree, presmooth, pair_degree, *refs
@@ -343,25 +364,26 @@
         step = DAMPING * product[:, at_outer] / pair_degree[:, at_outer]
         outer[...] = presmooth[:, at_outer] - step
 
-    def fix_body(index, mates, outer_mates, arrived, partial, beside, further, *refs):
+    def fix_body(masks, arrived, partial, beside, further, *refs):
         product, coarse, fix, pair_degree, presmooth, second, outer, inner = refs
 
         def one(block):
             at = lanes(block, length)
-            image = product[:, at] + arrived[2 * split(mates[block], blocks)[0]]
+            image = product[:, at] + chosen(masks, arrived, block, 0)
             step = DAMPING * (coarse[:, at] - image) / pair_degree[:, at]
             second[:, at] = presmooth[:, at] + (fix[:, at] + step)
 
         def other(block):
             at = lanes(block, length)
-            source = beside_slot(index, outer_mates, block)
-            image = further[rows:, at] - arrived[2 * source + 1]
-            step = DAMPING * image / beside[pl.ds(block, 1), width:]
+            image = further[rows:, at] - chosen(masks, arrived, blocks + block, 1)
+            step = DAMPING * image / beside[block : block + 1, width:]
             outer[:, at] = partial[:, at] + (further[:rows, at] + step)
 
-        each(blocks, one)
-        each(margin, other)
-        inner[...] = second[:, halves(parity_of(index))[1]]
+        for block in range(blocks):
+            one(block)
+        for block in range(margin):
+            other(block)
+        inner[...] = inner_half(masks, second[...])
 
     def diagonal():
         lane = lax.broadcasted_iota(jnp.int32, (rows, length), 1)
@@ -439,11 +461,17 @@
     )
     arrived = swapped(out, "rows")
     beside = across_outer(beside, "rows")
+    (masks,) = kernel_call(
+        masks_body,
+        [((blocks + margin) * row_devices + 8, length)],
+        [adj_index, partner, outer_mates],
+        [],
+    )
     coarse, fix, further, inner = kernel_call(
         coarse_body,
         [full, full, (2 * rows, width), edge],
-        [adj_index, partner, outer_mates],
-        [arrived, beside, remain, pair_degree],
+        [],
+        [masks, arrived, beside, remain, pair_degree],
     )
     inner = across_inner(inner, "rows")
     out, product, outer = kernel_call(
@@ -458,8 +486,8 @@
     second, outer, inner = kernel_call(
         fix_body,
         [full, edge, edge],
-        [adj_index, partner, outer_mates],
-        [arrived, outer, beside, further, product, coarse, fix, pair_degree, presmooth],
+        [],
+        [masks, arrived, outer, beside, further, product, coarse, fix, pair_degree, presmooth],
     )
     inner = across_inner(inner, "rows")
     smooth, squares = kernel_call(

time: 71.4 us -> 70.5 us (0.987)
    pallas_call x11 -> x12, Pallas kernels: 10.7 us -> 10.3 us  [kernel_call(): pl.pallas_call(body, out_shape=[out if isinstance(out, jax.ShapeDtypeStru...]
  transfers between devices with their start and end apart: 13 -> 13, of which waited for: 7 -> 7; matrix products, arithmetic and copies ran while one was open for 0% -> 0% of each run, Pallas kernels for 4% -> 5%
where the time goes in v10:
time: 70.5 us; the launch traced here: 69.9 us
  starting transfers between devices  26 us (37%)
  waiting for transfers between devices  23.3 us (33%)
  Pallas kernels  10.3 us (15%)
  blocking collectives  9.12 us (13%)
  local copies, waits for them, and re-layouts  1.01 us (1%)
    all_to_all x3, waiting for transfers between devices, swapped(): return lax.all_to_all(value, axis, split_axis=0, concat_axis=0, tiled=True)  20.5 us
    all_to_all x3, starting transfers between devices, swapped(): return lax.all_to_all(value, axis, split_axis=0, concat_axis=0, tiled=True)  12.3 us
    pallas_call x12, Pallas kernels, kernel_call(): pl.pallas_call(body, out_shape=[out if isinstance(out, jax.ShapeDtypeStru...  10.3 us
    all_to_all x1, blocking collectives, swapped(): return lax.all_to_all(value, axis, split_axis=0, concat_axis=0, tiled=True)  9.12 us
    ppermute x4, starting transfers between devices, across_inner(): lax.ppermute(value, axis, [(i, i ^ 1) for i in range(lax.axis_size(axis))])  7.82 us
    ppermute x2, starting transfers between devices, exchanged(): lax.ppermute(value, axis, [(i, i ^ mask) for i in range(peers)])  3.1 us
    ppermute x4, starting transfers between devices, across_outer(): return lax.ppermute(value, axis, up + [(j, i) for i, j in up])  2.76 us
    ppermute x4, waiting for transfers between devices, across_inner(): lax.ppermute(value, axis, [(i, i ^ 1) for i in range(lax.axis_size(axis))])  2.39 us
  transfers between devices with their start and end apart: 13, of which 7 were waited for; matrix products, arithmetic and copies ran while one was open for 0% of the time, Pallas kernels for 5%

profile of v10, /device:TPU:0, one launch (start us, length us, event | category | flops | bytes accessed | tf_op | source)
XLA Modules:
  0.0 69.9 jit_solution(8479036978138167064)
XLA Ops:
  0.0 0.8 %collective-permute-start = (f32[16,1024]{1,0:T(8,128)}, f32[16,1024]{1,0:T(8,128)S(1)}, u32[]{:S(2)}, u32[]{:S(2)}) collective-permute-start(f32[16,1024]{1,0:T(8,128)} %refs_0_.3), channel_id=1, source_target_pairs={{2,4},{6,8},{10,12},{14,16},{18,20},{22,24},{26,28},{4,2},{8,6},{1... | collective-permute-start | bytes 196616 | tf_op jit(solution)/shard_map/ppermute | solution.py:48
  0.8 4.4 %collective-permute-start.1 = (f32[16,1024]{1,0:T(8,128)}, f32[16,1024]{1,0:T(8,128)S(1)}, u32[]{:S(2)}, u32[]{:S(2)}) collective-permute-start(f32[16,1024]{1,0:T(8,128)} %refs_0_.3), channel_id=1, source_target_pairs={{0,2},{2,0},{4,6},{6,4},{8,10},{10,8},{12,14},{14,12},{16,18},{18,... | collective-permute-start | bytes 196616 | tf_op jit(solution)/shard_map/ppermute | solution.py:52
  5.2 1.5 %collective-permute-start.4 = (f32[16,1024]{1,0:T(8,128)}, f32[16,1024]{1,0:T(8,128)S(1)}, u32[]{:S(2)}, u32[]{:S(2)}) collective-permute-start(f32[16,1024]{1,0:T(8,128)} %refs_0_.3), channel_id=1, source_target_pairs={{0,1},{1,0},{2,3},{3,2},{4,5},{5,4},{6,7},{7,6},{8,9},{9,8},{10,11... | collective-permute-start | bytes 196616 | tf_op jit(solution)/shard_map/ppermute | solution.py:37
  6.7 0.7 copy-done.2
  7.4 0.5 shard_map.47.degree.refs_3_.refs_6_
  7.9 0.3 copy-done.1
  8.2 1.1 %shard_map.48 = (f32[16,1024]{1,0:T(8,128)S(1)}, f32[16,1024]{1,0:T(8,128)S(1)}, f32[16,1024]{1,0:T(8,128)S(1)}, f32[16,640]{1,0:T(8,128)S(1)}, f32[16,512]{1,0:T(8,128)S(1)}, /*index=5*/f32[16,1,128]{2,1,0:T(1,128)S(1)}) custom-call(s32[3,8]{1,0:T(4,128)S(1)} %bitcast.4, s32[8]{0:T(128)S(1)} %copy-done.3, bf16[8,3,128,128]{3,2,1,0:T(8,128)(2,1)S(1)} %copy-done, ...), custom_call_target="tpu_custom_call" | custom-call | flops 2000000 | bytes 2000000 | tf_op jit(solution)/shard_map/pallas_call | solution.py:20
  9.4 0.3 collective-permute-done.4.refs_1_
  9.7 1.0 %shard_map.50 = f32[16,1,2176]{2,1,0:T(1,128)} custom-call(f32[16,1024]{1,0:T(8,128)S(1)} %copy-done.1, f32[16,1024]{1,0:T(8,128)S(1)} %collective-permute-done.4.refs_1_, f32[16,1024]{1,0:T(8,128)S(1)} %get-tuple-element.31.refs_2_.refs_4_, f32[1,1024]{1,0:T(1,128)S(1)} %shard_map.47.degree.refs_3_.refs_6_, f32[16,1,128]{2,1,0:T(1,128)S(1)} %get-tuple-element.32.refs_4_), custom_call_target="tpu_custom_call" | custom-call | flops 2000000 | bytes 2000000 | tf_op jit(solution)/shard_map/pallas_call | solution.py:20
  10.7 5.0 %all-to-all-start = ((f32[16,1,2176]{2,1,0:T(1,128)}), f32[16,1,2176]{2,1,0:T(1,128)S(1)}, u32[]{:S(2)}, u32[]{:S(2)}) async-start(f32[16,1,2176]{2,1,0:T(1,128)} %shard_map.50), calls=%async_computation | async-start | bytes 278528 | tf_op jit(solution)/shard_map/all_to_all | solution.py:42
  15.7 1.6 %collective-permute-start.5 = (f32[16,1024]{1,0:T(8,128)S(1)}, f32[16,1024]{1,0:T(8,128)S(1)}, u32[]{:S(2)}, u32[]{:S(2)}) collective-permute-start(f32[16,1024]{1,0:T(8,128)S(1)} %get-tuple-element.33.refs_2_), channel_id=1, source_target_pairs={{0,1},{1,0},{2,3},{3,2},{4,5},{5,4},{6,7},{7,6},{8,9},{9,8},{10,11... | collective-permute-start | bytes 196616 | tf_op jit(solution)/shard_map/ppermute | solution.py:37
  17.3 0.7 collective-permute-start.2
  17.9 3.3 %collective-permute-start.3 = (f32[16,512]{1,0:T(8,128)S(1)}, f32[16,512]{1,0:T(8,128)S(1)}, u32[]{:S(2)}, u32[]{:S(2)}) collective-permute-start(f32[16,512]{1,0:T(8,128)S(1)} %get-tuple-element.30), channel_id=1, source_target_pairs={{0,2},{2,0},{4,6},{6,4},{8,10},{10,8},{12,14},{14,12},{16,18},{18,... | collective-permute-start | bytes 98312 | tf_op jit(solution)/shard_map/ppermute | solution.py:52
  21.2 2.5 %all-to-all-done.shared = f32[16,1,2176]{2,1,0:T(1,128)S(1)} async-done(((f32[16,1,2176]{2,1,0:T(1,128)}), f32[16,1,2176]{2,1,0:T(1,128)S(1)}, u32[]{:S(2)}, u32[]{:S(2)}) %all-to-all-start) | async-done | bytes 139296 | tf_op jit(solution)/shard_map/all_to_all | solution.py:42
  23.7 0.9 %shard_map.51.ritz = f32[16,32]{1,0:T(8,128)S(1)} custom-call(f32[16,1,2176]{2,1,0:T(1,128)S(1)} %all-to-all-done.shared), custom_call_target="tpu_custom_call" | custom-call | flops 2000000 | bytes 2000000 | tf_op jit(solution)/shard_map/pallas_call | solution.py:20
  24.8 2.0 %shard_map.52 = (f32[32,16,128]{2,1,0:T(8,128)}, f32[16,1024]{1,0:T(8,128)S(1)}, f32[16,1024]{1,0:T(8,128)S(1)}, f32[16,1024]{1,0:T(8,128)S(1)}, f32[1,1024]{1,0:T(1,128)S(1)}, /*index=5*/f32[16,640]{1,0:T(8,128)S(1)}) custom-call(s32[3,8]{1,0:T(4,128)S(1)} %bitcast.5, s32[8]{0:T(128)S(1)} %copy-done.3, bf16[8,3,128,128]{3,2,1,0:T(8,128)(2,1)S(1)} %copy-done, ...), custom_call_target="tpu_custom_call" | custom-call | flops 2000000 | bytes 2000000 | tf_op jit(solution)/shard_map/pallas_call | solution.py:20
  26.8 3.8 %all-to-all-start.1 = ((f32[32,16,128]{2,1,0:T(8,128)}), f32[32,16,128]{2,1,0:T(8,128)S(1)}, u32[]{:S(2)}, u32[]{:S(2)}) async-start(f32[32,16,128]{2,1,0:T(8,128)} %get-tuple-element.35), calls=%async_computation.1 | async-start | bytes 524288 | tf_op jit(solution)/shard_map/all_to_all | solution.py:42
  30.6 0.7 collective-permute-start.6
  31.3 0.6 shard_map.49.masks
  31.9 8.7 %all-to-all-done.1.arrived = f32[32,16,128]{2,1,0:T(8,128)S(1)} async-done(((f32[32,16,128]{2,1,0:T(8,128)}), f32[32,16,128]{2,1,0:T(8,128)S(1)}, u32[]{:S(2)}, u32[]{:S(2)}) %all-to-all-start.1) | async-done | bytes 262176 | tf_op jit(solution)/shard_map/all_to_all | solution.py:42
  40.6 0.1 shard_map.53
  40.7 0.1 collective-permute-start.7
  40.8 1.2 %collective-permute-done.7.inner = f32[16,512]{1,0:T(8,128)S(1)} collective-permute-done((f32[16,512]{1,0:T(8,128)S(1)}, f32[16,512]{1,0:T(8,128)S(1)}, u32[]{:S(2)}, u32[]{:S(2)}) %collective-permute-start.7) | collective-permute-done | bytes 32800 | tf_op jit(solution)/shard_map/ppermute | solution.py:52
  42.0 1.8 %shard_map.54 = (f32[32,16,128]{2,1,0:T(8,128)}, f32[16,1024]{1,0:T(8,128)S(1)}, f32[16,512]{1,0:T(8,128)S(1)}) custom-call(s32[3,8]{1,0:T(4,128)S(1)} %bitcast.7, s32[8]{0:T(128)S(1)} %copy-done.3, bf16[8,3,128,128]{3,2,1,0:T(8,128)(2,1)S(1)} %copy-done, f32[32,512]{1,0:T(8,128)S(1)} %get-tuple-element.39.further, ...), custom_call_target="tpu_custom_call" | custom-call | flops 2000000 | bytes 2000000 | tf_op jit(solution)/shard_map/pallas_call | solution.py:20
  43.8 3.5 %all-to-all-start.2 = ((f32[32,16,128]{2,1,0:T(8,128)}), f32[32,16,128]{2,1,0:T(8,128)S(1)}, u32[]{:S(2)}, u32[]{:S(2)}) async-start(f32[32,16,128]{2,1,0:T(8,128)} %get-tuple-element.43), calls=%async_computation.2 | async-start | bytes 524288 | tf_op jit(solution)/shard_map/all_to_all | solution.py:42
  47.4 0.7 collective-permute-start.8
  48.1 9.3 %all-to-all-done.2.arrived = f32[32,16,128]{2,1,0:T(8,128)S(1)} async-done(((f32[32,16,128]{2,1,0:T(8,128)}), f32[32,16,128]{2,1,0:T(8,128)S(1)}, u32[]{:S(2)}, u32[]{:S(2)}) %all-to-all-start.2) | async-done | bytes 262176 | tf_op jit(solution)/shard_map/all_to_all | solution.py:42
  57.4 0.1 shard_map.55
  57.6 1.2 %collective-permute-done.9.inner = f32[16,512]{1,0:T(8,128)S(1)} collective-permute-done((f32[16,512]{1,0:T(8,128)S(1)}, f32[16,512]{1,0:T(8,128)S(1)}, u32[]{:S(2)}, u32[]{:S(2)}) %collective-permute-start.9) | collective-permute-done | bytes 32800 | tf_op jit(solution)/shard_map/ppermute | solution.py:52
  58.8 1.2 %shard_map.56 = (f32[16,1024]{1,0:T(8,128)S(1)}, f32[16,1,128]{2,1,0:T(1,128)S(1)}) custom-call(s32[3,8]{1,0:T(4,128)S(1)} %bitcast.8, bf16[8,3,128,128]{3,2,1,0:T(8,128)(2,1)S(1)} %copy-done, f32[16,512]{1,0:T(8,128)S(1)} %get-tuple-element.47.outer, f32[16,512]{1,0:T(8,128)S(1)} %collective-permute-done.9.inner, f32[16,1024]{1,0:T(8,128)S(1)} %get-tuple-element.49.second, ...), custom_call_target="tpu_custom_call" | custom-call | flops 2000000 | bytes 2000000 | tf_op jit(solution)/shard_map/pallas_call | solution.py:20
  60.0 9.1 %all_to_all.20.squares = f32[16,1,128]{2,1,0:T(1,128)S(1)} all-to-all(f32[16,1,128]{2,1,0:T(1,128)S(1)} %get-tuple-element.51), channel_id=1, replica_groups=mesh['rows'=16,'cols'=2] {'rows'}, dimensions={0} | all-to-all | bytes 16384 | tf_op jit(solution)/shard_map/all_to_all | solution.py:42
  69.2 0.7 %shard_map.57 = f32[16,1024]{1,0:T(8,128)} custom-call(f32[16,1,128]{2,1,0:T(1,128)S(1)} %all_to_all.20.squares, f32[16,1024]{1,0:T(8,128)S(1)} %get-tuple-element.52.smooth), custom_call_target="tpu_custom_call" | custom-call | flops 2000000 | bytes 2000000 | tf_op jit(solution)/shard_map/pallas_call | solution.py:20
  (16 shorter events, 0.2 us)
Async XLA Ops:
  0.0 6.7 %copy-start = (bf16[8,3,128,128]{3,2,1,0:T(8,128)(2,1)S(1)}, bf16[8,3,128,128]{3,2,1,0:T(8,128)(2,1)}, u32[]{:S(2)}) copy-start(bf16[8,3,128,128]{3,2,1,0:T(8,128)(2,1)} %weight.9) | copy-start | bytes 2359300
  0.0 7.9 %collective-permute-start = (f32[16,1024]{1,0:T(8,128)}, f32[16,1024]{1,0:T(8,128)S(1)}, u32[]{:S(2)}, u32[]{:S(2)}) collective-permute-start(f32[16,1024]{1,0:T(8,128)} %refs_0_.3), channel_id=1, source_target_pairs={{2,4},{6,8},{10,12},{14,16},{18,20},{22,24},{26,28},{4,2},{8,6},{1... | collective-permute-start | bytes 196616 | tf_op jit(solution)/shard_map/ppermute | solution.py:48
  0.8 7.1 %collective-permute-start.1 = (f32[16,1024]{1,0:T(8,128)}, f32[16,1024]{1,0:T(8,128)S(1)}, u32[]{:S(2)}, u32[]{:S(2)}) collective-permute-start(f32[16,1024]{1,0:T(8,128)} %refs_0_.3), channel_id=1, source_target_pairs={{0,2},{2,0},{4,6},{6,4},{8,10},{10,8},{12,14},{14,12},{16,18},{18,... | collective-permute-start | bytes 196616 | tf_op jit(solution)/shard_map/ppermute | solution.py:52
  5.2 4.5 %collective-permute-start.4 = (f32[16,1024]{1,0:T(8,128)}, f32[16,1024]{1,0:T(8,128)S(1)}, u32[]{:S(2)}, u32[]{:S(2)}) collective-permute-start(f32[16,1024]{1,0:T(8,128)} %refs_0_.3), channel_id=1, source_target_pairs={{0,1},{1,0},{2,3},{3,2},{4,5},{5,4},{6,7},{7,6},{8,9},{9,8},{10,11... | collective-permute-start | bytes 196616 | tf_op jit(solution)/shard_map/ppermute | solution.py:37
  6.7 0.7 copy-start.2
  6.7 0.7 copy-start.3
  7.4 0.8 %copy-start.1 = (f32[16,1024]{1,0:T(8,128)S(1)}, f32[16,1024]{1,0:T(8,128)}, u32[]{:S(2)}) copy-start(f32[16,1024]{1,0:T(8,128)} %refs_0_.3) | copy-start | bytes 196612
  10.7 13.0 %all-to-all-start = ((f32[16,1,2176]{2,1,0:T(1,128)}), f32[16,1,2176]{2,1,0:T(1,128)S(1)}, u32[]{:S(2)}, u32[]{:S(2)}) async-start(f32[16,1,2176]{2,1,0:T(1,128)} %shard_map.50), calls=%async_computation | async-start | bytes 278528 | tf_op jit(solution)/shard_map/all_to_all | solution.py:42
  15.7 9.1 %collective-permute-start.5 = (f32[16,1024]{1,0:T(8,128)S(1)}, f32[16,1024]{1,0:T(8,128)S(1)}, u32[]{:S(2)}, u32[]{:S(2)}) collective-permute-start(f32[16,1024]{1,0:T(8,128)S(1)} %get-tuple-element.33.refs_2_), channel_id=1, source_target_pairs={{0,1},{1,0},{2,3},{3,2},{4,5},{5,4},{6,7},{7,6},{8,9},{9,8},{10,11... | collective-permute-start | bytes 196616 | tf_op jit(solution)/shard_map/ppermute | solution.py:37
  17.3 7.5 %collective-permute-start.2 = (f32[16,640]{1,0:T(8,128)S(1)}, f32[16,640]{1,0:T(8,128)S(1)}, u32[]{:S(2)}, u32[]{:S(2)}) collective-permute-start(f32[16,640]{1,0:T(8,128)S(1)} %get-tuple-element.29), channel_id=1, source_target_pairs={{2,4},{6,8},{10,12},{14,16},{18,20},{22,24},{26,28},{4,2},{8,6},{1... | collective-permute-start | bytes 122888 | tf_op jit(solution)/shard_map/ppermute | solution.py:48
  17.9 6.7 %collective-permute-start.3 = (f32[16,512]{1,0:T(8,128)S(1)}, f32[16,512]{1,0:T(8,128)S(1)}, u32[]{:S(2)}, u32[]{:S(2)}) collective-permute-start(f32[16,512]{1,0:T(8,128)S(1)} %get-tuple-element.30), channel_id=1, source_target_pairs={{0,2},{2,0},{4,6},{6,4},{8,10},{10,8},{12,14},{14,12},{16,18},{18,... | collective-permute-start | bytes 98312 | tf_op jit(solution)/shard_map/ppermute | solution.py:52
  26.8 13.8 %all-to-all-start.1 = ((f32[32,16,128]{2,1,0:T(8,128)}), f32[32,16,128]{2,1,0:T(8,128)S(1)}, u32[]{:S(2)}, u32[]{:S(2)}) async-start(f32[32,16,128]{2,1,0:T(8,128)} %get-tuple-element.35), calls=%async_computation.1 | async-start | bytes 524288 | tf_op jit(solution)/shard_map/all_to_all | solution.py:42
  30.6 1.3 %collective-permute-start.6 = (f32[16,640]{1,0:T(8,128)S(1)}, f32[16,640]{1,0:T(8,128)S(1)}, u32[]{:S(2)}, u32[]{:S(2)}) collective-permute-start(f32[16,640]{1,0:T(8,128)S(1)} %get-tuple-element.36), channel_id=1, source_target_pairs={{2,4},{6,8},{10,12},{14,16},{18,20},{22,24},{26,28},{4,2},{8,6},{1... | collective-permute-start | bytes 122888 | tf_op jit(solution)/shard_map/ppermute | solution.py:48
  40.7 1.3 %collective-permute-start.7 = (f32[16,512]{1,0:T(8,128)S(1)}, f32[16,512]{1,0:T(8,128)S(1)}, u32[]{:S(2)}, u32[]{:S(2)}) collective-permute-start(f32[16,512]{1,0:T(8,128)S(1)} %get-tuple-element.40), channel_id=1, source_target_pairs={{0,2},{2,0},{4,6},{6,4},{8,10},{10,8},{12,14},{14,12},{16,18},{18,... | collective-permute-start | bytes 98312 | tf_op jit(solution)/shard_map/ppermute | solution.py:52
  43.8 13.5 %all-to-all-start.2 = ((f32[32,16,128]{2,1,0:T(8,128)}), f32[32,16,128]{2,1,0:T(8,128)S(1)}, u32[]{:S(2)}, u32[]{:S(2)}) async-start(f32[32,16,128]{2,1,0:T(8,128)} %get-tuple-element.43), calls=%async_computation.2 | async-start | bytes 524288 | tf_op jit(solution)/shard_map/all_to_all | solution.py:42
  47.4 0.7 collective-permute-start.8
  57.5 1.3 %collective-permute-start.9 = (f32[16,512]{1,0:T(8,128)S(1)}, f32[16,512]{1,0:T(8,128)S(1)}, u32[]{:S(2)}, u32[]{:S(2)}) collective-permute-start(f32[16,512]{1,0:T(8,128)S(1)} %get-tuple-element.48), channel_id=1, source_target_pairs={{0,2},{2,0},{4,6},{6,4},{8,10},{10,8},{12,14},{14,12},{16,18},{18,... | collective-permute-start | bytes 98312 | tf_op jit(solution)/shard_map/ppermute | solution.py:52

commit v11 on v10

--- a/solution.py
+++ b/solution.py
@@ -157,7 +157,7 @@
 
 def local(states, adj_weight, adj_index, partner):
     local_cols, vertices = states.shape
-    blocks, _, length, _ = adj_weight.shape
+    blocks, entries, length, _ = adj_weight.shape
     row_devices, col_devices = lax.axis_size("rows"), lax.axis_size("cols")
     total_cols = local_cols * col_devices
     margin = blocks // 2
@@ -313,7 +313,15 @@
                 mate = outer_mates[(1 - parity) * margin + block - blocks]
             here = source == split(mate, blocks)[0]
             masks[block * row_devices : (block + 1) * row_devices, :] = jnp.where(here, 1.0, 0.0)
-        masks[(blocks + margin) * row_devices :, :] = jnp.full((8, length), parity, F32)
+        base = (blocks + margin) * row_devices
+        masks[base : base + 8, :] = jnp.full((8, length), parity, F32)
+        base += 8
+        place_id = lax.broadcasted_iota(jnp.int32, (margin, length), 0)
+        first = (1 - parity) * (margin + blocks) - margin + index[0, 0]
+        for pair in range(blocks * (entries - 1)):
+            block, k = pair // (entries - 1), 1 + pair % (entries - 1)
+            here = place_id == index[k, block] - first
+            masks[base + pair * margin : base + (pair + 1) * margin, :] = jnp.where(here, 1.0, 0.0)
 
     def chosen(masks, arrived, block, slot):
         value = arrived[slot]
@@ -323,6 +331,25 @@
             value = jnp.where(here, arrived[2 * device + slot], value)
         return value
 
+    def inner_terms(masks, weight, inner, block):
+        base = (blocks + margin) * row_devices + 8
+        total = None
+        for k in range(1, entries):
+            start = base + (block * (entries - 1) + k - 1) * margin
+            value = jnp.zeros((rows, length), F32)
+            for j in range(margin):
+                row = masks[start + j : start + j + 1, :]
+                here = jnp.broadcast_to(row, (rows, length)) > 0.5
+                value = jnp.where(here, inner[:, lanes(j, length)], value)
+            term = lax.dot_general(
+                in_parts(value),
+                weight[block, k],
+                (((1,), (1,)), ((), ())),
+                preferred_element_type=F32,
+            )
+            total = term if total is None else total + term
+        return folded(total, rows)
+
     def inner_half(masks, value):
         row = (blocks + margin) * row_devices
         odd = jnp.broadcast_to(masks[row : row + 1, :1], (rows, width)) > 0.5
@@ -389,18 +416,23 @@
         lane = lax.broadcasted_iota(jnp.int32, (rows, length), 1)
         return lane == lax.broadcasted_iota(jnp.int32, (rows, length), 0)
 
-    def smooth_body(
-        index, weight, outer, inner, second, residual, degree, smooth, squares, spread
-    ):
-        fill_extended(spread, parity_of(index), outer[...], second[...], inner[...], length)
+    def smooth_early_body(index, weight, outer, second, residual, degree, early, spread):
+        nothing = jnp.zeros((rows, width), F32)
+        fill_extended(spread, parity_of(index), outer[...], second[...], nothing, length)
 
         def one(block):
             at = lanes(block, length)
             value, here = second[:, at], degree[:, at]
             image = here * value - folded(neighbours(index, weight, spread, block), rows)
-            smooth[:, at] = value + DAMPING * (residual[:, at] - image) / here
+            early[:, at] = value + DAMPING * (residual[:, at] - image) / here
 
         each(blocks, one)
+
+    def smooth_body(masks, weight, inner, early, degree, smooth, squares):
+        for block in range(blocks):
+            at = lanes(block, length)
+            step = DAMPING * inner_terms(masks, weight, inner, block) / degree[:, at]
+            smooth[:, at] = early[:, at] + step
         value = smooth[...]
         total = jnp.broadcast_to(jnp.sum(value * value, axis=1, keepdims=True), (rows, length))
         packed = jnp.sum(jnp.where(diagonal(), total, 0.0), axis=0, keepdims=True)
@@ -463,7 +495,7 @@
     beside = across_outer(beside, "rows")
     (masks,) = kernel_call(
         masks_body,
-        [((blocks + margin) * row_devices + 8, length)],
+        [((blocks + margin) * row_devices + 8 + blocks * (entries - 1) * margin, length)],
         [adj_index, partner, outer_mates],
         [],
     )
@@ -490,12 +522,15 @@
         [masks, arrived, outer, beside, further, product, coarse, fix, pair_degree, presmooth],
     )
     inner = across_inner(inner, "rows")
+    (early,) = kernel_call(
+        smooth_early_body,
+        [full],
+        [adj_index],
+        [adj_weight, outer, second, residual, degree],
+        [field],
+    )
     smooth, squares = kernel_call(
-        smooth_body,
-        [full, (row_devices, 1, length)],
-        [adj_index],
-        [adj_weight, outer, inner, second, residual, degree],
-        [field],
+        smooth_body, [full, (row_devices, 1, length)], [], [masks, adj_weight, inner, early, degree]
     )
     squares = swapped(squares, "rows")
     (correction,) = kernel_call(scale_body, [states.shape], [], [squares, smooth])

time: 70.5 us -> 70 us (level)
  waiting for transfers between devices: 23.3 us -> 22.2 us
    ppermute x4, waiting for transfers between devices: 2.39 us -> 1.29 us  [across_inner(): lax.ppermute(value, axis, [(i, i ^ 1) for i in range(lax.axis_size(axis))])]
    pallas_call x12 -> x13, Pallas kernels: 10.3 us -> 10.7 us  [kernel_call(): pl.pallas_call(body, out_shape=[out if isinstance(out, jax.ShapeDtypeStru...]
  transfers between devices with their start and end apart: 13 -> 13, of which waited for: 7 -> 7; matrix products, arithmetic and copies ran while one was open for 0% -> 0% of each run, Pallas kernels for 5% -> 6%
where the time goes in v11:
time: 70 us; the launch traced here: 69.3 us
  starting transfers between devices  26 us (37%)
  waiting for transfers between devices  22.2 us (32%)
  Pallas kernels  10.7 us (15%)
  blocking collectives  9.26 us (13%)
  local copies, waits for them, and re-layouts  1.01 us (1%)
    all_to_all x3, waiting for transfers between devices, swapped(): return lax.all_to_all(value, axis, split_axis=0, concat_axis=0, tiled=True)  20.5 us
    all_to_all x3, starting transfers between devices, swapped(): return lax.all_to_all(value, axis, split_axis=0, concat_axis=0, tiled=True)  12.3 us
    pallas_call x13, Pallas kernels, kernel_call(): pl.pallas_call(body, out_shape=[out if isinstance(out, jax.ShapeDtypeStru...  10.7 us
    all_to_all x1, blocking collectives, swapped(): return lax.all_to_all(value, axis, split_axis=0, concat_axis=0, tiled=True)  9.26 us
    ppermute x4, starting transfers between devices, across_inner(): lax.ppermute(value, axis, [(i, i ^ 1) for i in range(lax.axis_size(axis))])  7.82 us
    ppermute x2, starting transfers between devices, exchanged(): lax.ppermute(value, axis, [(i, i ^ mask) for i in range(peers)])  3.11 us
    ppermute x4, starting transfers between devices, across_outer(): return lax.ppermute(value, axis, up + [(j, i) for i, j in up])  2.76 us
  transfers between devices with their start and end apart: 13, of which 7 were waited for; matrix products, arithmetic and copies ran while one was open for 0% of the time, Pallas kernels for 6%

profile of v11, /device:TPU:0, one launch (start us, length us, event | category | flops | bytes accessed | tf_op | source)
XLA Modules:
  0.0 69.3 jit_solution(1040280282968738161)
XLA Ops:
  0.0 0.8 %collective-permute-start = (f32[16,1024]{1,0:T(8,128)}, f32[16,1024]{1,0:T(8,128)S(1)}, u32[]{:S(2)}, u32[]{:S(2)}) collective-permute-start(f32[16,1024]{1,0:T(8,128)} %refs_0_.3), channel_id=1, source_target_pairs={{2,4},{6,8},{10,12},{14,16},{18,20},{22,24},{26,28},{4,2},{8,6},{1... | collective-permute-start | bytes 196616 | tf_op jit(solution)/shard_map/ppermute | solution.py:48
  0.8 4.4 %collective-permute-start.1 = (f32[16,1024]{1,0:T(8,128)}, f32[16,1024]{1,0:T(8,128)S(1)}, u32[]{:S(2)}, u32[]{:S(2)}) collective-permute-start(f32[16,1024]{1,0:T(8,128)} %refs_0_.3), channel_id=1, source_target_pairs={{0,2},{2,0},{4,6},{6,4},{8,10},{10,8},{12,14},{14,12},{16,18},{18,... | collective-permute-start | bytes 196616 | tf_op jit(solution)/shard_map/ppermute | solution.py:52
  5.2 1.5 %collective-permute-start.4 = (f32[16,1024]{1,0:T(8,128)}, f32[16,1024]{1,0:T(8,128)S(1)}, u32[]{:S(2)}, u32[]{:S(2)}) collective-permute-start(f32[16,1024]{1,0:T(8,128)} %refs_0_.3), channel_id=1, source_target_pairs={{0,1},{1,0},{2,3},{3,2},{4,5},{5,4},{6,7},{7,6},{8,9},{9,8},{10,11... | collective-permute-start | bytes 196616 | tf_op jit(solution)/shard_map/ppermute | solution.py:37
  6.7 0.7 copy-done.2
  7.4 0.5 shard_map.47.degree.refs_3_.refs_6_
  7.9 0.3 copy-done.1
  8.2 1.1 %shard_map.48 = (f32[16,1024]{1,0:T(8,128)S(1)}, f32[16,1024]{1,0:T(8,128)S(1)}, f32[16,1024]{1,0:T(8,128)S(1)}, f32[16,640]{1,0:T(8,128)S(1)}, f32[16,512]{1,0:T(8,128)S(1)}, /*index=5*/f32[16,1,128]{2,1,0:T(1,128)S(1)}) custom-call(s32[3,8]{1,0:T(4,128)S(1)} %bitcast.4, s32[8]{0:T(128)S(1)} %copy-done.3, bf16[8,3,128,128]{3,2,1,0:T(8,128)(2,1)S(1)} %copy-done, ...), custom_call_target="tpu_custom_call" | custom-call | flops 2000000 | bytes 2000000 | tf_op jit(solution)/shard_map/pallas_call | solution.py:20
  9.3 0.3 collective-permute-done.4.refs_1_
  9.7 1.0 %shard_map.50 = f32[16,1,2176]{2,1,0:T(1,128)} custom-call(f32[16,1024]{1,0:T(8,128)S(1)} %copy-done.1, f32[16,1024]{1,0:T(8,128)S(1)} %collective-permute-done.4.refs_1_, f32[16,1024]{1,0:T(8,128)S(1)} %get-tuple-element.31.refs_2_.refs_4_, f32[1,1024]{1,0:T(1,128)S(1)} %shard_map.47.degree.refs_3_.refs_6_, f32[16,1,128]{2,1,0:T(1,128)S(1)} %get-tuple-element.32.refs_4_), custom_call_target="tpu_custom_call" | custom-call | flops 2000000 | bytes 2000000 | tf_op jit(solution)/shard_map/pallas_call | solution.py:20
  10.7 5.0 %all-to-all-start = ((f32[16,1,2176]{2,1,0:T(1,128)}), f32[16,1,2176]{2,1,0:T(1,128)S(1)}, u32[]{:S(2)}, u32[]{:S(2)}) async-start(f32[16,1,2176]{2,1,0:T(1,128)} %shard_map.50), calls=%async_computation | async-start | bytes 278528 | tf_op jit(solution)/shard_map/all_to_all | solution.py:42
  15.7 1.6 %collective-permute-start.5 = (f32[16,1024]{1,0:T(8,128)S(1)}, f32[16,1024]{1,0:T(8,128)S(1)}, u32[]{:S(2)}, u32[]{:S(2)}) collective-permute-start(f32[16,1024]{1,0:T(8,128)S(1)} %get-tuple-element.33.refs_2_), channel_id=1, source_target_pairs={{0,1},{1,0},{2,3},{3,2},{4,5},{5,4},{6,7},{7,6},{8,9},{9,8},{10,11... | collective-permute-start | bytes 196616 | tf_op jit(solution)/shard_map/ppermute | solution.py:37
  17.3 0.7 collective-permute-start.2
  17.9 3.3 %collective-permute-start.3 = (f32[16,512]{1,0:T(8,128)S(1)}, f32[16,512]{1,0:T(8,128)S(1)}, u32[]{:S(2)}, u32[]{:S(2)}) collective-permute-start(f32[16,512]{1,0:T(8,128)S(1)} %get-tuple-element.30), channel_id=1, source_target_pairs={{0,2},{2,0},{4,6},{6,4},{8,10},{10,8},{12,14},{14,12},{16,18},{18,... | collective-permute-start | bytes 98312 | tf_op jit(solution)/shard_map/ppermute | solution.py:52
  21.2 2.5 %all-to-all-done.shared = f32[16,1,2176]{2,1,0:T(1,128)S(1)} async-done(((f32[16,1,2176]{2,1,0:T(1,128)}), f32[16,1,2176]{2,1,0:T(1,128)S(1)}, u32[]{:S(2)}, u32[]{:S(2)}) %all-to-all-start) | async-done | bytes 139296 | tf_op jit(solution)/shard_map/all_to_all | solution.py:42
  23.7 0.9 %shard_map.51.ritz = f32[16,32]{1,0:T(8,128)S(1)} custom-call(f32[16,1,2176]{2,1,0:T(1,128)S(1)} %all-to-all-done.shared), custom_call_target="tpu_custom_call" | custom-call | flops 2000000 | bytes 2000000 | tf_op jit(solution)/shard_map/pallas_call | solution.py:20
  24.8 2.0 %shard_map.52 = (f32[32,16,128]{2,1,0:T(8,128)}, f32[16,1024]{1,0:T(8,128)S(1)}, f32[16,1024]{1,0:T(8,128)S(1)}, f32[16,1024]{1,0:T(8,128)S(1)}, f32[1,1024]{1,0:T(1,128)S(1)}, /*index=5*/f32[16,640]{1,0:T(8,128)S(1)}) custom-call(s32[3,8]{1,0:T(4,128)S(1)} %bitcast.5, s32[8]{0:T(128)S(1)} %copy-done.3, bf16[8,3,128,128]{3,2,1,0:T(8,128)(2,1)S(1)} %copy-done, ...), custom_call_target="tpu_custom_call" | custom-call | flops 2000000 | bytes 2000000 | tf_op jit(solution)/shard_map/pallas_call | solution.py:20
  26.8 3.8 %all-to-all-start.1 = ((f32[32,16,128]{2,1,0:T(8,128)}), f32[32,16,128]{2,1,0:T(8,128)S(1)}, u32[]{:S(2)}, u32[]{:S(2)}) async-start(f32[32,16,128]{2,1,0:T(8,128)} %get-tuple-element.35), calls=%async_computation.1 | async-start | bytes 524288 | tf_op jit(solution)/shard_map/all_to_all | solution.py:42
  30.6 0.7 collective-permute-start.6
  31.3 0.6 shard_map.49.masks
  31.9 8.7 %all-to-all-done.1.arrived = f32[32,16,128]{2,1,0:T(8,128)S(1)} async-done(((f32[32,16,128]{2,1,0:T(8,128)}), f32[32,16,128]{2,1,0:T(8,128)S(1)}, u32[]{:S(2)}, u32[]{:S(2)}) %all-to-all-start.1) | async-done | bytes 262176 | tf_op jit(solution)/shard_map/all_to_all | solution.py:42
  40.6 0.1 shard_map.53
  40.8 1.2 %collective-permute-done.7.inner = f32[16,512]{1,0:T(8,128)S(1)} collective-permute-done((f32[16,512]{1,0:T(8,128)S(1)}, f32[16,512]{1,0:T(8,128)S(1)}, u32[]{:S(2)}, u32[]{:S(2)}) %collective-permute-start.7) | collective-permute-done | bytes 32800 | tf_op jit(solution)/shard_map/ppermute | solution.py:52
  42.0 1.8 %shard_map.54 = (f32[32,16,128]{2,1,0:T(8,128)}, f32[16,1024]{1,0:T(8,128)S(1)}, f32[16,512]{1,0:T(8,128)S(1)}) custom-call(s32[3,8]{1,0:T(4,128)S(1)} %bitcast.7, s32[8]{0:T(128)S(1)} %copy-done.3, bf16[8,3,128,128]{3,2,1,0:T(8,128)(2,1)S(1)} %copy-done, f32[32,512]{1,0:T(8,128)S(1)} %get-tuple-element.39.further, ...), custom_call_target="tpu_custom_call" | custom-call | flops 2000000 | bytes 2000000 | tf_op jit(solution)/shard_map/pallas_call | solution.py:20
  43.9 3.5 %all-to-all-start.2 = ((f32[32,16,128]{2,1,0:T(8,128)}), f32[32,16,128]{2,1,0:T(8,128)S(1)}, u32[]{:S(2)}, u32[]{:S(2)}) async-start(f32[32,16,128]{2,1,0:T(8,128)} %get-tuple-element.43), calls=%async_computation.2 | async-start | bytes 524288 | tf_op jit(solution)/shard_map/all_to_all | solution.py:42
  47.4 0.7 collective-permute-start.8
  48.1 9.3 %all-to-all-done.2.arrived = f32[32,16,128]{2,1,0:T(8,128)S(1)} async-done(((f32[32,16,128]{2,1,0:T(8,128)}), f32[32,16,128]{2,1,0:T(8,128)S(1)}, u32[]{:S(2)}, u32[]{:S(2)}) %all-to-all-start.2) | async-done | bytes 262176 | tf_op jit(solution)/shard_map/all_to_all | solution.py:42
  57.4 0.1 shard_map.55
  57.6 1.1 %shard_map.56.early = f32[16,1024]{1,0:T(8,128)S(1)} custom-call(s32[3,8]{1,0:T(4,128)S(1)} %bitcast.8, bf16[8,3,128,128]{3,2,1,0:T(8,128)(2,1)S(1)} %copy-done, f32[16,512]{1,0:T(8,128)S(1)} %get-tuple-element.48.outer, f32[16,1024]{1,0:T(8,128)S(1)} %get-tuple-element.49.second, f32[16,1024]{1,0:T(8,128)S(1)} %get-tuple-element.50.residual, ...), custom_call_target="tpu_custom_call" | custom-call | flops 2000000 | bytes 2000000 | tf_op jit(solution)/shard_map/pallas_call | solution.py:20
  58.7 0.1 collective-permute-done.9.inner
  58.8 0.5 shard_map.57
  59.3 9.3 %all_to_all.20.squares = f32[16,1,128]{2,1,0:T(1,128)S(1)} all-to-all(f32[16,1,128]{2,1,0:T(1,128)S(1)} %get-tuple-element.51), channel_id=1, replica_groups=mesh['rows'=16,'cols'=2] {'rows'}, dimensions={0} | all-to-all | bytes 16384 | tf_op jit(solution)/shard_map/all_to_all | solution.py:42
  68.6 0.7 %shard_map.58 = f32[16,1024]{1,0:T(8,128)} custom-call(f32[16,1,128]{2,1,0:T(1,128)S(1)} %all_to_all.20.squares, f32[16,1024]{1,0:T(8,128)S(1)} %get-tuple-element.52.smooth), custom_call_target="tpu_custom_call" | custom-call | flops 2000000 | bytes 2000000 | tf_op jit(solution)/shard_map/pallas_call | solution.py:20
  (17 shorter events, 0.2 us)
Async XLA Ops:
  0.0 6.7 %copy-start = (bf16[8,3,128,128]{3,2,1,0:T(8,128)(2,1)S(1)}, bf16[8,3,128,128]{3,2,1,0:T(8,128)(2,1)}, u32[]{:S(2)}) copy-start(bf16[8,3,128,128]{3,2,1,0:T(8,128)(2,1)} %weight.11) | copy-start | bytes 2359300
  0.0 7.9 %collective-permute-start = (f32[16,1024]{1,0:T(8,128)}, f32[16,1024]{1,0:T(8,128)S(1)}, u32[]{:S(2)}, u32[]{:S(2)}) collective-permute-start(f32[16,1024]{1,0:T(8,128)} %refs_0_.3), channel_id=1, source_target_pairs={{2,4},{6,8},{10,12},{14,16},{18,20},{22,24},{26,28},{4,2},{8,6},{1... | collective-permute-start | bytes 196616 | tf_op jit(solution)/shard_map/ppermute | solution.py:48
  0.8 7.1 %collective-permute-start.1 = (f32[16,1024]{1,0:T(8,128)}, f32[16,1024]{1,0:T(8,128)S(1)}, u32[]{:S(2)}, u32[]{:S(2)}) collective-permute-start(f32[16,1024]{1,0:T(8,128)} %refs_0_.3), channel_id=1, source_target_pairs={{0,2},{2,0},{4,6},{6,4},{8,10},{10,8},{12,14},{14,12},{16,18},{18,... | collective-permute-start | bytes 196616 | tf_op jit(solution)/shard_map/ppermute | solution.py:52
  5.2 4.5 %collective-permute-start.4 = (f32[16,1024]{1,0:T(8,128)}, f32[16,1024]{1,0:T(8,128)S(1)}, u32[]{:S(2)}, u32[]{:S(2)}) collective-permute-start(f32[16,1024]{1,0:T(8,128)} %refs_0_.3), channel_id=1, source_target_pairs={{0,1},{1,0},{2,3},{3,2},{4,5},{5,4},{6,7},{7,6},{8,9},{9,8},{10,11... | collective-permute-start | bytes 196616 | tf_op jit(solution)/shard_map/ppermute | solution.py:37
  6.7 0.7 copy-start.2
  6.7 0.7 copy-start.3
  7.4 0.8 %copy-start.1 = (f32[16,1024]{1,0:T(8,128)S(1)}, f32[16,1024]{1,0:T(8,128)}, u32[]{:S(2)}) copy-start(f32[16,1024]{1,0:T(8,128)} %refs_0_.3) | copy-start | bytes 196612
  10.7 13.0 %all-to-all-start = ((f32[16,1,2176]{2,1,0:T(1,128)}), f32[16,1,2176]{2,1,0:T(1,128)S(1)}, u32[]{:S(2)}, u32[]{:S(2)}) async-start(f32[16,1,2176]{2,1,0:T(1,128)} %shard_map.50), calls=%async_computation | async-start | bytes 278528 | tf_op jit(solution)/shard_map/all_to_all | solution.py:42
  15.7 9.1 %collective-permute-start.5 = (f32[16,1024]{1,0:T(8,128)S(1)}, f32[16,1024]{1,0:T(8,128)S(1)}, u32[]{:S(2)}, u32[]{:S(2)}) collective-permute-start(f32[16,1024]{1,0:T(8,128)S(1)} %get-tuple-element.33.refs_2_), channel_id=1, source_target_pairs={{0,1},{1,0},{2,3},{3,2},{4,5},{5,4},{6,7},{7,6},{8,9},{9,8},{10,11... | collective-permute-start | bytes 196616 | tf_op jit(solution)/shard_map/ppermute | solution.py:37
  17.3 7.5 %collective-permute-start.2 = (f32[16,640]{1,0:T(8,128)S(1)}, f32[16,640]{1,0:T(8,128)S(1)}, u32[]{:S(2)}, u32[]{:S(2)}) collective-permute-start(f32[16,640]{1,0:T(8,128)S(1)} %get-tuple-element.29), channel_id=1, source_target_pairs={{2,4},{6,8},{10,12},{14,16},{18,20},{22,24},{26,28},{4,2},{8,6},{1... | collective-permute-start | bytes 122888 | tf_op jit(solution)/shard_map/ppermute | solution.py:48
  17.9 6.7 %collective-permute-start.3 = (f32[16,512]{1,0:T(8,128)S(1)}, f32[16,512]{1,0:T(8,128)S(1)}, u32[]{:S(2)}, u32[]{:S(2)}) collective-permute-start(f32[16,512]{1,0:T(8,128)S(1)} %get-tuple-element.30), channel_id=1, source_target_pairs={{0,2},{2,0},{4,6},{6,4},{8,10},{10,8},{12,14},{14,12},{16,18},{18,... | collective-permute-start | bytes 98312 | tf_op jit(solution)/shard_map/ppermute | solution.py:52
  26.8 13.8 %all-to-all-start.1 = ((f32[32,16,128]{2,1,0:T(8,128)}), f32[32,16,128]{2,1,0:T(8,128)S(1)}, u32[]{:S(2)}, u32[]{:S(2)}) async-start(f32[32,16,128]{2,1,0:T(8,128)} %get-tuple-element.35), calls=%async_computation.1 | async-start | bytes 524288 | tf_op jit(solution)/shard_map/all_to_all | solution.py:42
  30.6 1.3 %collective-permute-start.6 = (f32[16,640]{1,0:T(8,128)S(1)}, f32[16,640]{1,0:T(8,128)S(1)}, u32[]{:S(2)}, u32[]{:S(2)}) collective-permute-start(f32[16,640]{1,0:T(8,128)S(1)} %get-tuple-element.36), channel_id=1, source_target_pairs={{2,4},{6,8},{10,12},{14,16},{18,20},{22,24},{26,28},{4,2},{8,6},{1... | collective-permute-start | bytes 122888 | tf_op jit(solution)/shard_map/ppermute | solution.py:48
  40.7 1.3 %collective-permute-start.7 = (f32[16,512]{1,0:T(8,128)S(1)}, f32[16,512]{1,0:T(8,128)S(1)}, u32[]{:S(2)}, u32[]{:S(2)}) collective-permute-start(f32[16,512]{1,0:T(8,128)S(1)} %get-tuple-element.40), channel_id=1, source_target_pairs={{0,2},{2,0},{4,6},{6,4},{8,10},{10,8},{12,14},{14,12},{16,18},{18,... | collective-permute-start | bytes 98312 | tf_op jit(solution)/shard_map/ppermute | solution.py:52
  43.9 13.5 %all-to-all-start.2 = ((f32[32,16,128]{2,1,0:T(8,128)}), f32[32,16,128]{2,1,0:T(8,128)S(1)}, u32[]{:S(2)}, u32[]{:S(2)}) async-start(f32[32,16,128]{2,1,0:T(8,128)} %get-tuple-element.43), calls=%async_computation.2 | async-start | bytes 524288 | tf_op jit(solution)/shard_map/all_to_all | solution.py:42
  47.4 0.7 collective-permute-start.8
  57.5 1.3 %collective-permute-start.9 = (f32[16,512]{1,0:T(8,128)S(1)}, f32[16,512]{1,0:T(8,128)S(1)}, u32[]{:S(2)}, u32[]{:S(2)}) collective-permute-start(f32[16,512]{1,0:T(8,128)S(1)} %get-tuple-element.47), channel_id=1, source_target_pairs={{0,2},{2,0},{4,6},{6,4},{8,10},{10,8},{12,14},{14,12},{16,18},{18,... | collective-permute-start | bytes 98312 | tf_op jit(solution)/shard_map/ppermute | solution.py:52
